TPU v7x, 32 devices: a whole 2x2x4 slice. The times are simulated.
32 devices in a mesh: dp: 8 (over z, x), tensor: 4 (over y, core).
Axes of the slice: x: 2, y: 2, z: 4, core: 2. Of those that a mesh axis runs over, the one named last changes fastest.
Arguments:
- inputs: bfloat16 [16384, 768], P(('dp', 'tensor')), may hold values from -6 to 6
- layout_cells: int32 [2, 16384], P(None, 'dp'), may hold values from 0 to 31
- page_lengths: int32 [32, 8], P('dp'), may hold values from 1 to 256, 512 in all within a row
- attend_weight: bfloat16 [3, 768, 768], P(None, None, 'tensor'), may hold values from -0.21875 to 0.21875
- attend_shift: bfloat16 [2, 768], P(None, 'tensor'), may hold values from -3 to 3
- merge_weight: bfloat16 [768, 768], P('tensor'), may hold values from -0.875 to 0.875
- merge_shift: bfloat16 [768], replicated, may hold values from -3 to 3
- norm_gains: bfloat16 [2, 768], replicated, may hold values from 0.099609375 to 1.8984375
- norm_shifts: bfloat16 [2, 768], replicated, may hold values from -3 to 3
- expand_weight: bfloat16 [768, 3072], P(None, 'tensor'), may hold values from -0.21875 to 0.21875
- expand_shift: bfloat16 [3072], P('tensor'), may hold values from -3 to 3
- reduce_weight: bfloat16 [3072, 768], P('tensor'), may hold values from -0.109375 to 0.109375
- reduce_shift: bfloat16 [768], replicated, may hold values from -3 to 3
- bias_tables: bfloat16 [2, 12, 32], P(None, 'tensor'), may hold values from -4 to 4
- cotangent: bfloat16 [16384, 768], P(('dp', 'tensor')), may hold values from -6 to 6
Outputs:
- output: bfloat16 [16384, 768], P(('dp', 'tensor'))
- input_grad: bfloat16 [16384, 768], P(('dp', 'tensor'))
- attend_weight_grad: float32 [3, 768, 768], P(None, 'dp', 'tensor')
- attend_shift_grad: float32 [2, 768], P(None, 'tensor')
- merge_weight_grad: float32 [768, 768], P('tensor', 'dp')
- merge_shift_grad: float32 [768], replicated
- norm_gains_grad: float32 [2, 768], replicated
- norm_shifts_grad: float32 [2, 768], replicated
- expand_weight_grad: float32 [768, 3072], P('dp', 'tensor')
- expand_shift_grad: float32 [3072], P('tensor')
- reduce_weight_grad: float32 [3072, 768], P('tensor', 'dp')
- reduce_shift_grad: float32 [768], replicated
- bias_tables_grad: float32 [2, 12, 32], P(None, 'tensor')
Inputs may be any that keep to these rules, and one draw needn't show every extreme that they name: `page_lengths`: each row sums to 512; in each row the longest page has exactly 256 tokens.
All inputs are finite; a program needn't handle non-finite values.
Results may differ from a plain program's by a relative error of at most 0.02.
Values may be sent and summed in bfloat16 or wider, within the bound.
A program may use at most 128 MiB of HBM per device.

v0:
```python
from functools import partial

import jax
import jax.numpy as jnp
from jax import lax
from jax.sharding import PartitionSpec as P

HEAD_DIM = 64
BUCKETS = 32


EPSILON = 1e-05
MASKED = -1000000000.0


def layer_norm(signal, gain_vec, shift_vec):
    center = signal - jnp.mean(signal, axis=-1, keepdims=True)
    spread = jnp.mean(center * center, axis=-1, keepdims=True)
    return center * lax.rsqrt(spread + EPSILON) * gain_vec + shift_vec


def exact_gelu(signal):
    return jax.nn.gelu(signal, approximate=False)


def bucket_fold():
    cells = jnp.arange(BUCKETS, dtype=jnp.int32)
    bucket_of = jnp.clip(cells[:, None] - cells[None, :] + BUCKETS // 2, 0, BUCKETS - 1)
    return (bucket_of[:, :, None] == cells[None, None, :]).astype(jnp.float32)


def window_layout(coords_win, lengths_win):
    window_len = coords_win.shape[1]
    bounds = jnp.cumsum(lengths_win)
    places = jnp.arange(window_len, dtype=jnp.int32)
    segment = jnp.sum((places[:, None] >= bounds[None, :]).astype(jnp.int32), axis=1)
    same_seg = segment[:, None] == segment[None, :]
    cell_hot = (coords_win[:, :, None] == jnp.arange(BUCKETS, dtype=jnp.int32)).astype(jnp.bfloat16)
    return (same_seg, cell_hot)


def window_scores(queries, key_rows, same_seg, cell_hot, pair_table):
    raw_scores = jnp.einsum(
        "ihd,jhd->hij", queries, key_rows, preferred_element_type=jnp.float32
    ) * HEAD_DIM ** (-0.5)
    left_part = jnp.einsum(
        "aix,ahxy->ahiy", cell_hot, pair_table, preferred_element_type=jnp.float32
    ).astype(jnp.bfloat16)
    position = jnp.einsum("ahiy,ajy->ahij", left_part, cell_hot, preferred_element_type=jnp.float32)
    return jnp.where(same_seg[None], raw_scores + (position[0] + position[1]), MASKED)


def attend_forward(pair_table, pieces):
    queries, key_rows, value_rows, coords_win, lengths_win = pieces
    same_seg, cell_hot = window_layout(coords_win, lengths_win)
    scores = window_scores(queries, key_rows, same_seg, cell_hot, pair_table)
    row_max = jnp.max(scores, axis=2, keepdims=True)
    weights = jnp.exp(scores - row_max)
    row_total = jnp.sum(weights, axis=2, keepdims=True)
    soft_probs = (weights / row_total).astype(jnp.bfloat16)
    context = jnp.einsum("hij,jhd->ihd", soft_probs, value_rows, preferred_element_type=jnp.float32)
    return (context.astype(jnp.bfloat16), (row_max + jnp.log(row_total))[:, :, 0])


def attend_backward(pair_table, pieces):
    queries, key_rows, value_rows, grad_ctx, log_total, coords_win, lengths_win = pieces
    same_seg, cell_hot = window_layout(coords_win, lengths_win)
    scores = window_scores(queries, key_rows, same_seg, cell_hot, pair_table)
    soft_probs = jnp.exp(scores - log_total[:, :, None])
    grad_probs = jnp.einsum(
        "ihd,jhd->hij", grad_ctx, value_rows, preferred_element_type=jnp.float32
    )
    row_inner = jnp.sum(soft_probs * grad_probs, axis=2, keepdims=True)
    grad_scores = (soft_probs * (grad_probs - row_inner)).astype(jnp.bfloat16)
    score_scale = HEAD_DIM ** (-0.5)
    grad_query = (
        jnp.einsum("hij,jhd->ihd", grad_scores, key_rows, preferred_element_type=jnp.float32)
        * score_scale
    ).astype(jnp.bfloat16)
    grad_keys = (
        jnp.einsum("hij,ihd->jhd", grad_scores, queries, preferred_element_type=jnp.float32)
        * score_scale
    ).astype(jnp.bfloat16)
    grad_values = jnp.einsum(
        "hij,ihd->jhd",
        soft_probs.astype(jnp.bfloat16),
        grad_ctx,
        preferred_element_type=jnp.float32,
    ).astype(jnp.bfloat16)
    grad_left = jnp.einsum(
        "aix,hij->ahxj", cell_hot, grad_scores, preferred_element_type=jnp.float32
    )
    grad_pairs = jnp.einsum("ahxj,ajy->ahxy", grad_left, cell_hot.astype(jnp.float32))
    return (grad_query, grad_keys, grad_values, grad_pairs)


def on_device(
    inputs,
    layout_cells,
    page_lengths,
    attend_weight,
    attend_shift,
    merge_weight,
    merge_shift,
    norm_gains,
    norm_shifts,
    expand_weight,
    expand_shift,
    reduce_weight,
    reduce_shift,
    bias_tables,
    cotangent,
):
    windows = page_lengths.shape[0]
    group_rows = layout_cells.shape[1]
    window_len = group_rows // windows
    local_dim = attend_weight.shape[2]
    heads_here = bias_tables.shape[1]
    coord_wins = jnp.moveaxis(layout_cells.reshape(2, windows, window_len), 0, 1)
    folding = bucket_fold()
    pair_table = jnp.einsum("xyb,ahb->ahxy", folding, bias_tables.astype(jnp.float32)).astype(
        jnp.bfloat16
    )
    gathered = lax.all_gather(inputs, "tensor", axis=0, tiled=True)
    project = jnp.einsum("td,mde->mte", gathered, attend_weight, preferred_element_type=jnp.float32)
    triple_shift = jnp.stack(
        [attend_shift[0], jnp.zeros_like(attend_shift[0]), attend_shift[1]]
    ).astype(jnp.float32)
    packed_rows = (project + triple_shift[:, None, :]).astype(jnp.bfloat16)
    heads_form = packed_rows.reshape(3, windows, window_len, heads_here, HEAD_DIM)
    context, log_totals = lax.map(
        partial(attend_forward, pair_table),
        (heads_form[0], heads_form[1], heads_form[2], coord_wins, page_lengths),
    )
    context_rows = context.reshape(group_rows, local_dim)
    attended = lax.psum_scatter(
        jnp.dot(context_rows, merge_weight, preferred_element_type=jnp.float32).astype(
            jnp.bfloat16
        ),
        "tensor",
        scatter_dimension=0,
        tiled=True,
    ).astype(jnp.float32)
    resid_one = inputs.astype(jnp.float32) + attended + merge_shift.astype(jnp.float32)
    normed, norm_one_back = jax.vjp(
        layer_norm, resid_one, norm_gains[0].astype(jnp.float32), norm_shifts[0].astype(jnp.float32)
    )
    hidden_in = lax.all_gather(normed.astype(jnp.bfloat16), "tensor", axis=0, tiled=True)
    pre_act = jnp.dot(
        hidden_in, expand_weight, preferred_element_type=jnp.float32
    ) + expand_shift.astype(jnp.float32)
    activation, gelu_back = jax.vjp(exact_gelu, pre_act)
    activation = activation.astype(jnp.bfloat16)
    reduced = lax.psum_scatter(
        jnp.dot(activation, reduce_weight, preferred_element_type=jnp.float32).astype(jnp.bfloat16),
        "tensor",
        scatter_dimension=0,
        tiled=True,
    ).astype(jnp.float32)
    resid_two = normed + reduced + reduce_shift.astype(jnp.float32)
    output, norm_two_back = jax.vjp(
        layer_norm, resid_two, norm_gains[1].astype(jnp.float32), norm_shifts[1].astype(jnp.float32)
    )
    grad_two, grad_gain_two, grad_shift_two = norm_two_back(cotangent.astype(jnp.float32))
    ffn_grad_all = lax.all_gather(grad_two.astype(jnp.bfloat16), "tensor", axis=0, tiled=True)
    grad_w_down = jnp.einsum(
        "tf,td->fd", activation, ffn_grad_all, preferred_element_type=jnp.float32
    )
    grad_act = jnp.einsum(
        "td,fd->tf", ffn_grad_all, reduce_weight, preferred_element_type=jnp.float32
    )
    grad_pre = gelu_back(grad_act)[0].astype(jnp.bfloat16)
    grad_b_in = jnp.sum(grad_pre.astype(jnp.float32), axis=0)
    grad_w_in = jnp.einsum("td,tf->df", hidden_in, grad_pre, preferred_element_type=jnp.float32)
    grad_normed = (
        lax.psum_scatter(
            jnp.einsum(
                "tf,df->td", grad_pre, expand_weight, preferred_element_type=jnp.float32
            ).astype(jnp.bfloat16),
            "tensor",
            scatter_dimension=0,
            tiled=True,
        ).astype(jnp.float32)
        + grad_two
    )
    grad_one, grad_gain_one, grad_shift_one = norm_one_back(grad_normed)
    attn_grad_all = lax.all_gather(grad_one.astype(jnp.bfloat16), "tensor", axis=0, tiled=True)
    grad_w_out = jnp.einsum(
        "te,td->ed", context_rows, attn_grad_all, preferred_element_type=jnp.float32
    )
    grad_context = jnp.einsum(
        "td,ed->te", attn_grad_all, merge_weight, preferred_element_type=jnp.float32
    ).astype(jnp.bfloat16)
    grad_heads = grad_context.reshape(windows, window_len, heads_here, HEAD_DIM)
    grad_query, grad_keys, grad_values, grad_pairs = lax.map(
        partial(attend_backward, pair_table),
        (
            heads_form[0],
            heads_form[1],
            heads_form[2],
            grad_heads,
            log_totals,
            coord_wins,
            page_lengths,
        ),
    )
    grad_packed = jnp.stack([grad_query, grad_keys, grad_values]).reshape(3, group_rows, local_dim)
    grad_b_qv = jnp.stack(
        [
            jnp.sum(grad_packed[0].astype(jnp.float32), axis=0),
            jnp.sum(grad_packed[2].astype(jnp.float32), axis=0),
        ]
    )
    grad_tables = jnp.einsum("ahxy,xyb->ahb", jnp.sum(grad_pairs, axis=0), folding)
    grad_w_qkv = jnp.einsum(
        "td,mte->mde", gathered, grad_packed, preferred_element_type=jnp.float32
    )
    input_grad = (
        lax.psum_scatter(
            jnp.einsum(
                "mte,mde->td", grad_packed, attend_weight, preferred_element_type=jnp.float32
            ).astype(jnp.bfloat16),
            "tensor",
            scatter_dimension=0,
            tiled=True,
        ).astype(jnp.float32)
        + grad_one
    ).astype(jnp.bfloat16)
    grad_w_qkv, grad_w_out, grad_w_in, grad_w_down = (
        lax.psum_scatter(grad_w_qkv, "dp", scatter_dimension=1, tiled=True),
        lax.psum_scatter(grad_w_out, "dp", scatter_dimension=1, tiled=True),
        lax.psum_scatter(grad_w_in, "dp", scatter_dimension=0, tiled=True),
        lax.psum_scatter(grad_w_down, "dp", scatter_dimension=1, tiled=True),
    )
    grad_b_qv, grad_b_in, grad_tables = lax.psum((grad_b_qv, grad_b_in, grad_tables), "dp")
    grad_gains, grad_shifts, grad_b_out, grad_b_down = lax.psum(
        (
            jnp.stack([grad_gain_one, grad_gain_two]),
            jnp.stack([grad_shift_one, grad_shift_two]),
            jnp.sum(grad_one, axis=0),
            jnp.sum(grad_two, axis=0),
        ),
        ("dp", "tensor"),
    )
    return (
        output.astype(jnp.bfloat16),
        input_grad,
        grad_w_qkv,
        grad_b_qv,
        grad_w_out,
        grad_b_out,
        grad_gains,
        grad_shifts,
        grad_w_in,
        grad_b_in,
        grad_w_down,
        grad_b_down,
        grad_tables,
    )


def solution(mesh):
    in_specs = (
        P(("dp", "tensor"), None),
        P(None, "dp"),
        P("dp", None),
        P(None, None, "tensor"),
        P(None, "tensor"),
        P("tensor", None),
        P(),
        P(),
        P(),
        P(None, "tensor"),
        P("tensor"),
        P("tensor", None),
        P(),
        P(None, "tensor", None),
        P(("dp", "tensor"), None),
    )
    out_specs = (
        P(("dp", "tensor"), None),
        P(("dp", "tensor"), None),
        P(None, "dp", "tensor"),
        P(None, "tensor"),
        P("tensor", "dp"),
        P(),
        P(),
        P(),
        P("dp", "tensor"),
        P("tensor"),
        P("tensor", "dp"),
        P(),
        P(None, "tensor", None),
    )
    return jax.shard_map(
        on_device, mesh=mesh, in_specs=in_specs, out_specs=out_specs, check_vma=False
    )
```

profile of v0, /device:TPU:0, one launch (start us, length us, event | category | flops | bytes accessed | tf_op | source)
XLA Modules:
  0.0 754.0 jit_solution(975357659261729138)
XLA Ops:
  10.3 30.6 %all-gather.5.cloned.1.call-done = bf16[2048,768]{1,0:T(8,128)(2,1)} async-done(((bf16[512,768]{1,0:T(8,128)(2,1)}), bf16[2048,768]{1,0:T(8,128)(2,1)}) %all-gather.5.cloned.1.call-update) | async-done | bytes 3145744 | tf_op jit(solution)/shard_map/all_gather | solution.py:124
  40.9 4.2 fusion.106
  57.8 31.3 %while.28 = (s32[]{:T(128)}, bf16[4,512,3,64]{1,3,2,0:T(8,128)(2,1)S(1)}, f32[4,3,512]{2,1,0:T(4,128)}, bf16[4,512,3,64]{1,3,2,0:T(8,128)(2,1)}, s32[4,8]{1,0:T(...) while((s32[]{:T(128)}, ...), condition=%wide.region_5.6_spmd, body=%wide.region_0.5_spmd.sunk | while | flops 316680256 | bytes 24207652 | solution.py:131
  94.8 36.8 %reduce-scatter.13.cloned.1.call-done = bf16[512,768]{1,0:T(8,128)(2,1)} async-done(((bf16[2048,768]{1,0:T(8,128)(2,1)}), bf16[512,768]{1,0:T(8,128)(2,1)}) %reduce-scatter.13.cloned.1.call-update) | async-done | bytes 786448 | tf_op jit(solution)/shard_map/reduce_scatter | solution.py:136
  138.4 27.1 %all-gather.7.cloned.1.call-done = bf16[2048,768]{1,0:T(8,128)(2,1)} async-done(((bf16[512,768]{1,0:T(8,128)(2,1)}), bf16[2048,768]{1,0:T(8,128)(2,1)}) %all-gather.7.cloned.1.call-update) | async-done | bytes 3145744 | tf_op jit(solution)/shard_map/all_gather | solution.py:148
  165.4 18.4 %multiply_convert_fusion.1 = (bf16[2048,768]{1,0:T(8,128)(2,1)S(1)}, f32[2048,768]{1,0:T(8,128)}, f32[2048,768]{1,0:T(8,128)}) fusion(f32[768]{0:T(1024)} %convert_element_type.169, bf16[2048,768]{1,0:T(8,128)(2,1)} %all-gather.7.cloned.1.call-done, bf16[768,768]{1,0:T(8,128)(2,1)S(1)} %copy-done), kind=kOutput, calls=%fused_computation.102 | convolution fusion | flops 2519728128 | bytes 20057088 | tf_op jit(solution)/shard_map/dot_general | solution.py:149
  190.8 36.8 %reduce-scatter.15.cloned.1.call-done = bf16[512,768]{1,0:T(8,128)(2,1)} async-done(((bf16[2048,768]{1,0:T(8,128)(2,1)}), bf16[512,768]{1,0:T(8,128)(2,1)}) %reduce-scatter.15.cloned.1.call-update) | async-done | bytes 786448 | tf_op jit(solution)/shard_map/reduce_scatter | solution.py:154
  236.4 28.1 %all-gather.9.cloned.1.call-done = bf16[2048,768]{1,0:T(8,128)(2,1)} async-done(((bf16[512,768]{1,0:T(8,128)(2,1)}), bf16[2048,768]{1,0:T(8,128)(2,1)}) %all-gather.9.cloned.1.call-update) | async-done | bytes 3145744 | tf_op jit(solution)/shard_map/all_gather | solution.py:165
  264.5 11.0 %convert_reduce_fusion.2 = (f32[768]{0:T(1024)}, bf16[2048,768]{1,0:T(8,128)(2,1)S(1)}) fusion(f32[2048,768]{1,0:T(8,128)} %get-tuple-element.348, f32[2048,768]{1,0:T(8,128)} %get-tuple-element.361, f32[768]{0:T(1024)} %convert_element_type.169, bf16[2048,768]{1,0:T(8,128)(2,1)} %all-gather.9.cloned.1.call-done, bf16[768,768]{1,0:T(8,128)(2,1)} %param.30), kind=kOutput, calls=%fused_computation.100 | convolution fusion | flops 2442657024 | bytes 20060160 | tf_op jit(solution)/shard_map/td,fd->tf/dot_general | solution.py:169
  281.3 38.1 %reduce-scatter.17.cloned.1.call-done = bf16[512,768]{1,0:T(8,128)(2,1)} async-done(((bf16[2048,768]{1,0:T(8,128)(2,1)}), bf16[512,768]{1,0:T(8,128)(2,1)}) %reduce-scatter.17.cloned.1.call-update) | async-done | bytes 786448 | tf_op jit(solution)/shard_map/reduce_scatter | solution.py:176
  327.2 28.5 %all-gather.11.cloned.1.call-done = bf16[2048,768]{1,0:T(8,128)(2,1)} async-done(((bf16[512,768]{1,0:T(8,128)(2,1)}), bf16[2048,768]{1,0:T(8,128)(2,1)}) %all-gather.11.cloned.1.call-update) | async-done | bytes 3145744 | tf_op jit(solution)/shard_map/all_gather | solution.py:187
  363.2 61.9 %while.29 = (s32[]{:T(128)}, bf16[4,512,3,64]{1,3,2,0:T(8,128)(2,1)}, bf16[4,512,3,64]{1,3,2,0:T(8,128)(2,1)}, bf16[4,512,3,64]{1,3,2,0:T(8,128)(2,1)}, f32[4,2,...) while((s32[]{:T(128)}, ...), condition=%wide.region_21.22_spmd, body=%wide.region_17.21_spmd.sunk | while | flops 726870080 | bytes 41203016 | solution.py:195
  425.2 4.5 convolution_bitcast_fusion
  443.7 5.9 fusion.113
  449.6 4.2 copy.121
  453.8 4.8 reshape.322
  458.6 6.0 bitcast_convert_fusion
  465.0 7.0 fusion.139
  472.1 6.9 fusion.140
  479.2 40.2 %all-reduce = (f32[768]{0:T(1024)}, f32[2,768]{1,0:T(2,128)}, f32[2,768]{1,0:T(2,128)}, f32[768]{0:T(1024)}) all-reduce(f32[768]{0:T(1024)S(1)} %get-tuple-element.357, f32[2,768]{1,0:T(2,128)S(1)} %pad_maximum_fusion, f32[2,768]{1,0:T(2,128)S(1)} %pad_maximum_fusion.1, ...), channel_id=1, replica_groups=mesh['dp'=8,'tensor'=4] {'dp','tensor'}, use_global_device_ids=true, to_apply=%region_29.30 | all-reduce | flops 4608 | bytes 36864 | tf_op jit(solution)/shard_map/psum | solution.py:236
  522.0 36.9 %all-reduce.1 = (f32[2,192]{1,0:T(2,128)}, f32[768]{0:T(1024)}, f32[2,3,32]{2,1,0:T(4,128)S(1)}) all-reduce(f32[2,192]{1,0:T(2,128)S(1)} %pad_maximum_fusion.2, f32[768]{0:T(1024)S(1)} %copy-done.29, f32[2,3,32]{2,1,0:T(4,128)S(1)} %convolution_bitcast_fusion.1), channel_id=1, replica_groups=mesh['dp'=8,'tensor'=4] {'dp'}, use_global_device_ids=true, to_apply=%region_26.27 | all-reduce | flops 1344 | bytes 10752 | tf_op jit(solution)/shard_map/psum | solution.py:235
  563.6 37.5 %reduce-scatter.19.cloned.1.call-done = bf16[512,768]{1,0:T(8,128)(2,1)} async-done(((bf16[2048,768]{1,0:T(8,128)(2,1)}), bf16[512,768]{1,0:T(8,128)(2,1)}) %reduce-scatter.19.cloned.1.call-update) | async-done | bytes 786448 | tf_op jit(solution)/shard_map/reduce_scatter | solution.py:219
  603.3 70.9 %reduce-scatter.21.cloned.1.call-done = f32[96,768]{1,0:T(8,128)} async-done(((f32[768,768]{1,0:T(8,128)}), f32[96,768]{1,0:T(8,128)}) %reduce-scatter.21.cloned.1.call-update) | async-done | bytes 294928 | tf_op jit(solution)/shard_map/reduce_scatter | solution.py:232
  674.2 72.5 %reduce-scatter.23.cloned.1.call-done = f32[768,96]{0,1:T(8,128)} async-done(((f32[768,768]{0,1:T(8,128)}), f32[768,96]{0,1:T(8,128)}) %reduce-scatter.23.cloned.1.call-update) | async-done | bytes 294928 | tf_op jit(solution)/shard_map/reduce_scatter | solution.py:233
  (277 shorter events, 181.8 us)
Async XLA Ops:
  7.2 158.3 %copy-start = (bf16[768,768]{1,0:T(8,128)(2,1)S(1)}, bf16[768,768]{1,0:T(8,128)(2,1)}, u32[]{:S(2)}) copy-start(bf16[768,768]{1,0:T(8,128)(2,1)} %param.28) | copy-start | bytes 3538948
  7.2 33.7 %all-gather.5.cloned.1.call-start = ((), (), s32[]{:S(2)}) async-start(), calls=%async_computation.8 | async-start | bytes 3932160 | tf_op jit(solution)/shard_map/all_gather | solution.py:124
  7.9 123.7 %reduce-scatter.13.cloned.1.call-start = ((), (), s32[]{:S(2)}) async-start(), calls=%async_computation.9 | async-start | bytes 3932160 | tf_op jit(solution)/shard_map/reduce_scatter | solution.py:136
  8.0 32.9 %copy-start.26 = (s32[32,32]{1,0:T(8,128)}, s32[32,32]{1,0:T(8,128)S(1)}, u32[]{:S(2)}) copy-start(s32[32,32]{1,0:T(8,128)S(1)} %add_clamp_fusion) | copy-start | bytes 12292
  93.5 38.1 %copy-start.2 = (bf16[512,768]{1,0:T(8,128)(2,1)S(1)}, bf16[512,768]{1,0:T(8,128)(2,1)}, u32[]{:S(2)}) copy-start(bf16[512,768]{1,0:T(8,128)(2,1)} %param.19) | copy-start | bytes 2359300
  93.5 71.9 %all-gather.7.cloned.1.call-start = ((), (), s32[]{:S(2)}) async-start(), calls=%async_computation.10 | async-start | bytes 3932160 | tf_op jit(solution)/shard_map/all_gather | solution.py:148
  136.7 90.9 %reduce-scatter.15.cloned.1.call-start = ((), (), s32[]{:S(2)}) async-start(), calls=%async_computation.11 | async-start | bytes 3932160 | tf_op jit(solution)/shard_map/reduce_scatter | solution.py:154
  165.4 20.1 %copy-start.31 = (bf16[768,768]{1,0:T(8,128)(2,1)S(1)}, bf16[768,768]{1,0:T(8,128)(2,1)}, u32[]{:S(2)}) copy-start(bf16[768,768]{1,0:T(8,128)(2,1)} %param.30) | copy-start | bytes 3538948
  189.5 75.0 %all-gather.9.cloned.1.call-start = ((), (), s32[]{:S(2)}) async-start(), calls=%async_computation.12 | async-start | bytes 3932160 | tf_op jit(solution)/shard_map/all_gather | solution.py:165
  235.8 83.5 %reduce-scatter.17.cloned.1.call-start = ((), (), s32[]{:S(2)}) async-start(), calls=%async_computation.13 | async-start | bytes 3932160 | tf_op jit(solution)/shard_map/reduce_scatter | solution.py:176
  281.2 38.1 %copy-start.20 = (f32[512]{0:T(512)S(1)}, f32[512]{0:T(512)}, u32[]{:S(2)}) copy-start(f32[512]{0:T(512)} %copy-done.19) | copy-start | bytes 6148
  281.2 40.9 %copy-start.22 = (f32[512]{0:T(512)S(1)}, f32[512]{0:T(512)}, u32[]{:S(2)}) copy-start(f32[512]{0:T(512)} %copy-done.21) | copy-start | bytes 6148
  281.3 74.4 %all-gather.11.cloned.1.call-start = ((), (), s32[]{:S(2)}) async-start(), calls=%async_computation.14 | async-start | bytes 3932160 | tf_op jit(solution)/shard_map/all_gather | solution.py:187
  322.1 33.5 %copy-start.16 = (bf16[192,768]{1,0:T(8,128)(2,1)S(1)}, bf16[192,768]{1,0:T(8,128)(2,1)}, u32[]{:S(2)}) copy-start(bf16[192,768]{1,0:T(8,128)(2,1)} %param.24) | copy-start | bytes 884740
  326.9 232.6 %reduce-scatter.27.cloned.1.call-start = ((), (), s32[]{:S(2)}) async-start(), calls=%async_computation.19 | async-start | bytes 884736
  429.7 132.0 %reduce-scatter.25.cloned.1.call-start = ((), (), s32[]{:S(2)}) async-start(), calls=%async_computation.18 | async-start | bytes 2211840
  458.6 142.5 %reduce-scatter.19.cloned.1.call-start = ((), (), s32[]{:S(2)}) async-start(), calls=%async_computation.15 | async-start | bytes 3932160 | tf_op jit(solution)/shard_map/reduce_scatter | solution.py:219
  464.7 209.5 %reduce-scatter.21.cloned.1.call-start = ((), (), s32[]{:S(2)}) async-start(), calls=%async_computation.16 | async-start | bytes 2654208 | tf_op jit(solution)/shard_map/reduce_scatter | solution.py:232
  472.0 7.0 copy-start.25
  472.0 7.0 copy-start.24
  472.1 274.6 %reduce-scatter.23.cloned.1.call-start = ((), (), s32[]{:S(2)}) async-start(), calls=%async_computation.17 | async-start | bytes 2654208 | tf_op jit(solution)/shard_map/reduce_scatter | solution.py:233
  479.0 43.0 %copy-start.29 = (f32[768]{0:T(1024)S(1)}, f32[768]{0:T(1024)}, u32[]{:S(2)}) copy-start(f32[768]{0:T(1024)} %get-tuple-element.339) | copy-start | bytes 9220
  479.0 122.0 %copy-start.6 = (f32[512,768]{1,0:T(8,128)S(1)}, f32[512,768]{1,0:T(8,128)}, u32[]{:S(2)}) copy-start(f32[512,768]{1,0:T(8,128)} %copy-done.5) | copy-start | bytes 4718596
  519.5 227.1 %copy-start.1 = (bf16[768,768]{1,0:T(8,128)(2,1)S(1)}, bf16[768,768]{1,0:T(8,128)(2,1)}, u32[]{:S(2)}) copy-start(bf16[768,768]{1,0:T(8,128)(2,1)} %param.28) | copy-start | bytes 3538948
  (23 other events, 60.1 us)
Sparse Core Ops, SparseCore 0:
  9.6 31.2 all-gather.4
  93.7 37.9 reduce-scatter.12
  136.9 28.5 all-gather.6
  189.6 37.9 reduce-scatter.14
  235.9 28.5 all-gather.8
  281.4 37.9 reduce-scatter.16
  327.1 28.5 all-gather.10
  429.8 62.5 reduce-scatter.26
  495.9 65.7 reduce-scatter.24
  564.2 36.8 reduce-scatter.18
  605.2 69.0 reduce-scatter.20
  678.1 68.5 reduce-scatter.22
where the time goes:
time: 765 us; the launch traced here: 754 us
  waiting for transfers between devices  408 us (53%)
  matrix products  148 us (19%)
  blocking collectives  77.1 us (10%)
  local copies, waits for them, and re-layouts  67.8 us (9%)
  other arithmetic  36 us (5%)
  between operations  15 us (2%)
    reduce_scatter x1, waiting for transfers between devices, on_device(): lax.psum_scatter(grad_w_down, 'dp', scatter_dimension=1, tiled=True)  72.5 us
    reduce_scatter x1, waiting for transfers between devices, on_device(): lax.psum_scatter(grad_w_in, 'dp', scatter_dimension=0, tiled=True)  70.9 us
    psum x1, blocking collectives, on_device(): lax.psum((jnp.stack([grad_gain_one, grad_gain_two]), jnp.stack([grad_shif...  40.2 us
    reduce_scatter x1, waiting for transfers between devices, on_device(): lax.psum_scatter(jnp.einsum('tf,df->td', grad_pre, expand_weight, preferr...  38.1 us
    reduce_scatter x1, waiting for transfers between devices, on_device(): lax.psum_scatter(jnp.einsum('mte,mde->td', grad_packed, attend_weight, pr...  37.5 us
    psum x1, blocking collectives, on_device(): lax.psum((grad_b_qv, grad_b_in, grad_tables), 'dp')  36.9 us
    reduce_scatter x1, waiting for transfers between devices, on_device(): lax.psum_scatter(jnp.dot(context_rows, merge_weight, preferred_element_ty...  36.8 us
    reduce_scatter x1, waiting for transfers between devices, on_device(): lax.psum_scatter(jnp.dot(activation, reduce_weight, preferred_element_typ...  36.8 us
  transfers between devices with their start and end apart: 12, of which 11 were waited for; matrix products, arithmetic and copies ran while one was open for 8% of the time, Pallas kernels for 0%

commit v1 on v0

v1 whole, which is shorter than its diff:
```python
import math

import jax
import jax.numpy as jnp
from jax import lax
from jax.experimental import pallas as pl
from jax.experimental.pallas import tpu as pltpu
from jax.sharding import PartitionSpec as P

HEAD_DIM = 64
BUCKETS = 32
EPSILON = 1e-05
MASKED = -1000000000.0
BF = jnp.bfloat16
F32 = jnp.float32
VMEM_LIMIT = 60 * 1024 * 1024


def mm(a, b, da, db):
    return lax.dot_general(a, b, (((da,), (db,)), ((), ())), preferred_element_type=F32)


def nn(a, b):
    return mm(a, b, 1, 0)


def nt(a, b):
    return mm(a, b, 1, 1)


def tn(a, b):
    return mm(a, b, 0, 0)


def iota(shape, dim):
    return lax.broadcasted_iota(jnp.int32, shape, dim)


def page_scalars(pages_ref, half):
    total = jnp.int32(0)
    begin = jnp.int32(0)
    bounds = []
    for k in range(pages_ref.shape[1]):
        length = pages_ref[0, k]
        begin = begin + jnp.where(length == half, total, 0)
        total = total + length
        bounds.append(total)
    return begin, bounds


def page_numbers(places, bounds):
    number = jnp.zeros(places.shape, jnp.int32)
    for bound in bounds:
        number = number + (places >= bound).astype(jnp.int32)
    return number


def half_lanes(which):
    return ((iota((1, 128), 1) // HEAD_DIM) == which).astype(BF)


def norm_stats(signal):
    mean = jnp.mean(signal, axis=1, keepdims=True)
    center = signal - mean
    spread = jnp.mean(center * center, axis=1, keepdims=True)
    scale = lax.rsqrt(spread + EPSILON)
    return center * scale, scale


def norm_back(grad, hat, scale, gain):
    scaled = grad * gain
    return scale * (
        scaled
        - jnp.mean(scaled, axis=1, keepdims=True)
        - hat * jnp.mean(scaled * hat, axis=1, keepdims=True)
    )


def attend_forward_kernel(
    pages_ref, x_ref, cells_ref, aw_ref, shift_ref, pt_ref, mw_ref, ms_ref, gain_ref, nshift_ref,
    xr_ref, hot_ref, q_ref, k_ref, v_ref, p_ref, ctx_ref, nb_ref, hat_ref, scale_ref, acc_ref,
):
    step = pl.program_id(0)
    rows = x_ref.shape[0]
    half = rows // 2
    begin, bounds = page_scalars(pages_ref, half)

    @pl.when(step == 0)
    def _():
        perm = (iota((rows, rows), 1) == ((iota((rows, rows), 0) + begin) & (rows - 1))).astype(BF)
        xr_ref[...] = nn(perm, x_ref[...]).astype(BF)
        bucket = iota((BUCKETS, rows), 0)
        one = (cells_ref[0:1, :] == bucket).astype(BF)
        two = (cells_ref[1:2, :] == bucket).astype(BF)
        hot_ref[...] = nt(perm, jnp.concatenate([one, two, one, two], axis=0)).astype(BF)
        acc_ref[...] = jnp.zeros_like(acc_ref)

    local = shift_ref.shape[2]
    heads = local // HEAD_DIM
    for out_ref in (q_ref, k_ref, v_ref):
        out_ref[0, :, local:] = jnp.zeros((rows, 256 - local), BF)
    queries = (nn(xr_ref[...], aw_ref[0, 0]) + shift_ref[0, 0:1, :].astype(F32)).astype(BF)
    q_ref[0, :, :local] = queries * jnp.asarray(HEAD_DIM ** -0.5, BF)
    k_ref[0, :, :local] = nn(xr_ref[...], aw_ref[0, 1]).astype(BF)
    v_ref[0, :, :local] = (
        nn(xr_ref[...], aw_ref[0, 2]) + shift_ref[0, 1:2, :].astype(F32)
    ).astype(BF)
    left = nn(hot_ref[:, : 2 * BUCKETS], pt_ref[0]).astype(BF)
    col = page_numbers((iota((half, 1), 0) + (half + begin)) & (rows - 1), bounds)
    row = page_numbers((iota((1, half), 1) + (half + begin)) & (rows - 1), bounds)
    same = col == row
    for block in range(2):
        at = slice(block * half, (block + 1) * half)
        for pair in range(2):
            lanes = slice(pair * 128, (pair + 1) * 128)
            key_side = jnp.concatenate([k_ref[0, at, lanes], hot_ref[at, :]], axis=1)
            total = None
            for which in range(min(2, heads - 2 * pair)):
                keep = half_lanes(which)
                query_side = jnp.concatenate(
                    [q_ref[0, at, lanes] * keep, left[at, lanes] * keep], axis=1
                )
                scores = nt(key_side, query_side)
                if block == 1:
                    scores = jnp.where(same, scores, MASKED)
                weights = jnp.exp(scores - jnp.max(scores, axis=0, keepdims=True))
                probs = (weights * (1.0 / jnp.sum(weights, axis=0, keepdims=True))).astype(BF)
                p_ref[0, (2 * pair + which) * 2 + block] = probs
                part = tn(probs, v_ref[0, at, lanes]) * keep.astype(F32)
                total = part if total is None else total + part
            ctx_ref[0, at, lanes] = total.astype(BF)
    acc_ref[...] += nn(ctx_ref[0, :, :local], mw_ref[0])

    @pl.when(step == pl.num_programs(0) - 1)
    def _():
        resid = xr_ref[...].astype(F32) + acc_ref[...] + ms_ref[...].astype(F32)
        hat, scale = norm_stats(resid)
        hat_ref[...] = hat
        scale_ref[...] = scale
        normed = hat * gain_ref[0:1, :].astype(F32) + nshift_ref[0:1, :].astype(F32)
        nb_ref[...] = normed.astype(BF)


def hidden_forward_kernel(
    pages_ref, nb_ref, hat_ref, gain_ref, nshift_ref, ew_ref, es_ref, rw_ref, rs_ref, cot_ref,
    act_ref, slope_ref, out_ref, gtwo_ref, small_ref, acc_ref,
):
    step = pl.program_id(0)
    rows = nb_ref.shape[0]
    pre = nn(nb_ref[...], ew_ref[0]) + es_ref[0].astype(F32)
    gate = 0.5 * (1.0 + lax.erf(pre * (0.5 ** 0.5)))
    act_ref[0] = (pre * gate).astype(BF)
    slope_ref[0] = (
        gate + pre * (jnp.exp(-0.5 * (pre * pre)) * (1.0 / math.sqrt(2.0 * math.pi)))
    ).astype(BF)
    part = nn(act_ref[0], rw_ref[0])

    @pl.when(step == 0)
    def _():
        acc_ref[...] = part

    @pl.when(step > 0)
    def _():
        acc_ref[...] += part

    @pl.when(step == pl.num_programs(0) - 1)
    def _():
        begin, _unused = page_scalars(pages_ref, rows // 2)
        normed = hat_ref[...] * gain_ref[0:1, :].astype(F32) + nshift_ref[0:1, :].astype(F32)
        resid = normed + acc_ref[...] + rs_ref[...].astype(F32)
        hat, scale = norm_stats(resid)
        gain = gain_ref[1:2, :].astype(F32)
        result = (hat * gain + nshift_ref[1:2, :].astype(F32)).astype(BF)
        perm = (iota((rows, rows), 1) == ((iota((rows, rows), 0) + begin) & (rows - 1))).astype(BF)
        out_ref[...] = tn(perm, result).astype(BF)
        cot = nn(perm, cot_ref[...])
        grad = norm_back(cot, hat, scale, gain)
        gtwo_ref[...] = grad
        small_ref[0:1, :] = jnp.sum(cot * hat, axis=0, keepdims=True)
        small_ref[1:2, :] = jnp.sum(cot, axis=0, keepdims=True)
        small_ref[2:3, :] = jnp.sum(grad, axis=0, keepdims=True)
        small_ref[3:8, :] = jnp.zeros((5, small_ref.shape[1]), F32)


def hidden_backward_kernel(
    gtwo_ref, act_ref, slope_ref, rw_ref, ew_ref, nb_ref, hat_ref, scale_ref, gain_ref,
    grw_ref, gew_ref, ges_ref, gone_ref, small_ref, acc_ref, gb_ref,
):
    step = pl.program_id(0)

    @pl.when(step == 0)
    def _():
        gb_ref[...] = gtwo_ref[...].astype(BF)
        acc_ref[...] = gtwo_ref[...]

    grad_pre = (nt(gb_ref[...], rw_ref[0]) * slope_ref[0].astype(F32)).astype(BF)
    ges_ref[0] = jnp.sum(grad_pre.astype(F32), axis=0, keepdims=True)
    grw_ref[0] = tn(gb_ref[...], act_ref[0]).astype(BF)
    gew_ref[0] = tn(nb_ref[...], grad_pre).astype(BF)
    acc_ref[...] += nt(grad_pre, ew_ref[0])

    @pl.when(step == pl.num_programs(0) - 1)
    def _():
        grad = acc_ref[...]
        hat = hat_ref[...]
        gone = norm_back(grad, hat, scale_ref[...], gain_ref[0:1, :].astype(F32))
        gone_ref[...] = gone
        small_ref[0:1, :] = jnp.sum(grad * hat, axis=0, keepdims=True)
        small_ref[1:2, :] = jnp.sum(grad, axis=0, keepdims=True)
        small_ref[2:3, :] = jnp.sum(gone, axis=0, keepdims=True)
        small_ref[3:8, :] = jnp.zeros((5, small_ref.shape[1]), F32)


def attend_backward_kernel(
    pages_ref, gone_ref, mw_ref, ctx_ref, aw_ref, q_ref, k_ref, v_ref, p_ref, xr_ref, hot_ref,
    gmw_ref, gaw_ref, gsh_ref, gpair_ref, gin_ref, acc_ref, gb_ref, gc_ref, dq_ref, dk_ref, dv_ref, e_ref,
):
    step = pl.program_id(0)
    rows = gone_ref.shape[0]
    half = rows // 2
    local = mw_ref.shape[1]
    heads = local // HEAD_DIM

    @pl.when(step == 0)
    def _():
        gb_ref[...] = gone_ref[...].astype(BF)
        acc_ref[...] = gone_ref[...]
        gc_ref[:, local:] = jnp.zeros((rows, 256 - local), BF)

    gc_ref[:, :local] = nt(gb_ref[...], mw_ref[0]).astype(BF)
    gmw_ref[0] = tn(gb_ref[...], ctx_ref[0, :, :local]).astype(BF)
    for block in range(2):
        at = slice(block * half, (block + 1) * half)
        for pair in range(2):
            lanes = slice(pair * 128, (pair + 1) * 128)
            key_side = jnp.concatenate([k_ref[0, at, lanes], hot_ref[at, :]], axis=1)
            sums = None
            for which in range(min(2, heads - 2 * pair)):
                keep = half_lanes(which)
                wide = keep.astype(F32)
                probs = p_ref[0, (2 * pair + which) * 2 + block]
                grad_probs = nt(v_ref[0, at, lanes] * keep, gc_ref[at, lanes])
                soft = probs.astype(F32)
                inner = jnp.sum(soft * grad_probs, axis=0, keepdims=True)
                grad_scores = (soft * (grad_probs - inner)).astype(BF)
                both = tn(grad_scores, key_side)
                parts = (
                    both[:, :128] * wide,
                    both[:, 128:] * wide,
                    nn(grad_scores, q_ref[0, at, lanes]) * wide,
                    nn(probs, gc_ref[at, lanes]) * wide,
                )
                sums = parts if sums is None else tuple(a + b for a, b in zip(sums, parts))
            dq_ref[at, lanes] = (sums[0] * (HEAD_DIM ** -0.5)).astype(BF)
            e_ref[at, lanes] = sums[1].astype(BF)
            dk_ref[at, lanes] = sums[2].astype(BF)
            dv_ref[at, lanes] = sums[3].astype(BF)
    for m, d_ref in enumerate((dq_ref, dk_ref, dv_ref)):
        piece = d_ref[:, :local]
        gaw_ref[0, m] = tn(xr_ref[...], piece).astype(BF)
        acc_ref[...] += nt(piece, aw_ref[0, m])
    gsh_ref[0, 0:1, :] = jnp.sum(dq_ref[:, :local].astype(F32), axis=0, keepdims=True)
    gsh_ref[0, 1:2, :] = jnp.sum(dv_ref[:, :local].astype(F32), axis=0, keepdims=True)
    gpair_ref[0] = tn(hot_ref[:, : 2 * BUCKETS], e_ref[...])

    @pl.when(step == pl.num_programs(0) - 1)
    def _():
        begin, _unused = page_scalars(pages_ref, half)
        perm = (iota((rows, rows), 1) == ((iota((rows, rows), 0) + begin) & (rows - 1))).astype(BF)
        gin_ref[...] = tn(perm, acc_ref[...].astype(BF)).astype(BF)


def whole(shape):
    return pl.BlockSpec(shape, lambda i, *_: (0,) * len(shape))


def slot(shape, order=None):
    pick = order if order is not None else (lambda i: i)
    return pl.BlockSpec((1,) + shape, lambda i, *_: (pick(i),) + (0,) * len(shape))


def late_first(i):
    return 3 - 2 * i + 3 * (i // 2)


def swap(value, axis, size, bit):
    return lax.ppermute(value, axis, [(i, i ^ bit) for i in range(size)])


def gather_slots(shard):
    core = swap(shard, "tensor", 4, 1)
    far = swap(shard, "tensor", 4, 2)
    far_core = swap(far, "tensor", 4, 1)
    return jnp.stack([shard, core, far, far_core])


def reduce_slots(partial_sums, dp):
    add = lambda a, b: (a.astype(F32) + b.astype(F32))
    got = swap(partial_sums[1::2], "tensor", 4, 1)
    two = add(partial_sums[0::2], got).astype(BF)
    got = swap(two[1], "tensor", 4, 2)
    one = add(two[0], got)
    lead = one.shape[:-2]
    rows, cols = one.shape[-2:]
    bits = dp.bit_length() - 1
    one = one.reshape(lead + (2,) * bits + (rows // dp, cols))
    me = lax.axis_index("dp")
    for bit in range(bits):
        axis = one.ndim - 3
        mine = (me >> bit) & 1
        keep = lax.dynamic_index_in_dim(one, mine, axis, keepdims=False)
        send = lax.dynamic_index_in_dim(one, 1 - mine, axis, keepdims=False).astype(BF)
        one = add(keep, swap(send, "dp", dp, 1 << bit))
    return one


def on_device(
    dp,
    inputs,
    layout_cells,
    page_lengths,
    attend_weight,
    attend_shift,
    merge_weight,
    merge_shift,
    norm_gains,
    norm_shifts,
    expand_weight,
    expand_shift,
    reduce_weight,
    reduce_shift,
    bias_tables,
    cotangent,
):
    rows, width = inputs.shape
    local = attend_weight.shape[2]
    heads = bias_tables.shape[1]
    hidden = expand_weight.shape[1]
    me = lax.axis_index("tensor")
    pages = lax.dynamic_slice_in_dim(page_lengths, me, 1, 0)
    cells = lax.dynamic_slice_in_dim(layout_cells, me * rows, rows, 1)

    spot = jnp.arange(BUCKETS, dtype=jnp.int32)
    bucket_of = jnp.clip(spot[:, None] - spot[None, :] + BUCKETS // 2, 0, BUCKETS - 1)
    folding = (bucket_of[:, :, None] == spot[None, None, :]).astype(F32)
    pairs = jnp.einsum("xyb,ahb->ahxy", folding, bias_tables.astype(F32))
    own_pt = jnp.zeros((2, BUCKETS, 4, 2, BUCKETS), F32)
    for a in range(2):
        own_pt = own_pt.at[a, :, :heads, a, :].set(jnp.transpose(pairs[a], (1, 0, 2)))
    own_pt = own_pt.reshape(2 * BUCKETS, 256).astype(BF)

    pt = gather_slots(own_pt)
    shift = gather_slots(attend_shift)
    es = gather_slots(expand_shift.reshape(1, hidden))
    aw = gather_slots(attend_weight)
    mw = gather_slots(merge_weight)
    ew = gather_slots(expand_weight)
    rw = gather_slots(reduce_weight)
    ms = merge_shift.reshape(1, width)
    rs = reduce_shift.reshape(1, width)

    sds = jax.ShapeDtypeStruct
    smem = pl.BlockSpec(memory_space=pltpu.SMEM)
    params = pltpu.CompilerParams(vmem_limit_bytes=VMEM_LIMIT)
    xr, hot, q, k, v, p, ctx, nb, hat, scale = pl.pallas_call(
        attend_forward_kernel,
        grid=(4,),
        in_specs=[
            smem, whole((rows, width)), whole((2, rows)), slot((3, width, local)), slot((2, local)),
            slot((2 * BUCKETS, 256)), slot((local, width)), whole((1, width)), whole((2, width)),
            whole((2, width)),
        ],
        out_specs=[
            whole((rows, width)), whole((rows, 128)), slot((rows, 256)), slot((rows, 256)),
            slot((rows, 256)), slot((2 * heads, rows // 2, rows // 2)), slot((rows, 256)),
            whole((rows, width)), whole((rows, width)), whole((rows, 1)),
        ],
        out_shape=[
            sds((rows, width), BF), sds((rows, 128), BF), sds((4, rows, 256), BF),
            sds((4, rows, 256), BF), sds((4, rows, 256), BF),
            sds((4, 2 * heads, rows // 2, rows // 2), BF), sds((4, rows, 256), BF),
            sds((rows, width), BF), sds((rows, width), F32), sds((rows, 1), F32),
        ],
        scratch_shapes=[pltpu.VMEM((rows, width), F32)],
        compiler_params=params,
    )(pages, inputs, cells, aw, shift, pt, mw, ms, norm_gains, norm_shifts)

    act, slope, output, gtwo, small_two = pl.pallas_call(
        hidden_forward_kernel,
        grid=(4,),
        in_specs=[
            smem, whole((rows, width)), whole((rows, width)), whole((2, width)), whole((2, width)),
            slot((width, hidden)), slot((1, hidden)), slot((hidden, width)), whole((1, width)),
            whole((rows, width)),
        ],
        out_specs=[
            slot((rows, hidden)), slot((rows, hidden)), whole((rows, width)), whole((rows, width)),
            whole((8, width)),
        ],
        out_shape=[
            sds((4, rows, hidden), BF), sds((4, rows, hidden), BF), sds((rows, width), BF),
            sds((rows, width), F32), sds((8, width), F32),
        ],
        scratch_shapes=[pltpu.VMEM((rows, width), F32)],
        compiler_params=params,
    )(pages, nb, hat, norm_gains, norm_shifts, ew, es, rw, rs, cotangent)

    late = late_first
    grw, gew, ges, gone, small_one = pl.pallas_call(
        hidden_backward_kernel,
        grid=(4,),
        in_specs=[
            whole((rows, width)), slot((rows, hidden), late), slot((rows, hidden), late),
            slot((hidden, width), late), slot((width, hidden), late), whole((rows, width)),
            whole((rows, width)), whole((rows, 1)), whole((2, width)),
        ],
        out_specs=[
            slot((width, hidden), late), slot((width, hidden), late), slot((1, hidden), late),
            whole((rows, width)), whole((8, width)),
        ],
        out_shape=[
            sds((4, width, hidden), BF), sds((4, width, hidden), BF), sds((4, 1, hidden), F32),
            sds((rows, width), F32), sds((8, width), F32),
        ],
        scratch_shapes=[pltpu.VMEM((rows, width), F32), pltpu.VMEM((rows, width), BF)],
        compiler_params=params,
    )(gtwo, act, slope, rw, ew, nb, hat, scale, norm_gains)

    gmw, gaw, gsh, gpair, input_grad = pl.pallas_call(
        attend_backward_kernel,
        grid=(4,),
        in_specs=[
            smem, whole((rows, width)), slot((local, width), late), slot((rows, 256), late),
            slot((3, width, local), late), slot((rows, 256), late), slot((rows, 256), late),
            slot((rows, 256), late), slot((2 * heads, rows // 2, rows // 2), late),
            whole((rows, width)), whole((rows, 128)),
        ],
        out_specs=[
            slot((width, local), late), slot((3, width, local), late), slot((2, local), late),
            slot((2 * BUCKETS, 256), late), whole((rows, width)),
        ],
        out_shape=[
            sds((4, width, local), BF), sds((4, 3, width, local), BF), sds((4, 2, local), F32),
            sds((4, 2 * BUCKETS, 256), F32), sds((rows, width), BF),
        ],
        scratch_shapes=[
            pltpu.VMEM((rows, width), F32), pltpu.VMEM((rows, width), BF),
            pltpu.VMEM((rows, 256), BF), pltpu.VMEM((rows, 256), BF), pltpu.VMEM((rows, 256), BF),
            pltpu.VMEM((rows, 256), BF), pltpu.VMEM((rows, 256), BF),
        ],
        compiler_params=params,
    )(pages, gone, mw, ctx, aw, q, k, v, p, xr, hot)

    grad_rw = reduce_slots(grw, dp).T
    grad_ew = reduce_slots(gew, dp)
    grad_mw = reduce_slots(gmw, dp).T
    grad_aw = reduce_slots(gaw, dp)

    split = gpair.reshape(4, 2, BUCKETS, 4, 2, BUCKETS)
    grad_pairs = jnp.stack([split[:, a, :, :heads, a, :] for a in range(2)], axis=1)
    grad_tables = jnp.einsum("raxhy,xyb->rahb", grad_pairs, folding, precision=lax.Precision.HIGHEST)
    spare = -(2 * local + hidden + 2 * heads * BUCKETS) % width
    own = jnp.concatenate(
        [
            gsh.reshape(4, -1),
            ges.reshape(4, -1),
            grad_tables.reshape(4, -1),
            jnp.zeros((4, spare), F32),
        ],
        axis=1,
    ).reshape(4, -1, width)
    shared = jnp.concatenate([small_one[:3], small_two[:3]], axis=0)
    lines = own.shape[1]
    for bit, take in ((1, 2), (2, 1)):
        got = swap(jnp.concatenate([shared, own[1::2].reshape(-1, width)], axis=0), "tensor", 4, bit)
        shared = shared + got[:6]
        own = own[0::2] + got[6:].reshape(take, lines, width)
    both = jnp.concatenate([shared, own[0]], axis=0)
    for bit in range(dp.bit_length() - 1):
        both = both + swap(both, "dp", dp, 1 << bit)
    flat = both[6:].reshape(-1)
    cut = 2 * local + hidden
    return (
        output,
        input_grad,
        grad_aw,
        flat[: 2 * local].reshape(2, local),
        grad_mw,
        both[2],
        jnp.stack([both[0], both[3]]),
        jnp.stack([both[1], both[4]]),
        grad_ew,
        flat[2 * local : cut],
        grad_rw,
        both[5],
        flat[cut : cut + 2 * heads * BUCKETS].reshape(2, heads, BUCKETS),
    )


def solution(mesh):
    in_specs = (
        P(("dp", "tensor"), None),
        P(None, "dp"),
        P("dp", None),
        P(None, None, "tensor"),
        P(None, "tensor"),
        P("tensor", None),
        P(),
        P(),
        P(),
        P(None, "tensor"),
        P("tensor"),
        P("tensor", None),
        P(),
        P(None, "tensor", None),
        P(("dp", "tensor"), None),
    )
    out_specs = (
        P(("dp", "tensor"), None),
        P(("dp", "tensor"), None),
        P(None, "dp", "tensor"),
        P(None, "tensor"),
        P("tensor", "dp"),
        P(),
        P(),
        P(),
        P("dp", "tensor"),
        P("tensor"),
        P("tensor", "dp"),
        P(),
        P(None, "tensor", None),
    )

    def run(*arrays):
        return on_device(mesh.shape["dp"], *arrays)

    return jax.shard_map(
        run, mesh=mesh, in_specs=in_specs, out_specs=out_specs, check_vma=False
    )
```

time: 765 us -> 344 us (0.45); the launches traced: 754 us -> 343 us
  waiting for transfers between devices: 408 us -> 165 us
  matrix products: 148 us -> 1.97 us
  blocking collectives: 77.1 us -> 0 us
  Pallas kernels: 0 us -> 68.4 us
  starting transfers between devices: 1.95 us -> 36.7 us
  local copies, waits for them, and re-layouts: 67.8 us -> 35.7 us
  between operations: 15 us -> 1.38 us
    reduce_scatter x6 -> x0, waiting for transfers between devices: 293 us -> none  [the longest x1 72.5 us: on_device(): lax.psum_scatter(grad_w_down, 'dp', scatter_dimension=1, tiled=True)]
    ppermute x0 -> x46, waiting for transfers between devices: none -> 165 us  [swap(): return lax.ppermute(value, axis, [(i, i ^ bit) for i in range(size)])]
    dot_general x53 -> x2, matrix products: 142 us -> 1.97 us  [the longest x1 1.19 us: on_device(): pairs = jnp.einsum('xyb,ahb->ahxy', folding, bias_tables.astype(F32))]
    all_gather x4 -> x0, waiting for transfers between devices: 114 us -> none  [the longest x1 30.6 us: on_device(): gathered = lax.all_gather(inputs, 'tensor', axis=0, tiled=True)]
    psum x2 -> x0, blocking collectives: 77.1 us -> none  [the longest x1 40.2 us: on_device(): lax.psum((jnp.stack([grad_gain_one, grad_gain_two]), jnp.stack([grad_shif...]
    pallas_call x0 -> x4, Pallas kernels: none -> 68.4 us  [the longest x1 20.3 us: on_device(): pl.pallas_call(attend_backward_kernel, grid=(4,), in_specs=[smem, whole((...]
    ppermute x0 -> x46, starting transfers between devices: none -> 36.7 us  [swap(): return lax.ppermute(value, axis, [(i, i ^ bit) for i in range(size)])]
    reduce_sum x24 -> x0, other arithmetic: 19.1 us -> none  [the longest x4 7.56 us: layer_norm(): center = signal - jnp.mean(signal, axis=-1, keepdims=True)]
  transfers between devices with their start and end apart: 12 -> 46, of which waited for: 11 -> 21; matrix products, arithmetic and copies ran while one was open for 8% -> 18% of each run, Pallas kernels for 0% -> 4%
where the time goes in v1:
time: 344 us; the launch traced here: 343 us
  waiting for transfers between devices  165 us (48%)
  Pallas kernels  68.4 us (20%)
  starting transfers between devices  36.7 us (11%)
  local copies, waits for them, and re-layouts  35.7 us (10%)
  other arithmetic  34.6 us (10%)
    ppermute x46, waiting for transfers between devices, swap(): return lax.ppermute(value, axis, [(i, i ^ bit) for i in range(size)])  165 us
    ppermute x46, starting transfers between devices, swap(): return lax.ppermute(value, axis, [(i, i ^ bit) for i in range(size)])  36.7 us
    pallas_call x1, Pallas kernels, on_device(): pl.pallas_call(attend_backward_kernel, grid=(4,), in_specs=[smem, whole((...  20.3 us
    pallas_call x1, Pallas kernels, on_device(): pl.pallas_call(hidden_backward_kernel, grid=(4,), in_specs=[whole((rows,...  17.8 us
    pallas_call x1, Pallas kernels, on_device(): pl.pallas_call(attend_forward_kernel, grid=(4,), in_specs=[smem, whole((r...  15.2 us
    pallas_call x1, Pallas kernels, on_device(): pl.pallas_call(hidden_forward_kernel, grid=(4,), in_specs=[smem, whole((r...  15.1 us
    another operation x7, other arithmetic, gather_slots(): return jnp.stack([shard, core, far, far_core])  14.8 us
    ppermute x6, local copies, waits for them, and re-layouts, swap(): return lax.ppermute(value, axis, [(i, i ^ bit) for i in range(size)])  9.84 us
  transfers between devices with their start and end apart: 46, of which 21 were waited for; matrix products, arithmetic and copies ran while one was open for 18% of the time, Pallas kernels for 4%

profile of v1, /device:TPU:0, one launch (start us, length us, event | category | flops | bytes accessed | tf_op | source)
XLA Modules:
  0.0 343.3 jit_solution(17698618469199946839)
XLA Ops:
  0.7 3.0 collective-permute-start.4
  13.3 71.3 %collective-permute-done.7 = bf16[64,256]{1,0:T(8,128)(2,1)S(1)} collective-permute-done((bf16[64,256]{1,0:T(8,128)(2,1)S(1)}, bf16[64,256]{1,0:T(8,128)(2,1)S(1)}, u32[]{:S(2)}, u32[]{:S(2)}) %collective-permute-start.7) | collective-permute-done | bytes 32800 | tf_op jit(solution)/shard_map/ppermute | solution.py:287
  104.5 3.9 %pad_maximum_fusion.aw_ref = bf16[4,3,768,192]{3,2,1,0:T(8,128)(2,1)} fusion(bf16[1,3,768,192]{3,2,1,0:T(8,128)(2,1)} %bitcast.171, bf16[1,3,768,192]{3,2,1,0:T(8,128)(2,1)S(1)} %bitcast.169, bf16[1,3,768,192]{3,2,1,0:T(8,128)(2,1)S(1)} %bitcast.170, bf16[1,3,768,192]{3,2,1,0:T(8,128)(2,1)S(1)} %bitcast.168), kind=kLoop, calls=%fused_computation | loop fusion | flops 5308416 | bytes 7077888 | tf_op jit(solution)/shard_map/stack | solution.py:294
  108.4 15.2 %shard_map.246 = (bf16[512,768]{1,0:T(8,128)(2,1)}, bf16[512,128]{1,0:T(8,128)(2,1)}, bf16[4,512,256]{2,1,0:T(8,128)(2,1)}, bf16[4,512,256]{2,1,0:T(8,128)(2,1)}...) custom-call(s32[1,8]{1,0:T(1,128)} %constant_dynamic-slice_fusion.9., ...), custom_call_target="tpu_custom_call" | custom-call | tf_op jit(solution)/shard_map/pallas_call | solution.py:365
  123.6 3.8 %pad_maximum_fusion.1.ew_ref = bf16[4,768,768]{2,1,0:T(8,128)(2,1)} fusion(bf16[1,768,768]{2,1,0:T(8,128)(2,1)} %bitcast.28, bf16[1,768,768]{2,1,0:T(8,128)(2,1)} %bitcast.27, bf16[1,768,768]{2,1,0:T(8,128)(2,1)} %bitcast.26, bf16[1,768,768]{2,1,0:T(8,128)(2,1)S(1)} %bitcast.174), kind=kLoop, calls=%fused_computation.1 | loop fusion | flops 7077888 | bytes 9437184 | tf_op jit(solution)/shard_map/stack | solution.py:294
  127.5 4.0 %pad_maximum_fusion.2.rw_ref = bf16[4,768,768]{2,1,0:T(8,128)(2,1)} fusion(bf16[1,768,768]{2,1,0:T(8,128)(2,1)} %bitcast.35, bf16[1,768,768]{2,1,0:T(8,128)(2,1)} %bitcast.34, bf16[1,768,768]{2,1,0:T(8,128)(2,1)} %bitcast.33, bf16[1,768,768]{2,1,0:T(8,128)(2,1)} %bitcast.32), kind=kLoop, calls=%fused_computation.2 | loop fusion | flops 7077888 | bytes 9437184 | tf_op jit(solution)/shard_map/stack | solution.py:294
  131.5 15.1 %shard_map.247 = (bf16[4,512,768]{2,1,0:T(8,128)(2,1)}, bf16[4,512,768]{2,1,0:T(8,128)(2,1)}, bf16[512,768]{1,0:T(8,128)(2,1)}, f32[512,768]{1,0:T(8,128)}, f32[8,768]{1,0:T(8,128)}) custom-call(s32[1,8]{1,0:T(1,128)} %constant_dynamic-slice_fusion.9.pages_ref, bf16[512,768]{1,0:T(8,128)(2,1)} %get-tuple-element.62.nb_ref, ...), custom_call_target="tpu_custom_call" | custom-call | tf_op jit(solution)/shard_map/pallas_call | solution.py:388
  146.6 17.8 %shard_map.248 = (bf16[4,768,768]{2,1,0:T(8,128)(2,1)}, bf16[4,768,768]{2,1,0:T(8,128)(2,1)}, f32[4,1,768]{2,1,0:T(1,128)}, f32[512,768]{1,0:T(8,128)}, f32[8,768]{1,0:T(8,128)}) custom-call(f32[512,768]{1,0:T(8,128)} %get-tuple-element.65.gtwo_ref, bf16[4,512,768]{2,1,0:T(8,128)(2,1)} %get-tuple-element.66.act_ref, ...), custom_call_target="tpu_custom_call" | custom-call | tf_op jit(solution)/shard_map/pallas_call | solution.py:409
  164.4 20.3 %shard_map.249 = (bf16[4,768,192]{2,1,0:T(8,128)(2,1)}, bf16[4,3,768,192]{3,2,1,0:T(8,128)(2,1)}, f32[4,2,192]{2,1,0:T(2,128)}, f32[4,64,256]{2,1,0:T(8,128)}, bf16[512,768]{1,0:T(8,128)(2,1)}) custom-call(s32[1,8]{1,0:T(1,128)} %constant_dynamic-slice_fusion.9.pages_ref, f32[512,768]{1,0:T(8,128)} %get-tuple-element.69.gone_ref, ...), custom_call_target="tpu_custom_call" | custom-call | tf_op jit(solution)/shard_map/pallas_call | solution.py:429
  202.3 2.8 collective-permute-start.30
  205.1 3.4 slice.237
  211.9 2.3 copy.71
  219.9 8.3 %collective-permute-done.32 = bf16[768,192]{1,0:T(8,128)(2,1)S(1)} collective-permute-done((bf16[768,192]{1,0:T(8,128)(2,1)S(1)}, bf16[768,192]{1,0:T(8,128)(2,1)S(1)}, u32[]{:S(2)}, u32[]{:S(2)}) %collective-permute-start.32) | collective-permute-done | bytes 294944 | tf_op jit(solution)/shard_map/ppermute | solution.py:287
  236.3 2.7 copy.72
  246.7 2.9 add_convert_fusion
  251.2 15.8 %collective-permute-done.22 = bf16[3,768,192]{1,2,0:T(8,128)(2,1)} collective-permute-done((bf16[3,768,192]{1,2,0:T(8,128)(2,1)}, bf16[3,768,192]{1,2,0:T(8,128)(2,1)}, u32[]{:S(2)}, u32[]{:S(2)}) %collective-permute-start.22) | collective-permute-done | bytes 884768 | tf_op jit(solution)/shard_map/ppermute | solution.py:287
  271.6 2.9 add_convert_fusion.1
  276.3 3.8 %collective-permute-done.23 = bf16[3,2,2,96,192]{4,3,0,1,2:T(8,128)(2,1)S(1)} collective-permute-done((bf16[3,2,2,96,192]{4,3,0,1,2:T(8,128)(2,1)S(1)}, bf16[3,2,2,96,192]{4,3,0,1,2:T(8,128)(2,1)S(1)}, u32[]{:S(2)}, u32[]{:S(2)}) %collective-permute-start.23) | collective-permute-done | bytes 442400 | tf_op jit(solution)/shard_map/ppermute | solution.py:287
  282.2 6.2 %collective-permute-done.24 = bf16[3,2,96,192]{3,2,0,1:T(8,128)(2,1)S(1)} collective-permute-done((bf16[3,2,96,192]{3,2,0,1:T(8,128)(2,1)S(1)}, bf16[3,2,96,192]{3,2,0,1:T(8,128)(2,1)S(1)}, u32[]{:S(2)}, u32[]{:S(2)}) %collective-permute-start.24) | collective-permute-done | bytes 221216 | tf_op jit(solution)/shard_map/ppermute | solution.py:287
  288.6 3.6 %collective-permute-done.42 = bf16[768,768]{1,0:T(8,128)(2,1)} collective-permute-done((bf16[768,768]{1,0:T(8,128)(2,1)}, bf16[768,768]{1,0:T(8,128)(2,1)}, u32[]{:S(2)}, u32[]{:S(2)}) %collective-permute-start.42) | collective-permute-done | bytes 1179680 | tf_op jit(solution)/shard_map/ppermute | solution.py:287
  295.4 19.0 %collective-permute-done.37 = bf16[768,768]{1,0:T(8,128)(2,1)S(1)} collective-permute-done((bf16[768,768]{1,0:T(8,128)(2,1)S(1)}, bf16[768,768]{1,0:T(8,128)(2,1)S(1)}, u32[]{:S(2)}, u32[]{:S(2)}) %collective-permute-start.37) | collective-permute-done | bytes 1179680 | tf_op jit(solution)/shard_map/ppermute | solution.py:287
  317.8 9.4 %collective-permute-done.38 = bf16[2,2,96,768]{3,2,0,1:T(8,128)(2,1)S(1)} collective-permute-done((bf16[2,2,96,768]{3,2,0,1:T(8,128)(2,1)S(1)}, bf16[2,2,96,768]{3,2,0,1:T(8,128)(2,1)S(1)}, u32[]{:S(2)}, u32[]{:S(2)}) %collective-permute-start.38) | collective-permute-done | bytes 589856 | tf_op jit(solution)/shard_map/ppermute | solution.py:287
  328.3 7.3 %collective-permute-done.39 = bf16[2,96,768]{2,1,0:T(8,128)(2,1)S(1)} collective-permute-done((bf16[2,96,768]{2,1,0:T(8,128)(2,1)S(1)}, bf16[2,96,768]{2,1,0:T(8,128)(2,1)S(1)}, u32[]{:S(2)}, u32[]{:S(2)}) %collective-permute-start.39) | collective-permute-done | bytes 294944 | tf_op jit(solution)/shard_map/ppermute | solution.py:287
  338.0 4.5 %collective-permute-done.40 = bf16[96,768]{1,0:T(8,128)(2,1)S(1)} collective-permute-done((bf16[96,768]{1,0:T(8,128)(2,1)S(1)}, bf16[96,768]{1,0:T(8,128)(2,1)S(1)}, u32[]{:S(2)}, u32[]{:S(2)}) %collective-permute-start.40) | collective-permute-done | bytes 147488 | tf_op jit(solution)/shard_map/ppermute | solution.py:287
  (227 shorter events, 92.5 us)
Async XLA Ops:
  4.9 85.6 %collective-permute-start.13 = (bf16[768,768]{1,0:T(8,128)(2,1)}, bf16[768,768]{1,0:T(8,128)(2,1)}, u32[]{:S(2)}, u32[]{:S(2)}) collective-permute-start(bf16[768,768]{1,0:T(8,128)(2,1)} %param.28), channel_id=1, source_target_pairs={{0,2},{1,3},{2,0},{3,1},{4,6},{5,7},{6,4},{7,5},{8,10},{9,11},{10,... | collective-permute-start | bytes 3538952 | tf_op jit(solution)/shard_map/ppermute | solution.py:287
  6.7 82.2 %collective-permute-start.1 = (bf16[3,768,192]{1,2,0:T(8,128)(2,1)}, bf16[3,768,192]{1,2,0:T(8,128)(2,1)}, u32[]{:S(2)}, u32[]{:S(2)}) collective-permute-start(bf16[3,768,192]{1,2,0:T(8,128)(2,1)} %param.22), channel_id=1, source_target_pairs={{0,2},{1,3},{2,0},{3,1},{4,6},{5,7},{6,4},{7,5},{8,10},{9,11},{10,... | collective-permute-start | bytes 2654216 | tf_op jit(solution)/shard_map/ppermute | solution.py:287
  8.7 78.4 %collective-permute-start.10 = (bf16[192,768]{1,0:T(8,128)(2,1)}, bf16[192,768]{1,0:T(8,128)(2,1)S(1)}, u32[]{:S(2)}, u32[]{:S(2)}) collective-permute-start(bf16[192,768]{1,0:T(8,128)(2,1)} %param.24), channel_id=1, source_target_pairs={{0,2},{1,3},{2,0},{3,1},{4,6},{5,7},{6,4},{7,5},{8,10},{9,11},{10,... | collective-permute-start | bytes 884744 | tf_op jit(solution)/shard_map/ppermute | solution.py:287
  10.1 86.2 %collective-permute-start.19 = (bf16[768,768]{1,0:T(8,128)(2,1)}, bf16[768,768]{1,0:T(8,128)(2,1)}, u32[]{:S(2)}, u32[]{:S(2)}) collective-permute-start(bf16[768,768]{1,0:T(8,128)(2,1)} %param.30), channel_id=1, source_target_pairs={{0,2},{1,3},{2,0},{3,1},{4,6},{5,7},{6,4},{7,5},{8,10},{9,11},{10,... | collective-permute-start | bytes 3538952 | tf_op jit(solution)/shard_map/ppermute | solution.py:287
  12.0 72.6 %collective-permute-start.7 = (bf16[64,256]{1,0:T(8,128)(2,1)S(1)}, bf16[64,256]{1,0:T(8,128)(2,1)S(1)}, u32[]{:S(2)}, u32[]{:S(2)}) collective-permute-start(bf16[64,256]{1,0:T(8,128)(2,1)S(1)} %convert_element_type.200), channel_id=1, source_target_pairs={{0,2},{1,3},{2,0},{3,1},{4,6},{5,7},{6,4},{7,5},{8,10},{9,11},{10,... | collective-permute-start | bytes 98312 | tf_op jit(solution)/shard_map/ppermute | solution.py:287
  89.0 13.2 %collective-permute-start.2 = (bf16[3,768,192]{1,2,0:T(8,128)(2,1)}, bf16[3,768,192]{1,2,0:T(8,128)(2,1)}, u32[]{:S(2)}, u32[]{:S(2)}) collective-permute-start(bf16[3,768,192]{1,2,0:T(8,128)(2,1)} %collective-permute-done.1), channel_id=1, source_target_pairs={{0,1},{1,0},{2,3},{3,2},{4,5},{5,4},{6,7},{7,6},{8,9},{9,8},{10,11... | collective-permute-start | bytes 2654216 | tf_op jit(solution)/shard_map/ppermute | solution.py:287
  90.4 33.2 %collective-permute-start.12 = (bf16[768,768]{1,0:T(8,128)(2,1)}, bf16[768,768]{1,0:T(8,128)(2,1)}, u32[]{:S(2)}, u32[]{:S(2)}) collective-permute-start(bf16[768,768]{1,0:T(8,128)(2,1)} %param.28), channel_id=1, source_target_pairs={{0,1},{1,0},{2,3},{3,2},{4,5},{5,4},{6,7},{7,6},{8,9},{9,8},{10,11... | collective-permute-start | bytes 3538952 | tf_op jit(solution)/shard_map/ppermute | solution.py:287
  90.5 33.1 %collective-permute-start.14 = (bf16[768,768]{1,0:T(8,128)(2,1)}, bf16[768,768]{1,0:T(8,128)(2,1)}, u32[]{:S(2)}, u32[]{:S(2)}) collective-permute-start(bf16[768,768]{1,0:T(8,128)(2,1)} %collective-permute-done.13), channel_id=1, source_target_pairs={{0,1},{1,0},{2,3},{3,2},{4,5},{5,4},{6,7},{7,6},{8,9},{9,8},{10,11... | collective-permute-start | bytes 3538952 | tf_op jit(solution)/shard_map/ppermute | solution.py:287
  96.2 31.3 %collective-permute-start.18 = (bf16[768,768]{1,0:T(8,128)(2,1)}, bf16[768,768]{1,0:T(8,128)(2,1)}, u32[]{:S(2)}, u32[]{:S(2)}) collective-permute-start(bf16[768,768]{1,0:T(8,128)(2,1)} %param.30), channel_id=1, source_target_pairs={{0,1},{1,0},{2,3},{3,2},{4,5},{5,4},{6,7},{7,6},{8,9},{9,8},{10,11... | collective-permute-start | bytes 3538952 | tf_op jit(solution)/shard_map/ppermute | solution.py:287
  96.3 31.2 %collective-permute-start.20 = (bf16[768,768]{1,0:T(8,128)(2,1)}, bf16[768,768]{1,0:T(8,128)(2,1)}, u32[]{:S(2)}, u32[]{:S(2)}) collective-permute-start(bf16[768,768]{1,0:T(8,128)(2,1)} %collective-permute-done.19), channel_id=1, source_target_pairs={{0,1},{1,0},{2,3},{3,2},{4,5},{5,4},{6,7},{7,6},{8,9},{9,8},{10,11... | collective-permute-start | bytes 3538952 | tf_op jit(solution)/shard_map/ppermute | solution.py:287
  192.1 23.3 %collective-permute-start.31 = (bf16[2,768,192]{1,2,0:T(8,128)(2,1)S(1)}, bf16[2,768,192]{1,2,0:T(8,128)(2,1)S(1)}, u32[]{:S(2)}, u32[]{:S(2)}) collective-permute-start(bf16[2,768,192]{1,2,0:T(8,128)(2,1)S(1)} %copy.80), channel_id=1, source_target_pairs={{0,1},{1,0},{2,3},{3,2},{4,5},{5,4},{6,7},{7,6},{8,9},{9,8},{10,11... | collective-permute-start | bytes 1769480 | tf_op jit(solution)/shard_map/ppermute | solution.py:287
  202.3 12.4 %collective-permute-start.30 = (f32[8,768]{1,0:T(8,128)}, f32[8,768]{1,0:T(8,128)}, u32[]{:S(2)}, u32[]{:S(2)}) collective-permute-start(f32[8,768]{1,0:T(8,128)} %add.173), channel_id=1, source_target_pairs={{0,16},{4,20},{8,24},{12,28},{16,0},{20,4},{24,8},{28,12},{1,17},{... | collective-permute-start | bytes 73736 | tf_op jit(solution)/shard_map/ppermute | solution.py:287
  208.5 38.1 %collective-permute-start.41 = (bf16[2,768,768]{2,1,0:T(8,128)(2,1)}, bf16[2,768,768]{2,1,0:T(8,128)(2,1)}, u32[]{:S(2)}, u32[]{:S(2)}) collective-permute-start(bf16[2,768,768]{2,1,0:T(8,128)(2,1)} %slice.237), channel_id=1, source_target_pairs={{0,1},{1,0},{2,3},{3,2},{4,5},{5,4},{6,7},{7,6},{8,9},{9,8},{10,11... | collective-permute-start | bytes 7077896 | tf_op jit(solution)/shard_map/ppermute | solution.py:287
  210.1 61.5 %collective-permute-start.36 = (bf16[2,768,768]{2,1,0:T(8,128)(2,1)}, bf16[2,768,768]{2,1,0:T(8,128)(2,1)}, u32[]{:S(2)}, u32[]{:S(2)}) collective-permute-start(bf16[2,768,768]{2,1,0:T(8,128)(2,1)} %slice.232), channel_id=1, source_target_pairs={{0,1},{1,0},{2,3},{3,2},{4,5},{5,4},{6,7},{7,6},{8,9},{9,8},{10,11... | collective-permute-start | bytes 7077896 | tf_op jit(solution)/shard_map/ppermute | solution.py:287
  214.2 22.1 %collective-permute-start.21 = (bf16[2,3,768,192]{2,3,1,0:T(8,128)(2,1)}, bf16[2,3,768,192]{2,3,1,0:T(8,128)(2,1)}, u32[]{:S(2)}, u32[]{:S(2)}) collective-permute-start(bf16[2,3,768,192]{2,3,1,0:T(8,128)(2,1)} %copy.71), channel_id=1, source_target_pairs={{0,1},{1,0},{2,3},{3,2},{4,5},{5,4},{6,7},{7,6},{8,9},{9,8},{10,11... | collective-permute-start | bytes 5308424 | tf_op jit(solution)/shard_map/ppermute | solution.py:287
  217.1 11.1 %collective-permute-start.32 = (bf16[768,192]{1,0:T(8,128)(2,1)S(1)}, bf16[768,192]{1,0:T(8,128)(2,1)S(1)}, u32[]{:S(2)}, u32[]{:S(2)}) collective-permute-start(bf16[768,192]{1,0:T(8,128)(2,1)S(1)} %slice_bitcast_fusion.6), channel_id=1, source_target_pairs={{0,2},{1,3},{2,0},{3,1},{4,6},{5,7},{6,4},{7,5},{8,10},{9,11},{10,... | collective-permute-start | bytes 884744 | tf_op jit(solution)/shard_map/ppermute | solution.py:287
  234.7 10.9 %collective-permute-start.34 = (bf16[2,96,192]{1,2,0:T(8,128)(2,1)S(1)}, bf16[2,96,192]{1,2,0:T(8,128)(2,1)S(1)}, u32[]{:S(2)}, u32[]{:S(2)}) collective-permute-start(bf16[2,96,192]{1,2,0:T(8,128)(2,1)S(1)} %fusion.19), channel_id=1, source_target_pairs={{0,8},{4,12},{8,0},{12,4},{16,24},{20,28},{24,16},{28,20},{1,9},{5... | collective-permute-start | bytes 221192 | tf_op jit(solution)/shard_map/ppermute | solution.py:287
  244.1 22.9 %collective-permute-start.22 = (bf16[3,768,192]{1,2,0:T(8,128)(2,1)}, bf16[3,768,192]{1,2,0:T(8,128)(2,1)}, u32[]{:S(2)}, u32[]{:S(2)}) collective-permute-start(bf16[3,768,192]{1,2,0:T(8,128)(2,1)} %copy.73), channel_id=1, source_target_pairs={{0,2},{1,3},{2,0},{3,1},{4,6},{5,7},{6,4},{7,5},{8,10},{9,11},{10,... | collective-permute-start | bytes 2654216 | tf_op jit(solution)/shard_map/ppermute | solution.py:287
  246.3 34.5 %collective-permute-start.35 = (bf16[96,192]{0,1:T(8,128)(2,1)}, bf16[96,192]{0,1:T(8,128)(2,1)}, u32[]{:S(2)}, u32[]{:S(2)}) collective-permute-start(bf16[96,192]{0,1:T(8,128)(2,1)} %fusion.21), channel_id=1, source_target_pairs={{0,16},{4,20},{8,24},{12,28},{16,0},{20,4},{24,8},{28,12},{1,17},{... | collective-permute-start | bytes 110600 | tf_op jit(solution)/shard_map/ppermute | solution.py:287
  250.7 41.6 %collective-permute-start.42 = (bf16[768,768]{1,0:T(8,128)(2,1)}, bf16[768,768]{1,0:T(8,128)(2,1)}, u32[]{:S(2)}, u32[]{:S(2)}) collective-permute-start(bf16[768,768]{1,0:T(8,128)(2,1)} %slice_bitcast_fusion), channel_id=1, source_target_pairs={{0,2},{1,3},{2,0},{3,1},{4,6},{5,7},{6,4},{7,5},{8,10},{9,11},{10,... | collective-permute-start | bytes 3538952 | tf_op jit(solution)/shard_map/ppermute | solution.py:287
  274.7 39.7 %collective-permute-start.37 = (bf16[768,768]{1,0:T(8,128)(2,1)S(1)}, bf16[768,768]{1,0:T(8,128)(2,1)S(1)}, u32[]{:S(2)}, u32[]{:S(2)}) collective-permute-start(bf16[768,768]{1,0:T(8,128)(2,1)S(1)} %slice_bitcast_fusion.2), channel_id=1, source_target_pairs={{0,2},{1,3},{2,0},{3,1},{4,6},{5,7},{6,4},{7,5},{8,10},{9,11},{10,... | collective-permute-start | bytes 3538952 | tf_op jit(solution)/shard_map/ppermute | solution.py:287
  288.6 27.8 %collective-permute-start.25 = (bf16[3,96,192]{2,1,0:T(8,128)(2,1)S(1)}, bf16[3,96,192]{2,1,0:T(8,128)(2,1)S(1)}, u32[]{:S(2)}, u32[]{:S(2)}) collective-permute-start(bf16[3,96,192]{2,1,0:T(8,128)(2,1)S(1)} %fusion.16), channel_id=1, source_target_pairs={{0,16},{4,20},{8,24},{12,28},{16,0},{20,4},{24,8},{28,12},{1,17},{... | collective-permute-start | bytes 331784 | tf_op jit(solution)/shard_map/ppermute | solution.py:287
  293.8 23.3 %collective-permute-start.43 = (bf16[2,2,96,768]{3,2,0,1:T(8,128)(2,1)S(1)}, bf16[2,2,96,768]{3,2,0,1:T(8,128)(2,1)S(1)}, u32[]{:S(2)}, u32[]{:S(2)}) collective-permute-start(bf16[2,2,96,768]{3,2,0,1:T(8,128)(2,1)S(1)} %fusion.2), channel_id=1, source_target_pairs={{0,4},{4,0},{8,12},{12,8},{16,20},{20,16},{24,28},{28,24},{1,5},{5... | collective-permute-start | bytes 1769480 | tf_op jit(solution)/shard_map/ppermute | solution.py:287
  314.8 12.4 %collective-permute-start.38 = (bf16[2,2,96,768]{3,2,0,1:T(8,128)(2,1)S(1)}, bf16[2,2,96,768]{3,2,0,1:T(8,128)(2,1)S(1)}, u32[]{:S(2)}, u32[]{:S(2)}) collective-permute-start(bf16[2,2,96,768]{3,2,0,1:T(8,128)(2,1)S(1)} %fusion.1), channel_id=1, source_target_pairs={{0,4},{4,0},{8,12},{12,8},{16,20},{20,16},{24,28},{28,24},{1,5},{5... | collective-permute-start | bytes 1769480 | tf_op jit(solution)/shard_map/ppermute | solution.py:287
  (43 other events, 750.6 us)

commit v2 on v1

v2 whole, which is shorter than its diff:
```python
import math

import jax
import jax.numpy as jnp
from jax import lax
from jax.experimental import pallas as pl
from jax.experimental.pallas import tpu as pltpu
from jax.sharding import PartitionSpec as P

HEAD_DIM = 64
BUCKETS = 32
EPSILON = 1e-05
MASKED = -1000000000.0
BF = jnp.bfloat16
F32 = jnp.float32
VMEM_LIMIT = 60 * 1024 * 1024


def mm(a, b, da, db):
    return lax.dot_general(a, b, (((da,), (db,)), ((), ())), preferred_element_type=F32)


def nn(a, b):
    return mm(a, b, 1, 0)


def nt(a, b):
    return mm(a, b, 1, 1)


def tn(a, b):
    return mm(a, b, 0, 0)


def iota(shape, dim):
    return lax.broadcasted_iota(jnp.int32, shape, dim)


def page_scalars(pages_ref, line, half):
    total = jnp.int32(0)
    begin = jnp.int32(0)
    bounds = []
    for k in range(pages_ref.shape[1]):
        length = pages_ref[line, k]
        begin = begin + jnp.where(length == half, total, 0)
        total = total + length
        bounds.append(total)
    return begin, bounds


def page_numbers(places, bounds):
    number = jnp.zeros(places.shape, jnp.int32)
    for bound in bounds:
        number = number + (places >= bound).astype(jnp.int32)
    return number


def half_lanes(which):
    return ((iota((1, 128), 1) // HEAD_DIM) == which).astype(BF)


def norm_stats(signal):
    mean = jnp.mean(signal, axis=1, keepdims=True)
    center = signal - mean
    spread = jnp.mean(center * center, axis=1, keepdims=True)
    scale = lax.rsqrt(spread + EPSILON)
    return center * scale, scale


def norm_back(grad, hat, scale, gain):
    scaled = grad * gain
    return scale * (
        scaled
        - jnp.mean(scaled, axis=1, keepdims=True)
        - hat * jnp.mean(scaled * hat, axis=1, keepdims=True)
    )


MESH = pl.DeviceIdType.MESH
SMALL_ROWS = 16


class Net:
    def __init__(self, bits):
        t = lax.axis_index("tensor")
        d = lax.axis_index("dp")
        self.t = t
        self.core = {"tensor": t + 1 - 2 * (t % 2)}
        self.y = {"tensor": (t + 2) % 4}
        self.bit = [(d // 2 ** b) % 2 for b in bits]
        self.dp = [{"dp": d + 2 ** b * (1 - 2 * k)} for b, k in zip(bits, self.bit)]


def remote(source, target, sems, index, partner):
    return pltpu.make_async_remote_copy(
        src_ref=source,
        dst_ref=target,
        send_sem=sems.at[0, index],
        recv_sem=sems.at[1, index],
        device_id=partner,
        device_id_type=MESH,
    )


def rows_at(ref, start, count):
    return ref.at[pl.ds(pl.multiple_of(start, 16), count), :]


class Piece:
    def __init__(self, net, number, own, slots, start, count, x_first, sems):
        self.net, self.number, self.own, self.slots = net, number, own, slots
        self.start, self.count, self.x_first = start, count, x_first
        self.y_sems, self.one_sems, self.two_sems, self.core_sems = sems
        self.first, self.second = (0, 1) if x_first else (1, 0)

    def quarter(self, ref, flip):
        net = self.net
        fast = net.bit[self.first]
        if flip:
            fast = 1 - fast
        index = net.bit[self.second] * 2 + fast
        return rows_at(ref, self.start + index * (self.count // 4), self.count // 4)

    def half(self, ref, flip):
        slow = self.net.bit[self.second]
        if flip:
            slow = 1 - slow
        return rows_at(ref, self.start + slow * (self.count // 2), self.count // 2)

    def full(self, ref):
        return rows_at(ref, self.start, self.count)

    def over_y(self):
        return remote(
            self.quarter(self.own, False), self.quarter(self.slots(2), False),
            self.y_sems, self.number, self.net.y,
        )

    def hop_one(self, flip=False):
        here = self.quarter(self.slots(2), flip)
        return remote(here, here, self.one_sems, self.number, self.net.dp[self.first])

    def hop_two(self, flip=False):
        here = self.half(self.slots(2), flip)
        return remote(here, here, self.two_sems, self.number, self.net.dp[self.second])

    def to_core(self):
        return remote(
            self.full(self.slots(2)), self.full(self.slots(3)),
            self.core_sems, self.number, self.net.core,
        )

    def event(self, stage):
        if stage == 0:
            self.over_y().start()
        elif stage == 1:
            self.over_y().wait_recv()
            self.hop_one().start()
        elif stage == 2:
            self.hop_one(True).wait_recv()
            self.hop_two().start()
        elif stage == 3:
            self.hop_two(True).wait_recv()
            self.to_core().start()
        elif stage == 4:
            self.to_core().wait_recv()
        else:
            self.over_y().wait_send()
            self.hop_one().wait_send()
            self.hop_two().wait_send()
            self.to_core().wait_send()


def at_step(index, table):
    for value, actions in table.items():

        @pl.when(index == value)
        def _():
            for action in actions:
                action()


def layer_kernel(
    bits,
    pages_ref, x_ref, cells_ref, shift_ref, es_ref, tables_ref, ms_ref, rs_ref, gain_ref, nshift_ref,
    aw_hbm, mw_hbm, ew_hbm, rw_hbm, cot_hbm,
    out_ref, gin_ref, small_ref, ges_ref, gsh_ref, gpair_ref, grw_hbm, gew_hbm, gat_hbm,
    AW, MW, EW, RW, XR, HOT, Q, K, V, PR, CTX, NB, HAT, SCALE, AS, ACC, GB, GC, DQ, DK, DV, E, DD, SM,
    y_sems, one_sems, two_sems, core_sems, own_sems, small_sems, local_sems,
):
    net = Net(bits)
    rows, width = x_ref.shape
    half = rows // 2
    local = aw_hbm.shape[2]
    heads = local // HEAD_DIM
    hidden = ew_hbm.shape[1]

    barrier = pltpu.get_barrier_semaphore()
    greeted = (net.core, net.y, net.dp[0], net.dp[1])
    for partner in greeted:
        pl.semaphore_signal(barrier, inc=1, device_id=partner, device_id_type=MESH)

    SM[0, 0:2, :local] = shift_ref[...].astype(F32)
    SM[0, 2:3, :] = es_ref[...].astype(F32)
    SM[0, 8 : 8 + 2 * heads, :BUCKETS] = tables_ref[...].astype(F32)

    plan = []
    sems = (y_sems, one_sems, two_sems, core_sems)
    for m in range(3):
        plan.append((aw_hbm.at[m], (lambda s, m=m: AW.at[s, m]), 0, width, m % 2 == 0))
    plan.append((mw_hbm, (lambda s: MW.at[s]), 0, local, False))
    for own, ref, count in ((ew_hbm, EW, width), (rw_hbm, RW, hidden)):
        for part in range(2):
            plan.append(
                (own, (lambda s, ref=ref: ref.at[s]), part * (count // 2), count // 2, part == 0)
            )
    pieces = [Piece(net, n, *entry, sems) for n, entry in enumerate(plan)]
    weights = ((aw_hbm, AW), (mw_hbm, MW), (ew_hbm, EW), (rw_hbm, RW))
    keep_own = [
        pltpu.make_async_copy(own, ref.at[0], local_sems.at[n]) for n, (own, ref) in enumerate(weights)
    ]
    give_own = [remote(own, ref.at[1], own_sems, n, net.core) for n, (own, ref) in enumerate(weights)]
    small_core = remote(SM.at[0], SM.at[1], small_sems, 0, net.core)
    small_y = remote(SM.at[0], SM.at[2], small_sems, 1, net.y)
    small_far = remote(SM.at[2], SM.at[3], small_sems, 2, net.core)
    fetch_cot = pltpu.make_async_copy(cot_hbm, GB, local_sems.at[4])

    keep_own[0].start()
    keep_own[1].start()
    pl.semaphore_wait(barrier, len(greeted))
    small_y.start()
    for piece in pieces[:4]:
        piece.event(0)
    small_core.start()
    for copy in give_own:
        copy.start()
    for piece in pieces[4:]:
        piece.event(0)
    keep_own[2].start()
    keep_own[3].start()
    fetch_cot.start()

    def happen(*pairs):
        return [lambda n=n, s=s: pieces[n].event(s) for n, s in pairs]

    begin, bounds = page_scalars(pages_ref, net.t, half)
    perm = (iota((rows, rows), 1) == ((iota((rows, rows), 0) + begin) & (rows - 1))).astype(BF)
    XR[...] = nn(perm, x_ref[...]).astype(BF)
    bucket = iota((BUCKETS, rows), 0)
    mine = pl.ds(pl.multiple_of(net.t * rows, 128), rows)
    one = (cells_ref[0:1, mine] == bucket).astype(BF)
    two = (cells_ref[1:2, mine] == bucket).astype(BF)
    HOT[...] = nt(perm, jnp.concatenate([one, two, one, two], axis=0)).astype(BF)
    ACC[...] = XR[...].astype(F32) + ms_ref[...].astype(F32)
    for ref in (Q, K, V):
        for s in range(4):
            ref[s, :, local:] = jnp.zeros((rows, 256 - local), BF)
    GC[:, local:] = jnp.zeros((rows, 256 - local), BF)
    DD[:, :local] = jnp.zeros((rows, local), BF)
    col = page_numbers((iota((half, 1), 0) + (half + begin)) & (rows - 1), bounds)
    row = page_numbers((iota((1, half), 1) + (half + begin)) & (rows - 1), bounds)

    spot = iota((BUCKETS, 128), 1)
    spot = jnp.where(spot < 64, spot, spot - 128)
    fold = (iota((BUCKETS, 128), 0) == jnp.clip(BUCKETS // 2 - spot, 0, BUCKETS - 1)).astype(BF)

    keep_own[0].wait()
    keep_own[1].wait()

    def attend(r, _):
        at_step(
            r,
            {
                1: [small_core.wait_recv, give_own[0].wait_recv, give_own[1].wait_recv],
                2: happen((2, 1), (1, 2), (3, 1), (0, 3), (2, 2), (3, 2), (4, 1), (1, 3), (2, 3), (3, 3))
                + [small_far.wait_recv]
                + happen((0, 4), (1, 4), (2, 4), (3, 4)),
            },
        )
        line = nn(SM[r, 8 : 8 + 2 * heads, :BUCKETS].astype(BF), fold)
        lanes_at = iota((BUCKETS, 128), 1)
        tiles = []
        for a in range(2):
            parts = []
            for pair in range(2):
                total = jnp.zeros((BUCKETS, 128), F32)
                for which in range(min(2, heads - 2 * pair)):
                    off = which * HEAD_DIM + a * BUCKETS
                    h = a * heads + 2 * pair + which
                    spread = jnp.broadcast_to(line[h : h + 1, :], (BUCKETS, 128))
                    spread = pltpu.roll(spread, off, axis=1, stride=1, stride_axis=0)
                    inside = (lanes_at >= off) & (lanes_at < off + BUCKETS)
                    total = jnp.where(inside, spread, total)
                parts.append(total.astype(BF))
            tiles.append(jnp.concatenate(parts, axis=1))
        pairs = jnp.concatenate(tiles, axis=0)
        left = nn(HOT[:, : 2 * BUCKETS], pairs).astype(BF)

        queries = (nn(XR[...], AW[r, 0]) + SM[r, 0:1, :local]).astype(BF)
        Q[r, :, :local] = queries * jnp.asarray(HEAD_DIM ** -0.5, BF)
        K[r, :, :local] = nn(XR[...], AW[r, 1]).astype(BF)
        V[r, :, :local] = (nn(XR[...], AW[r, 2]) + SM[r, 1:2, :local]).astype(BF)
        at_step(r, {1: happen((0, 1), (1, 1)) + [small_y.wait_recv, small_far.start]})
        same = col == row
        for block in range(2):
            at = slice(block * half, (block + 1) * half)
            if block == 1:
                at_step(r, {1: happen((0, 2)), 2: happen((5, 1)), 3: happen((7, 1), (5, 2))})
            for pair in range(2):
                lanes = slice(pair * 128, (pair + 1) * 128)
                key_side = jnp.concatenate([K[r, at, lanes], HOT[at, :]], axis=1)
                total = None
                for which in range(min(2, heads - 2 * pair)):
                    keep = half_lanes(which)
                    query_side = jnp.concatenate(
                        [Q[r, at, lanes] * keep, left[at, lanes] * keep], axis=1
                    )
                    scores = nt(key_side, query_side)
                    if block == 1:
                        scores = jnp.where(same, scores, MASKED)
                    weights = jnp.exp(scores - jnp.max(scores, axis=0, keepdims=True))
                    probs = (weights * (1.0 / jnp.sum(weights, axis=0, keepdims=True))).astype(BF)
                    PR[r, (2 * pair + which) * 2 + block] = probs
                    part = tn(probs, V[r, at, lanes]) * keep.astype(F32)
                    total = part if total is None else total + part
                CTX[r, at, lanes] = total.astype(BF)
        at_step(r, {2: happen((4, 2), (6, 1)), 3: happen((4, 3), (6, 2))})
        ACC[...] += nn(CTX[r, :, :local], MW[r])
        return 0

    lax.fori_loop(0, 4, attend, 0)

    hat, scale = norm_stats(ACC[...])
    HAT[...] = hat
    SCALE[...] = scale
    normed = hat * gain_ref[0:1, :].astype(F32) + nshift_ref[0:1, :].astype(F32)
    NB[...] = normed.astype(BF)
    ACC[...] = normed + rs_ref[...].astype(F32)
    keep_own[2].wait()
    keep_own[3].wait()

    def feed(r, _):
        at_step(
            r,
            {
                0: happen((7, 2)),
                1: [give_own[2].wait_recv, give_own[3].wait_recv] + happen((5, 3)),
                2: happen((6, 3), (7, 3), (4, 4), (5, 4), (6, 4), (7, 4)),
            },
        )
        pre = nn(NB[...], EW[r]) + SM[r, 2:3, :]
        gate = 0.5 * (1.0 + lax.erf(pre * (0.5 ** 0.5)))
        AS[r, :rows] = (pre * gate).astype(BF)
        AS[r, rows:] = (
            gate + pre * (jnp.exp(-0.5 * (pre * pre)) * (1.0 / math.sqrt(2.0 * math.pi)))
        ).astype(BF)
        ACC[...] += nn(AS[r, :rows], RW[r])
        return 0

    lax.fori_loop(0, 4, feed, 0)

    fetch_cot.wait()
    hat, scale = norm_stats(ACC[...])
    gain = gain_ref[1:2, :].astype(F32)
    result = (hat * gain + nshift_ref[1:2, :].astype(F32)).astype(BF)
    perm = (iota((rows, rows), 1) == ((iota((rows, rows), 0) + begin) & (rows - 1))).astype(BF)
    out_ref[...] = tn(perm, result).astype(BF)
    cot = nn(perm, GB[...])
    grad = norm_back(cot, hat, scale, gain)
    ACC[...] = grad
    GB[...] = grad.astype(BF)
    small_ref[3:4, :] = jnp.sum(cot * hat, axis=0, keepdims=True)
    small_ref[4:5, :] = jnp.sum(cot, axis=0, keepdims=True)
    small_ref[5:6, :] = jnp.sum(grad, axis=0, keepdims=True)
    small_ref[6:8, :] = jnp.zeros((2, width), F32)

    for piece in pieces[4:]:
        piece.event(5)

    def feed_back(i, _):
        r = 3 - i
        grad_pre = (nt(GB[...], RW[r]) * AS[r, rows:].astype(F32)).astype(BF)
        RW[r] = tn(GB[...], AS[r, :rows]).astype(BF)
        ges_ref[r] = jnp.sum(grad_pre.astype(F32), axis=0, keepdims=True)
        ACC[...] += nt(grad_pre, EW[r])
        EW[r] = tn(NB[...], grad_pre).astype(BF)
        pltpu.make_async_copy(RW.at[r], grw_hbm.at[r], local_sems.at[5 + r]).start()
        pltpu.make_async_copy(EW.at[r], gew_hbm.at[r], local_sems.at[9 + r]).start()
        return 0

    lax.fori_loop(0, 4, feed_back, 0)

    grad = ACC[...]
    hat = HAT[...]
    gone = norm_back(grad, hat, SCALE[...], gain_ref[0:1, :].astype(F32))
    ACC[...] = gone
    GB[...] = gone.astype(BF)
    small_ref[0:1, :] = jnp.sum(grad * hat, axis=0, keepdims=True)
    small_ref[1:2, :] = jnp.sum(grad, axis=0, keepdims=True)
    small_ref[2:3, :] = jnp.sum(gone, axis=0, keepdims=True)

    def attend_back(i, _):
        r = 3 - i
        GC[:, :local] = nt(GB[...], MW[r]).astype(BF)
        for block in range(2):
            at = slice(block * half, (block + 1) * half)
            for pair in range(2):
                lanes = slice(pair * 128, (pair + 1) * 128)
                key_side = jnp.concatenate([K[r, at, lanes], HOT[at, :]], axis=1)
                sums = None
                for which in range(min(2, heads - 2 * pair)):
                    keep = half_lanes(which)
                    wide = keep.astype(F32)
                    probs = PR[r, (2 * pair + which) * 2 + block]
                    grad_probs = nt(V[r, at, lanes] * keep, GC[at, lanes])
                    soft = probs.astype(F32)
                    inner = jnp.sum(soft * grad_probs, axis=0, keepdims=True)
                    grad_scores = (soft * (grad_probs - inner)).astype(BF)
                    both = tn(grad_scores, key_side)
                    parts = (
                        both[:, :128] * wide,
                        both[:, 128:] * wide,
                        nn(grad_scores, Q[r, at, lanes]) * wide,
                        nn(probs, GC[at, lanes]) * wide,
                    )
                    sums = parts if sums is None else tuple(a + b for a, b in zip(sums, parts))
                DQ[at, lanes] = (sums[0] * (HEAD_DIM ** -0.5)).astype(BF)
                E[at, lanes] = sums[1].astype(BF)
                DK[at, lanes] = sums[2].astype(BF)
                DV[at, lanes] = sums[3].astype(BF)
        for m, ref in enumerate((DQ, DK, DV)):
            DD[:, (m + 1) * local : (m + 2) * local] = ref[:, :local]
            ACC[...] += nt(ref[:, :local], AW[r, m])
        weight_grad = tn(XR[...], DD[...])
        AS[r, :width, 256:] = weight_grad[:, 256:].astype(BF)
        AS[r, :width, :256] = (weight_grad[:, :256] + tn(GB[...], CTX[r])).astype(BF)
        gsh_ref[r, 0:1, :] = jnp.sum(DQ[:, :local].astype(F32), axis=0, keepdims=True)
        gsh_ref[r, 1:2, :] = jnp.sum(DV[:, :local].astype(F32), axis=0, keepdims=True)
        gpair_ref[r] = tn(HOT[:, : 2 * BUCKETS], E[...])
        pltpu.make_async_copy(AS.at[r, :width], gat_hbm.at[r], local_sems.at[13 + r]).start()
        return 0

    lax.fori_loop(0, 4, attend_back, 0)

    perm = (iota((rows, rows), 1) == ((iota((rows, rows), 0) + begin) & (rows - 1))).astype(BF)
    gin_ref[...] = tn(perm, ACC[...].astype(BF)).astype(BF)

    for r in range(4):
        pltpu.make_async_copy(RW.at[r], grw_hbm.at[r], local_sems.at[5 + r]).wait()
        pltpu.make_async_copy(EW.at[r], gew_hbm.at[r], local_sems.at[9 + r]).wait()
        pltpu.make_async_copy(AS.at[r, :width], gat_hbm.at[r], local_sems.at[13 + r]).wait()
    for piece in pieces[:4]:
        piece.event(5)
    for copy in give_own + [small_core, small_y, small_far]:
        copy.wait_send()


def swap(value, axis, size, bit):
    return lax.ppermute(value, axis, [(i, i ^ bit) for i in range(size)])


def reduce_slots(partial_sums, dp):
    add = lambda a, b: (a.astype(F32) + b.astype(F32))
    got = swap(partial_sums[1::2], "tensor", 4, 1)
    two = add(partial_sums[0::2], got).astype(BF)
    got = swap(two[1], "tensor", 4, 2)
    one = add(two[0], got)
    lead = one.shape[:-2]
    rows, cols = one.shape[-2:]
    bits = dp.bit_length() - 1
    one = one.reshape(lead + (2,) * bits + (rows // dp, cols))
    me = lax.axis_index("dp")
    for bit in range(bits):
        axis = one.ndim - 3
        mine = (me >> bit) & 1
        keep = lax.dynamic_index_in_dim(one, mine, axis, keepdims=False)
        send = lax.dynamic_index_in_dim(one, 1 - mine, axis, keepdims=False).astype(BF)
        one = add(keep, swap(send, "dp", dp, 1 << bit))
    return one


def on_device(
    dp,
    inputs,
    layout_cells,
    page_lengths,
    attend_weight,
    attend_shift,
    merge_weight,
    merge_shift,
    norm_gains,
    norm_shifts,
    expand_weight,
    expand_shift,
    reduce_weight,
    reduce_shift,
    bias_tables,
    cotangent,
):
    rows, width = inputs.shape
    half = rows // 2
    local = attend_weight.shape[2]
    heads = bias_tables.shape[1]
    hidden = expand_weight.shape[1]
    top = dp.bit_length() - 1
    bits = (top - 3, top - 2, top - 1)

    sds = jax.ShapeDtypeStruct
    smem = pl.BlockSpec(memory_space=pltpu.SMEM)
    vmem = pl.BlockSpec(memory_space=pltpu.VMEM)
    hbm = pl.BlockSpec(memory_space=pl.ANY)

    def kernel(*refs):
        return layer_kernel(bits, *refs)

    dma = pltpu.SemaphoreType.DMA
    output, input_grad, small, ges, gsh, gpair, grw, gew, gat = pl.pallas_call(
        kernel,
        in_specs=[smem] + [vmem] * 9 + [hbm] * 5,
        out_specs=[vmem] * 6 + [hbm] * 3,
        out_shape=[
            sds((rows, width), BF), sds((rows, width), BF), sds((8, width), F32),
            sds((4, 1, hidden), F32), sds((4, 2, local), F32), sds((4, 2 * BUCKETS, 256), F32),
            sds((4, width, hidden), BF), sds((4, width, hidden), BF), sds((4, width, 4 * local), BF),
        ],
        scratch_shapes=[
            pltpu.VMEM((4, 3, width, local), BF),
            pltpu.VMEM((4, local, width), BF),
            pltpu.VMEM((4, width, hidden), BF),
            pltpu.VMEM((4, hidden, width), BF),
            pltpu.VMEM((rows, width), BF),
            pltpu.VMEM((rows, 128), BF),
            pltpu.VMEM((4, rows, 256), BF),
            pltpu.VMEM((4, rows, 256), BF),
            pltpu.VMEM((4, rows, 256), BF),
            pltpu.VMEM((4, 2 * heads, half, half), BF),
            pltpu.VMEM((4, rows, 256), BF),
            pltpu.VMEM((rows, width), BF),
            pltpu.VMEM((rows, width), F32),
            pltpu.VMEM((rows, 1), F32),
            pltpu.VMEM((4, 2 * rows, hidden), BF),
            pltpu.VMEM((rows, width), F32),
            pltpu.VMEM((rows, width), BF),
            pltpu.VMEM((rows, 256), BF),
            pltpu.VMEM((rows, 256), BF),
            pltpu.VMEM((rows, 256), BF),
            pltpu.VMEM((rows, 256), BF),
            pltpu.VMEM((rows, 256), BF),
            pltpu.VMEM((rows, 4 * local), BF),
            pltpu.VMEM((4, SMALL_ROWS, hidden), F32),
            dma((2, 8)), dma((2, 8)), dma((2, 8)), dma((2, 8)), dma((2, 4)), dma((2, 3)), dma((17,)),
        ],
        compiler_params=pltpu.CompilerParams(
            collective_id=0, has_side_effects=True, vmem_limit_bytes=VMEM_LIMIT
        ),
    )(
        page_lengths, inputs, layout_cells, attend_shift, expand_shift.reshape(1, hidden),
        bias_tables.reshape(2 * heads, BUCKETS), merge_shift.reshape(1, width),
        reduce_shift.reshape(1, width), norm_gains, norm_shifts,
        attend_weight, merge_weight, expand_weight, reduce_weight, cotangent,
    )

    grad_rw = reduce_slots(grw, dp).T
    grad_ew = reduce_slots(gew, dp)
    grad_at = reduce_slots(gat, dp)
    grad_mw = grad_at[:, :local].T
    grad_aw = jnp.transpose(grad_at[:, local:].reshape(-1, 3, local), (1, 0, 2))

    spot = jnp.arange(BUCKETS, dtype=jnp.int32)
    bucket_of = jnp.clip(spot[:, None] - spot[None, :] + BUCKETS // 2, 0, BUCKETS - 1)
    folding = (bucket_of[:, :, None] == spot[None, None, :]).astype(F32)
    split = gpair.reshape(4, 2, BUCKETS, 4, 2, BUCKETS)
    grad_pairs = jnp.stack([split[:, a, :, :heads, a, :] for a in range(2)], axis=1)
    grad_tables = jnp.einsum("raxhy,xyb->rahb", grad_pairs, folding, precision=lax.Precision.HIGHEST)
    spare = -(2 * local + hidden + 2 * heads * BUCKETS) % width
    own = jnp.concatenate(
        [
            gsh.reshape(4, -1),
            ges.reshape(4, -1),
            grad_tables.reshape(4, -1),
            jnp.zeros((4, spare), F32),
        ],
        axis=1,
    ).reshape(4, -1, width)
    shared = small[:6]
    lines = own.shape[1]
    for bit, take in ((1, 2), (2, 1)):
        got = swap(jnp.concatenate([shared, own[1::2].reshape(-1, width)], axis=0), "tensor", 4, bit)
        shared = shared + got[:6]
        own = own[0::2] + got[6:].reshape(take, lines, width)
    both = jnp.concatenate([shared, own[0]], axis=0)
    for bit in range(dp.bit_length() - 1):
        both = both + swap(both, "dp", dp, 1 << bit)
    flat = both[6:].reshape(-1)
    cut = 2 * local + hidden
    return (
        output,
        input_grad,
        grad_aw,
        flat[: 2 * local].reshape(2, local),
        grad_mw,
        both[2],
        jnp.stack([both[0], both[3]]),
        jnp.stack([both[1], both[4]]),
        grad_ew,
        flat[2 * local : cut],
        grad_rw,
        both[5],
        flat[cut : cut + 2 * heads * BUCKETS].reshape(2, heads, BUCKETS),
    )


def solution(mesh):
    in_specs = (
        P(("dp", "tensor"), None),
        P(None, "dp"),
        P("dp", None),
        P(None, None, "tensor"),
        P(None, "tensor"),
        P("tensor", None),
        P(),
        P(),
        P(),
        P(None, "tensor"),
        P("tensor"),
        P("tensor", None),
        P(),
        P(None, "tensor", None),
        P(("dp", "tensor"), None),
    )
    out_specs = (
        P(("dp", "tensor"), None),
        P(("dp", "tensor"), None),
        P(None, "dp", "tensor"),
        P(None, "tensor"),
        P("tensor", "dp"),
        P(),
        P(),
        P(),
        P("dp", "tensor"),
        P("tensor"),
        P("tensor", "dp"),
        P(),
        P(None, "tensor", None),
    )

    def run(*arrays):
        return on_device(mesh.shape["dp"], *arrays)

    return jax.shard_map(
        run, mesh=mesh, in_specs=in_specs, out_specs=out_specs, check_vma=False
    )
```

time: 344 us -> 255 us (0.74)
  waiting for transfers between devices: 165 us -> 75.4 us
  Pallas kernels: 68.4 us -> 92.2 us
  starting transfers between devices: 36.7 us -> 21.2 us
  other arithmetic: 34.6 us -> 24.3 us
    ppermute x46 -> x20, waiting for transfers between devices: 165 us -> 75.4 us  [swap(): return lax.ppermute(value, axis, [(i, i ^ bit) for i in range(size)])]
    pallas_call x4 -> x1, Pallas kernels: 68.4 us -> 92.2 us  [on_device(): pl.pallas_call(kernel, in_specs=[smem] + [vmem] * 9 + [hbm] * 5, out_spec...]
    ppermute x46 -> x20, starting transfers between devices: 36.7 us -> 21.2 us  [swap(): return lax.ppermute(value, axis, [(i, i ^ bit) for i in range(size)])]
    another operation x7 -> x0, other arithmetic: 14.8 us -> none  [gather_slots(): return jnp.stack([shard, core, far, far_core])]
    ppermute x6 -> x1, local copies, waits for them, and re-layouts: 9.84 us -> 1.44 us  [swap(): return lax.ppermute(value, axis, [(i, i ^ bit) for i in range(size)])]
    add x14 -> x11, other arithmetic: 5.49 us -> 11.9 us  [reduce_slots(): add = lambda a, b: a.astype(F32) + b.astype(F32)]
    convert_element_type x11 -> x9, local copies, waits for them, and re-layouts: 1.11 us -> 5.01 us  [reduce_slots(): lax.dynamic_index_in_dim(one, 1 - mine, axis, keepdims=False).astype(BF)]
    unnamed x46 -> x37, local copies, waits for them, and re-layouts: 4.96 us -> 8.33 us
  transfers between devices with their start and end apart: 46 -> 20, of which waited for: 21 -> 11; matrix products, arithmetic and copies ran while one was open for 18% -> 19% of each run, Pallas kernels for 4% -> 0%
where the time goes in v2:
time: 255 us; the launch traced here: 254 us
  Pallas kernels  92.2 us (36%)
  waiting for transfers between devices  75.4 us (30%)
  local copies, waits for them, and re-layouts  38.8 us (15%)
  other arithmetic  24.3 us (10%)
  starting transfers between devices  21.2 us (8%)
    pallas_call x1, Pallas kernels, on_device(): pl.pallas_call(kernel, in_specs=[smem] + [vmem] * 9 + [hbm] * 5, out_spec...  92.2 us
    ppermute x20, waiting for transfers between devices, swap(): return lax.ppermute(value, axis, [(i, i ^ bit) for i in range(size)])  75.4 us
    ppermute x20, starting transfers between devices, swap(): return lax.ppermute(value, axis, [(i, i ^ bit) for i in range(size)])  21.2 us
    add x11, other arithmetic, reduce_slots(): add = lambda a, b: a.astype(F32) + b.astype(F32)  11.9 us
    unnamed x37, local copies, waits for them, and re-layouts  8.33 us
    convert_element_type x3, other arithmetic, reduce_slots(): two = add(partial_sums[0::2], got).astype(BF)  8.08 us
    slice x3, local copies, waits for them, and re-layouts, reduce_slots(): got = swap(partial_sums[1::2], 'tensor', 4, 1)  6.84 us
  transfers between devices with their start and end apart: 20, of which 11 were waited for; matrix products, arithmetic and copies ran while one was open for 19% of the time, Pallas kernels for 0%

profile of v2, /device:TPU:0, one launch (start us, length us, event | category | flops | bytes accessed | tf_op | source)
XLA Modules:
  0.0 253.8 jit_solution(17746730266605153728)
XLA Ops:
  0.6 2.3 copy.68.refs_10_
  8.1 92.2 %shard_map.246 = (bf16[512,768]{1,0:T(8,128)(2,1)}, bf16[512,768]{1,0:T(8,128)(2,1)}, f32[8,768]{1,0:T(8,128)}, f32[4,1,768]{2,1,0:T(1,128)}, f32[4,2,192]{2,1,0...) custom-call(s32[4,8]{1,0:T(4,128)} %refs_0_.1, ...), custom_call_target="tpu_custom_call" | custom-call | tf_op jit(solution)/shard_map/pallas_call | solution.py:517
  100.3 1.8 slice.144
  102.2 1.8 reshape.123
  106.4 3.4 %slice.139 = bf16[2,768,768]{2,1,0:T(8,128)(2,1)} slice(bf16[4,768,768]{2,1,0:T(8,128)(2,1)} %get-tuple-element.29), slice={[1:4:2], [0:768:1], [0:768:1]} | slice | bytes 4718592 | tf_op jit(solution)/shard_map/slice | solution.py:464
  113.4 2.6 %collective-permute-done.6 = f32[8,768]{1,0:T(8,128)S(1)} collective-permute-done((f32[8,768]{1,0:T(8,128)S(1)}, f32[8,768]{1,0:T(8,128)S(1)}, u32[]{:S(2)}, u32[]{:S(2)}) %collective-permute-start.6) | collective-permute-done | bytes 24608 | tf_op jit(solution)/shard_map/ppermute | solution.py:459
  116.8 3.1 %collective-permute-done.7 = f32[8,768]{1,0:T(8,128)S(1)} collective-permute-done((f32[8,768]{1,0:T(8,128)S(1)}, f32[8,768]{1,0:T(8,128)S(1)}, u32[]{:S(2)}, u32[]{:S(2)}) %collective-permute-start.7) | collective-permute-done | bytes 24608 | tf_op jit(solution)/shard_map/ppermute | solution.py:459
  121.4 2.4 collective-permute-done.8
  123.8 2.6 %collective-permute-start.9 = (f32[8,768]{1,0:T(8,128)S(1)}, f32[8,768]{1,0:T(8,128)S(1)}, u32[]{:S(2)}, u32[]{:S(2)}) collective-permute-start(f32[8,768]{1,0:T(8,128)S(1)} %add.130), channel_id=1, source_target_pairs={{0,16},{4,20},{8,24},{12,28},{16,0},{20,4},{24,8},{28,12},{1,17},{... | collective-permute-start | bytes 73736 | tf_op jit(solution)/shard_map/ppermute | solution.py:459
  126.4 2.1 collective-permute-done.9
  128.5 2.9 %add_convert_fusion = bf16[2,768,768]{2,1,0:T(8,128)(2,1)S(1)} fusion(bf16[2,768,768]{2,1,0:T(8,128)(2,1)} %collective-permute-done.15, bf16[4,768,768]{2,1,0:T(8,128)(2,1)} %get-tuple-element.30), kind=kLoop, calls=%fused_computation | loop fusion | flops 4718592 | bytes 7077888 | tf_op jit(solution)/shard_map/convert_element_type | solution.py:465
  132.9 2.9 %add_convert_fusion.1 = bf16[2,768,768]{2,1,0:T(8,128)(2,1)S(1)} fusion(bf16[2,768,768]{2,1,0:T(8,128)(2,1)} %collective-permute-done.10, bf16[4,768,768]{2,1,0:T(8,128)(2,1)} %get-tuple-element.29), kind=kLoop, calls=%fused_computation.1 | loop fusion | flops 4718592 | bytes 7077888 | tf_op jit(solution)/shard_map/convert_element_type | solution.py:465
  138.4 2.2 add_convert_fusion.2
  151.5 9.1 %collective-permute-done.16 = bf16[768,768]{1,0:T(8,128)(2,1)} collective-permute-done((bf16[768,768]{1,0:T(8,128)(2,1)S(1)}, bf16[768,768]{1,0:T(8,128)(2,1)}, u32[]{:S(2)}, u32[]{:S(2)}) %collective-permute-start.16) | collective-permute-done | bytes 1179680 | tf_op jit(solution)/shard_map/ppermute | solution.py:459
  165.2 20.7 %collective-permute-done.11 = bf16[768,768]{1,0:T(8,128)(2,1)} collective-permute-done((bf16[768,768]{1,0:T(8,128)(2,1)}, bf16[768,768]{1,0:T(8,128)(2,1)}, u32[]{:S(2)}, u32[]{:S(2)}) %collective-permute-start.11) | collective-permute-done | bytes 1179680 | tf_op jit(solution)/shard_map/ppermute | solution.py:459
  189.1 16.5 %collective-permute-done.1 = bf16[768,768]{1,0:T(8,128)(2,1)} collective-permute-done((bf16[768,768]{1,0:T(8,128)(2,1)}, bf16[768,768]{1,0:T(8,128)(2,1)}, u32[]{:S(2)}, u32[]{:S(2)}) %collective-permute-start.1) | collective-permute-done | bytes 1179680 | tf_op jit(solution)/shard_map/ppermute | solution.py:459
  208.9 1.6 copy.69
  216.2 2.0 collective-permute-done.2
  219.7 1.6 bitcast_add_fusion
  225.7 1.8 collective-permute-start.19
  227.5 9.4 %collective-permute-done.3 = bf16[2,96,768]{1,2,0:T(8,128)(2,1)S(1)} collective-permute-done((bf16[2,96,768]{1,2,0:T(8,128)(2,1)S(1)}, bf16[2,96,768]{1,2,0:T(8,128)(2,1)S(1)}, u32[]{:S(2)}, u32[]{:S(2)}) %collective-permute-start.3) | collective-permute-done | bytes 294944 | tf_op jit(solution)/shard_map/ppermute | solution.py:459
  240.7 6.4 %collective-permute-done.4 = bf16[96,768]{0,1:T(8,128)(2,1)S(1)} collective-permute-done((bf16[96,768]{0,1:T(8,128)(2,1)S(1)}, bf16[96,768]{0,1:T(8,128)(2,1)S(1)}, u32[]{:S(2)}, u32[]{:S(2)}) %collective-permute-start.4) | collective-permute-done | bytes 147488 | tf_op jit(solution)/shard_map/ppermute | solution.py:459
  248.1 1.7 fusion.11
  250.4 1.7 bitcast_add_fusion.8
  (130 shorter events, 57.8 us)
Async XLA Ops:
  102.1 26.4 %collective-permute-start.15 = (bf16[2,768,768]{2,1,0:T(8,128)(2,1)S(1)}, bf16[2,768,768]{2,1,0:T(8,128)(2,1)}, u32[]{:S(2)}, u32[]{:S(2)}) collective-permute-start(bf16[2,768,768]{2,1,0:T(8,128)(2,1)S(1)} %slice.144), channel_id=1, source_target_pairs={{0,1},{1,0},{2,3},{3,2},{4,5},{5,4},{6,7},{7,6},{8,9},{9,8},{10,11... | collective-permute-start | bytes 7077896 | tf_op jit(solution)/shard_map/ppermute | solution.py:459
  105.9 6.1 %collective-permute-start.5 = (f32[10,768]{1,0:T(8,128)S(1)}, f32[10,768]{1,0:T(8,128)S(1)}, u32[]{:S(2)}, u32[]{:S(2)}) collective-permute-start(f32[10,768]{1,0:T(8,128)S(1)} %pad_maximum_fusion), channel_id=1, source_target_pairs={{0,1},{1,0},{2,3},{3,2},{4,5},{5,4},{6,7},{7,6},{8,9},{9,8},{10,11... | collective-permute-start | bytes 92168 | tf_op jit(solution)/shard_map/ppermute | solution.py:459
  109.9 23.0 %collective-permute-start.10 = (bf16[2,768,768]{2,1,0:T(8,128)(2,1)}, bf16[2,768,768]{2,1,0:T(8,128)(2,1)}, u32[]{:S(2)}, u32[]{:S(2)}) collective-permute-start(bf16[2,768,768]{2,1,0:T(8,128)(2,1)} %slice.139), channel_id=1, source_target_pairs={{0,1},{1,0},{2,3},{3,2},{4,5},{5,4},{6,7},{7,6},{8,9},{9,8},{10,11... | collective-permute-start | bytes 7077896 | tf_op jit(solution)/shard_map/ppermute | solution.py:459
  111.5 26.9 %collective-permute-start = (bf16[2,768,768]{2,1,0:T(8,128)(2,1)}, bf16[2,768,768]{2,1,0:T(8,128)(2,1)}, u32[]{:S(2)}, u32[]{:S(2)}) collective-permute-start(bf16[2,768,768]{2,1,0:T(8,128)(2,1)} %slice.114), channel_id=1, source_target_pairs={{0,1},{1,0},{2,3},{3,2},{4,5},{5,4},{6,7},{7,6},{8,9},{9,8},{10,11... | collective-permute-start | bytes 7077896 | tf_op jit(solution)/shard_map/ppermute | solution.py:459
  112.1 3.9 %collective-permute-start.6 = (f32[8,768]{1,0:T(8,128)S(1)}, f32[8,768]{1,0:T(8,128)S(1)}, u32[]{:S(2)}, u32[]{:S(2)}) collective-permute-start(f32[8,768]{1,0:T(8,128)S(1)} %pad_maximum_fusion.1), channel_id=1, source_target_pairs={{0,2},{1,3},{2,0},{3,1},{4,6},{5,7},{6,4},{7,5},{8,10},{9,11},{10,... | collective-permute-start | bytes 73736 | tf_op jit(solution)/shard_map/ppermute | solution.py:459
  116.0 3.9 %collective-permute-start.7 = (f32[8,768]{1,0:T(8,128)S(1)}, f32[8,768]{1,0:T(8,128)S(1)}, u32[]{:S(2)}, u32[]{:S(2)}) collective-permute-start(f32[8,768]{1,0:T(8,128)S(1)} %pad_maximum_fusion.2), channel_id=1, source_target_pairs={{0,4},{4,0},{8,12},{12,8},{16,20},{20,16},{24,28},{28,24},{1,5},{5... | collective-permute-start | bytes 73736 | tf_op jit(solution)/shard_map/ppermute | solution.py:459
  119.9 3.9 %collective-permute-start.8 = (f32[8,768]{1,0:T(8,128)S(1)}, f32[8,768]{1,0:T(8,128)S(1)}, u32[]{:S(2)}, u32[]{:S(2)}) collective-permute-start(f32[8,768]{1,0:T(8,128)S(1)} %fusion.21), channel_id=1, source_target_pairs={{0,8},{4,12},{8,0},{12,4},{16,24},{20,28},{24,16},{28,20},{1,9},{5... | collective-permute-start | bytes 73736 | tf_op jit(solution)/shard_map/ppermute | solution.py:459
  123.8 4.7 %collective-permute-start.9 = (f32[8,768]{1,0:T(8,128)S(1)}, f32[8,768]{1,0:T(8,128)S(1)}, u32[]{:S(2)}, u32[]{:S(2)}) collective-permute-start(f32[8,768]{1,0:T(8,128)S(1)} %add.130), channel_id=1, source_target_pairs={{0,16},{4,20},{8,24},{12,28},{16,0},{20,4},{24,8},{28,12},{1,17},{... | collective-permute-start | bytes 73736 | tf_op jit(solution)/shard_map/ppermute | solution.py:459
  131.5 6.9 %slice-start = ((s8[4718592]{0:T(1024)(128)(4,1)}), s8[4194304]{0:T(1024)(128)(4,1)S(1)}, s32[]{:S(2)}) async-start(s8[4718592]{0:T(1024)(128)(4,1)} %bitcast.105), calls=%async_computation | async-start | bytes 8388608
  131.6 29.1 %collective-permute-start.16 = (bf16[768,768]{1,0:T(8,128)(2,1)S(1)}, bf16[768,768]{1,0:T(8,128)(2,1)}, u32[]{:S(2)}, u32[]{:S(2)}) collective-permute-start(bf16[768,768]{1,0:T(8,128)(2,1)S(1)} %slice_bitcast_fusion), channel_id=1, source_target_pairs={{0,2},{1,3},{2,0},{3,1},{4,6},{5,7},{6,4},{7,5},{8,10},{9,11},{10,... | collective-permute-start | bytes 3538952 | tf_op jit(solution)/shard_map/ppermute | solution.py:459
  137.1 48.8 %collective-permute-start.11 = (bf16[768,768]{1,0:T(8,128)(2,1)}, bf16[768,768]{1,0:T(8,128)(2,1)}, u32[]{:S(2)}, u32[]{:S(2)}) collective-permute-start(bf16[768,768]{1,0:T(8,128)(2,1)} %slice_bitcast_fusion.2), channel_id=1, source_target_pairs={{0,2},{1,3},{2,0},{3,1},{4,6},{5,7},{6,4},{7,5},{8,10},{9,11},{10,... | collective-permute-start | bytes 3538952 | tf_op jit(solution)/shard_map/ppermute | solution.py:459
  142.4 63.2 %collective-permute-start.1 = (bf16[768,768]{1,0:T(8,128)(2,1)}, bf16[768,768]{1,0:T(8,128)(2,1)}, u32[]{:S(2)}, u32[]{:S(2)}) collective-permute-start(bf16[768,768]{1,0:T(8,128)(2,1)} %slice_bitcast_fusion.4), channel_id=1, source_target_pairs={{0,2},{1,3},{2,0},{3,1},{4,6},{5,7},{6,4},{7,5},{8,10},{9,11},{10,... | collective-permute-start | bytes 3538952 | tf_op jit(solution)/shard_map/ppermute | solution.py:459
  151.5 34.4 %copy-start.1 = (bf16[2,768,768]{2,1,0:T(8,128)(2,1)S(1)}, bf16[2,768,768]{2,1,0:T(8,128)(2,1)}, u32[]{:S(2)}) copy-start(bf16[2,768,768]{2,1,0:T(8,128)(2,1)} %copy-done) | copy-start | bytes 7077892
  164.5 41.1 %copy-start.3 = (bf16[2,768,768]{2,1,0:T(8,128)(2,1)S(1)}, bf16[2,768,768]{2,1,0:T(8,128)(2,1)}, u32[]{:S(2)}) copy-start(bf16[2,768,768]{2,1,0:T(8,128)(2,1)} %copy-done.2) | copy-start | bytes 7077892
  164.5 46.0 %collective-permute-start.17 = (bf16[2,2,96,768]{3,2,0,1:T(8,128)(2,1)}, bf16[2,2,96,768]{3,2,0,1:T(8,128)(2,1)}, u32[]{:S(2)}, u32[]{:S(2)}) collective-permute-start(bf16[2,2,96,768]{3,2,0,1:T(8,128)(2,1)} %fusion.1), channel_id=1, source_target_pairs={{0,4},{4,0},{8,12},{12,8},{16,20},{20,16},{24,28},{28,24},{1,5},{5... | collective-permute-start | bytes 1769480 | tf_op jit(solution)/shard_map/ppermute | solution.py:459
  188.4 25.6 %collective-permute-start.12 = (bf16[2,2,96,768]{3,2,0,1:T(8,128)(2,1)}, bf16[2,2,96,768]{3,2,0,1:T(8,128)(2,1)}, u32[]{:S(2)}, u32[]{:S(2)}) collective-permute-start(bf16[2,2,96,768]{3,2,0,1:T(8,128)(2,1)} %fusion), channel_id=1, source_target_pairs={{0,4},{4,0},{8,12},{12,8},{16,20},{20,16},{24,28},{28,24},{1,5},{5... | collective-permute-start | bytes 1769480 | tf_op jit(solution)/shard_map/ppermute | solution.py:459
  208.1 10.2 %collective-permute-start.2 = (bf16[2,2,96,768]{3,2,1,0:T(8,128)(2,1)}, bf16[2,2,96,768]{3,2,1,0:T(8,128)(2,1)}, u32[]{:S(2)}, u32[]{:S(2)}) collective-permute-start(bf16[2,2,96,768]{3,2,1,0:T(8,128)(2,1)} %fusion.2), channel_id=1, source_target_pairs={{0,4},{4,0},{8,12},{12,8},{16,20},{20,16},{24,28},{28,24},{1,5},{5... | collective-permute-start | bytes 1769480 | tf_op jit(solution)/shard_map/ppermute | solution.py:459
  212.9 11.1 %collective-permute-start.18 = (bf16[2,96,768]{2,1,0:T(8,128)(2,1)}, bf16[2,96,768]{2,1,0:T(8,128)(2,1)}, u32[]{:S(2)}, u32[]{:S(2)}) collective-permute-start(bf16[2,96,768]{2,1,0:T(8,128)(2,1)} %fusion.10), channel_id=1, source_target_pairs={{0,8},{4,12},{8,0},{12,4},{16,24},{20,28},{24,16},{28,20},{1,9},{5... | collective-permute-start | bytes 884744 | tf_op jit(solution)/shard_map/ppermute | solution.py:459
  215.3 23.1 %collective-permute-start.13 = (bf16[2,96,768]{2,1,0:T(8,128)(2,1)S(1)}, bf16[2,96,768]{2,1,0:T(8,128)(2,1)S(1)}, u32[]{:S(2)}, u32[]{:S(2)}) collective-permute-start(bf16[2,96,768]{2,1,0:T(8,128)(2,1)S(1)} %fusion.9), channel_id=1, source_target_pairs={{0,8},{4,12},{8,0},{12,4},{16,24},{20,28},{24,16},{28,20},{1,9},{5... | collective-permute-start | bytes 884744 | tf_op jit(solution)/shard_map/ppermute | solution.py:459
  221.4 15.4 %collective-permute-start.3 = (bf16[2,96,768]{1,2,0:T(8,128)(2,1)S(1)}, bf16[2,96,768]{1,2,0:T(8,128)(2,1)S(1)}, u32[]{:S(2)}, u32[]{:S(2)}) collective-permute-start(bf16[2,96,768]{1,2,0:T(8,128)(2,1)S(1)} %fusion.5), channel_id=1, source_target_pairs={{0,8},{4,12},{8,0},{12,4},{16,24},{20,28},{24,16},{28,20},{1,9},{5... | collective-permute-start | bytes 884744 | tf_op jit(solution)/shard_map/ppermute | solution.py:459
  225.7 22.4 %collective-permute-start.19 = (bf16[96,768]{1,0:T(8,128)(2,1)}, bf16[96,768]{1,0:T(8,128)(2,1)}, u32[]{:S(2)}, u32[]{:S(2)}) collective-permute-start(bf16[96,768]{1,0:T(8,128)(2,1)} %fusion.15), channel_id=1, source_target_pairs={{0,16},{4,20},{8,24},{12,28},{16,0},{20,4},{24,8},{28,12},{1,17},{... | collective-permute-start | bytes 442376 | tf_op jit(solution)/shard_map/ppermute | solution.py:459
  237.0 10.2 %collective-permute-start.4 = (bf16[96,768]{0,1:T(8,128)(2,1)S(1)}, bf16[96,768]{0,1:T(8,128)(2,1)S(1)}, u32[]{:S(2)}, u32[]{:S(2)}) collective-permute-start(bf16[96,768]{0,1:T(8,128)(2,1)S(1)} %fusion.13), channel_id=1, source_target_pairs={{0,16},{4,20},{8,24},{12,28},{16,0},{20,4},{24,8},{28,12},{1,17},{... | collective-permute-start | bytes 442376 | tf_op jit(solution)/shard_map/ppermute | solution.py:459
  238.5 13.6 %copy-start.9 = (bf16[512,768]{1,0:T(8,128)(2,1)S(1)}, bf16[512,768]{1,0:T(8,128)(2,1)}, u32[]{:S(2)}) copy-start(bf16[512,768]{1,0:T(8,128)(2,1)} %get-tuple-element.95) | copy-start | bytes 2359300
  239.2 11.2 %collective-permute-start.14 = (bf16[96,768]{1,0:T(8,128)(2,1)}, bf16[96,768]{1,0:T(8,128)(2,1)}, u32[]{:S(2)}, u32[]{:S(2)}) collective-permute-start(bf16[96,768]{1,0:T(8,128)(2,1)} %fusion.14), channel_id=1, source_target_pairs={{0,16},{4,20},{8,24},{12,28},{16,0},{20,4},{24,8},{28,12},{1,17},{... | collective-permute-start | bytes 442376 | tf_op jit(solution)/shard_map/ppermute | solution.py:459
  (11 other events, 42.1 us)

commit v3 on v2

--- a/solution.py
+++ b/solution.py
@@ -171,6 +171,92 @@
             self.to_core().wait_send()
 
 
+CHUNK = 256
+SHARED = 9
+ORDERS = (
+    (("y", 0, 1, 2), (0, "y", 1, 2), (1, "y", 0, 2)),
+    (("y", 0, 1, 2), (0, "y", 1, 2), (1, 0, "y", 2)),
+    (("y", 0, 1, 2), (0, "y", 1, 2), (1, 0, "y", 2)),
+)
+
+
+class Stage:
+    def __init__(self, net, axis, slot, fixed, values, room, index, sems, block):
+        self.net, self.axis, self.slot, self.fixed, self.values = net, axis, slot, dict(fixed), values
+        self.room, self.index, self.sems, self.block = room, index, sems, block
+        self.kept = slot if axis != "y" else 0
+        self.partner = net.y if axis == "y" else net.dp[axis]
+
+    def runs(self, bits):
+        low = 0
+        while low < 3 and low not in bits:
+            low += 1
+        starts = [0]
+        for k in range(low, 3):
+            choice = [bits[k]] if k in bits else [0, 1]
+            starts = [start + value * (2 ** k * self.block) for start in starts for value in choice]
+        return [(start, 2 ** low * self.block) for start in starts]
+
+    def theirs(self):
+        bits = dict(self.fixed)
+        if self.axis != "y":
+            bits[self.axis] = 1 - self.net.bit[self.axis]
+        return self.runs(bits)
+
+    def ours(self):
+        bits = dict(self.fixed)
+        if self.axis != "y":
+            bits[self.axis] = self.net.bit[self.axis]
+        return self.runs(bits)
+
+    def send(self):
+        at = 0
+        for start, count in self.theirs():
+            remote(
+                self.values(self.slot, start, count), self.room(at, count),
+                self.sems, self.index, self.partner,
+            ).start()
+            at += count
+
+    def all_of_it(self):
+        total = sum(count for _, count in self.ours())
+        return remote(self.room(0, total), self.room(0, total), self.sems, self.index, self.partner)
+
+    def take(self):
+        self.all_of_it().wait_recv()
+        at = 0
+        for start, count in self.ours():
+            here = self.values(self.kept, start, count)
+            here[...] = here[...] + self.room(at, count)[...]
+            at += count
+
+    def sent(self):
+        self.all_of_it().wait_send()
+
+
+def chunk_stages(net, unit, chunk, slots, got, sems, first, block):
+    lanes = pl.ds(chunk * CHUNK, CHUNK)
+
+    def values(slot, start, count):
+        return slots(slot).at[pl.ds(pl.multiple_of(start, 32), count), lanes]
+
+    stages, fixed, live, at = {}, {}, (2, 0), 0
+    for axis in ORDERS[unit][chunk]:
+        exchanges = (2,) if axis == "y" else live
+        for slot in exchanges:
+            count = (8 * block) >> (len(fixed) + (axis != "y"))
+            room = lambda start, rows, at=at: got.at[pl.ds(at + start, rows), :]
+            stages[(axis, slot)] = Stage(
+                net, axis, slot, fixed, values, room, first + len(stages), sems, block
+            )
+            at += count
+        if axis == "y":
+            live = (0,)
+        else:
+            fixed[axis] = net.bit[axis]
+    return stages
+
+
 def at_step(index, table):
     for value, actions in table.items():
 
@@ -184,30 +270,33 @@
     bits,
     pages_ref, x_ref, cells_ref, shift_ref, es_ref, tables_ref, ms_ref, rs_ref, gain_ref, nshift_ref,
     aw_hbm, mw_hbm, ew_hbm, rw_hbm, cot_hbm,
-    out_ref, gin_ref, small_ref, ges_ref, gsh_ref, gpair_ref, grw_hbm, gew_hbm, gat_hbm,
-    AW, MW, EW, RW, XR, HOT, Q, K, V, PR, CTX, NB, HAT, SCALE, AS, ACC, GB, GC, DQ, DK, DV, E, DD, SM,
+    out_ref, gin_ref, gaw_ref, gmw_ref, gew_ref, grw_ref, both_ref,
+    AW, MW, EW, RW, XR, HOT, BACK, Q, K, V, PR, CTX, NB, HAT, SCALE, AS, ACC, GB, GC, DQ, DK, DV, E, DD, SM,
+    FROM_CORE, FROM, SUMS, SUMS_CORE, SUMS_FAR,
     y_sems, one_sems, two_sems, core_sems, own_sems, small_sems, local_sems,
+    unit_sems, stage_sems, total_sems,
 ):
     net = Net(bits)
     rows, width = x_ref.shape
     half = rows // 2
-    local = aw_hbm.shape[2]
+    local = aw_hbm.shape[1]
     heads = local // HEAD_DIM
     hidden = ew_hbm.shape[1]
 
     barrier = pltpu.get_barrier_semaphore()
-    greeted = (net.core, net.y, net.dp[0], net.dp[1])
+    greeted = (net.core, net.y, net.dp[0], net.dp[1], net.dp[2])
     for partner in greeted:
         pl.semaphore_signal(barrier, inc=1, device_id=partner, device_id_type=MESH)
 
     SM[0, 0:2, :local] = shift_ref[...].astype(F32)
-    SM[0, 2:3, :] = es_ref[...].astype(F32)
-    SM[0, 8 : 8 + 2 * heads, :BUCKETS] = tables_ref[...].astype(F32)
+    SM[0, 2:3, :] = es_ref[...].reshape(1, hidden).astype(F32)
+    for h in range(heads):
+        SM[0, 8 + 2 * h : 10 + 2 * h, :BUCKETS] = tables_ref[h].astype(F32)
 
     plan = []
     sems = (y_sems, one_sems, two_sems, core_sems)
     for m in range(3):
-        plan.append((aw_hbm.at[m], (lambda s, m=m: AW.at[s, m]), 0, width, m % 2 == 0))
+        plan.append((aw_hbm.at[m], (lambda s, m=m: AW.at[s, m]), 0, local, m % 2 == 0))
     plan.append((mw_hbm, (lambda s: MW.at[s]), 0, local, False))
     for own, ref, count in ((ew_hbm, EW, width), (rw_hbm, RW, hidden)):
         for part in range(2):
@@ -240,6 +329,46 @@
     keep_own[3].start()
     fetch_cot.start()
 
+    block = width // 8
+    units = (
+        (lambda slot: RW.at[slot]),
+        (lambda slot: EW.at[slot]),
+        (lambda slot: AS.at[slot, pl.ds(0, width), :]),
+    )
+    flows, first = {}, 0
+    for unit in range(3):
+        for chunk in range(3):
+            stages = chunk_stages(
+                net, unit, chunk, units[unit], FROM.at[unit * 3 + chunk], stage_sems, first, block
+            )
+            flows[unit, chunk] = stages
+            first += len(stages)
+
+    def to_core(unit, slot):
+        return remote(
+            units[unit](slot), FROM_CORE.at[unit, slot // 2], unit_sems, unit * 2 + slot // 2, net.core
+        )
+
+    def add_core(unit, slot):
+        to_core(unit, slot + 1).wait_recv()
+        here = units[unit](slot)
+        here[...] = here[...] + FROM_CORE[unit, slot // 2]
+
+    def send(unit, chunk, axis, slot=0):
+        return flows[unit, chunk][axis, 2 if axis == "y" else slot].send
+
+    def take(unit, chunk, axis, slot=0):
+        return flows[unit, chunk][axis, 2 if axis == "y" else slot].take
+
+    def open_far(unit):
+        return [
+            lambda: add_core(unit, 2),
+            send(unit, 0, "y"), send(unit, 1, 0, 2), send(unit, 2, 1, 2),
+        ]
+
+    def open_near(unit):
+        return [lambda: add_core(unit, 0), send(unit, 1, 0, 0), send(unit, 2, 1, 0)]
+
     def happen(*pairs):
         return [lambda n=n, s=s: pieces[n].event(s) for n, s in pairs]
 
@@ -251,7 +380,10 @@
     one = (cells_ref[0:1, mine] == bucket).astype(BF)
     two = (cells_ref[1:2, mine] == bucket).astype(BF)
     HOT[...] = nt(perm, jnp.concatenate([one, two, one, two], axis=0)).astype(BF)
-    ACC[...] = XR[...].astype(F32) + ms_ref[...].astype(F32)
+    one = (cells_ref[0:1, mine] == BUCKETS - 1 - bucket).astype(BF)
+    two = (cells_ref[1:2, mine] == BUCKETS - 1 - bucket).astype(BF)
+    BACK[...] = nt(perm, jnp.concatenate([one, two], axis=0)).astype(BF)
+    ACC[...] = XR[...].astype(F32) + ms_ref[...].reshape(1, width).astype(F32)
     for ref in (Q, K, V):
         for s in range(4):
             ref[s, :, local:] = jnp.zeros((rows, 256 - local), BF)
@@ -263,6 +395,8 @@
     spot = iota((BUCKETS, 128), 1)
     spot = jnp.where(spot < 64, spot, spot - 128)
     fold = (iota((BUCKETS, 128), 0) == jnp.clip(BUCKETS // 2 - spot, 0, BUCKETS - 1)).astype(BF)
+
+    fold_f32 = fold.astype(F32)
 
     keep_own[0].wait()
     keep_own[1].wait()
@@ -286,7 +420,7 @@
                 total = jnp.zeros((BUCKETS, 128), F32)
                 for which in range(min(2, heads - 2 * pair)):
                     off = which * HEAD_DIM + a * BUCKETS
-                    h = a * heads + 2 * pair + which
+                    h = (2 * pair + which) * 2 + a
                     spread = jnp.broadcast_to(line[h : h + 1, :], (BUCKETS, 128))
                     spread = pltpu.roll(spread, off, axis=1, stride=1, stride_axis=0)
                     inside = (lanes_at >= off) & (lanes_at < off + BUCKETS)
@@ -296,10 +430,10 @@
         pairs = jnp.concatenate(tiles, axis=0)
         left = nn(HOT[:, : 2 * BUCKETS], pairs).astype(BF)
 
-        queries = (nn(XR[...], AW[r, 0]) + SM[r, 0:1, :local]).astype(BF)
+        queries = (nt(XR[...], AW[r, 0]) + SM[r, 0:1, :local]).astype(BF)
         Q[r, :, :local] = queries * jnp.asarray(HEAD_DIM ** -0.5, BF)
-        K[r, :, :local] = nn(XR[...], AW[r, 1]).astype(BF)
-        V[r, :, :local] = (nn(XR[...], AW[r, 2]) + SM[r, 1:2, :local]).astype(BF)
+        K[r, :, :local] = nt(XR[...], AW[r, 1]).astype(BF)
+        V[r, :, :local] = (nt(XR[...], AW[r, 2]) + SM[r, 1:2, :local]).astype(BF)
         at_step(r, {1: happen((0, 1), (1, 1)) + [small_y.wait_recv, small_far.start]})
         same = col == row
         for block in range(2):
@@ -335,7 +469,7 @@
     SCALE[...] = scale
     normed = hat * gain_ref[0:1, :].astype(F32) + nshift_ref[0:1, :].astype(F32)
     NB[...] = normed.astype(BF)
-    ACC[...] = normed + rs_ref[...].astype(F32)
+    ACC[...] = normed + rs_ref[...].reshape(1, width).astype(F32)
     keep_own[2].wait()
     keep_own[3].wait()
 
@@ -369,10 +503,13 @@
     grad = norm_back(cot, hat, scale, gain)
     ACC[...] = grad
     GB[...] = grad.astype(BF)
-    small_ref[3:4, :] = jnp.sum(cot * hat, axis=0, keepdims=True)
-    small_ref[4:5, :] = jnp.sum(cot, axis=0, keepdims=True)
-    small_ref[5:6, :] = jnp.sum(grad, axis=0, keepdims=True)
-    small_ref[6:8, :] = jnp.zeros((2, width), F32)
+    shared_two = (
+        jnp.sum(cot * hat, axis=0, keepdims=True),
+        jnp.sum(cot, axis=0, keepdims=True),
+        jnp.sum(grad, axis=0, keepdims=True),
+    )
+    for n, line in enumerate(shared_two):
+        SUMS[0, SHARED + 3 + n : SHARED + 4 + n, :] = line
 
     for piece in pieces[4:]:
         piece.event(5)
@@ -381,11 +518,27 @@
         r = 3 - i
         grad_pre = (nt(GB[...], RW[r]) * AS[r, rows:].astype(F32)).astype(BF)
         RW[r] = tn(GB[...], AS[r, :rows]).astype(BF)
-        ges_ref[r] = jnp.sum(grad_pre.astype(F32), axis=0, keepdims=True)
+        at_step(
+            r,
+            {
+                3: [to_core(0, 3).start],
+                2: open_far(0),
+                1: [to_core(0, 1).start],
+                0: open_near(0),
+            },
+        )
+        SUMS[r, 0:1, :] = jnp.sum(grad_pre.astype(F32), axis=0, keepdims=True)
         ACC[...] += nt(grad_pre, EW[r])
         EW[r] = tn(NB[...], grad_pre).astype(BF)
-        pltpu.make_async_copy(RW.at[r], grw_hbm.at[r], local_sems.at[5 + r]).start()
-        pltpu.make_async_copy(EW.at[r], gew_hbm.at[r], local_sems.at[9 + r]).start()
+        at_step(
+            r,
+            {
+                3: [to_core(1, 3).start],
+                2: open_far(1),
+                1: [to_core(1, 1).start],
+                0: open_near(1),
+            },
+        )
         return 0
 
     lax.fori_loop(0, 4, feed_back, 0)
@@ -395,12 +548,60 @@
     gone = norm_back(grad, hat, SCALE[...], gain_ref[0:1, :].astype(F32))
     ACC[...] = gone
     GB[...] = gone.astype(BF)
-    small_ref[0:1, :] = jnp.sum(grad * hat, axis=0, keepdims=True)
-    small_ref[1:2, :] = jnp.sum(grad, axis=0, keepdims=True)
-    small_ref[2:3, :] = jnp.sum(gone, axis=0, keepdims=True)
+    shared_one = (
+        jnp.sum(grad * hat, axis=0, keepdims=True),
+        jnp.sum(grad, axis=0, keepdims=True),
+        jnp.sum(gone, axis=0, keepdims=True),
+    )
+    for n, line in enumerate(shared_one):
+        SUMS[0, SHARED + n : SHARED + 1 + n, :] = line
+
+    for action in (
+        take(0, 0, "y"), send(0, 0, 0),
+        take(0, 1, 0, 2), send(0, 1, "y"),
+        take(0, 2, 1, 2), send(0, 2, "y"),
+    ):
+        action()
 
     def attend_back(i, _):
         r = 3 - i
+
+        def early():
+            at_step(
+                r,
+                {
+                    3: [
+                        take(0, 1, 0, 0), take(0, 2, 1, 0),
+                        take(1, 1, 0, 2), send(1, 1, "y"),
+                        take(1, 2, 1, 2), send(1, 2, 0, 2),
+                    ],
+                    2: [take(1, 1, 0, 0), take(1, 2, 1, 0), send(1, 2, 0, 0)],
+                    1: [take(0, 2, "y"), send(0, 2, 0), take(1, 2, 0, 2), send(1, 2, "y")],
+                    0: [
+                        take(1, 1, "y"), send(1, 1, 1), take(1, 2, 0, 0),
+                        take(0, 2, 0), send(0, 2, 2),
+                    ],
+                },
+            )
+
+        def late():
+            at_step(
+                r,
+                {
+                    3: [to_core(2, 3).start, take(1, 0, "y"), send(1, 0, 0)],
+                    2: open_far(2)
+                    + [take(0, 0, 0), send(0, 0, 1), take(0, 1, "y"), send(0, 1, 1)],
+                    1: [
+                        to_core(2, 1).start,
+                        take(1, 0, 0), send(1, 0, 1),
+                        take(0, 0, 1), send(0, 0, 2), take(0, 1, 1), send(0, 1, 2),
+                    ],
+                    0: open_near(2)
+                    + [take(1, 2, "y"), send(1, 2, 2), take(1, 0, 1), send(1, 0, 2)]
+                    + [take(1, 1, 1), send(1, 1, 2)],
+                },
+            )
+
         GC[:, :local] = nt(GB[...], MW[r]).astype(BF)
         for block in range(2):
             at = slice(block * half, (block + 1) * half)
@@ -428,27 +629,115 @@
                 E[at, lanes] = sums[1].astype(BF)
                 DK[at, lanes] = sums[2].astype(BF)
                 DV[at, lanes] = sums[3].astype(BF)
+            if block == 0:
+                early()
         for m, ref in enumerate((DQ, DK, DV)):
             DD[:, (m + 1) * local : (m + 2) * local] = ref[:, :local]
-            ACC[...] += nt(ref[:, :local], AW[r, m])
+            ACC[...] += nn(ref[:, :local], AW[r, m])
         weight_grad = tn(XR[...], DD[...])
         AS[r, :width, 256:] = weight_grad[:, 256:].astype(BF)
         AS[r, :width, :256] = (weight_grad[:, :256] + tn(GB[...], CTX[r])).astype(BF)
-        gsh_ref[r, 0:1, :] = jnp.sum(DQ[:, :local].astype(F32), axis=0, keepdims=True)
-        gsh_ref[r, 1:2, :] = jnp.sum(DV[:, :local].astype(F32), axis=0, keepdims=True)
-        gpair_ref[r] = tn(HOT[:, : 2 * BUCKETS], E[...])
-        pltpu.make_async_copy(AS.at[r, :width], gat_hbm.at[r], local_sems.at[13 + r]).start()
+        late()
+        SUMS[r, 1:2, :local] = jnp.sum(DQ[:, :local].astype(F32), axis=0, keepdims=True)
+        SUMS[r, 2:3, :local] = jnp.sum(DV[:, :local].astype(F32), axis=0, keepdims=True)
+        grad_pairs = tn(BACK[...], E[...])
+        lanes_at = iota((BUCKETS, 128), 1)
+        for h in range(heads):
+            for a in range(2):
+                off = (h % 2) * HEAD_DIM + a * BUCKETS
+                part = grad_pairs[a * BUCKETS : (a + 1) * BUCKETS, (h // 2) * 128 : (h // 2 + 1) * 128]
+                part = jnp.where((lanes_at >= off) & (lanes_at < off + BUCKETS), part, 0.0)
+                part = pltpu.roll(part, (129 - BUCKETS - off) % 128, axis=1, stride=1, stride_axis=0)
+                SUMS[r, 3 + 2 * h + a : 4 + 2 * h + a, :128] = jnp.sum(part, axis=0, keepdims=True)
         return 0
 
+    SUMS[1, SHARED : SHARED + 6, :] = SUMS[0, SHARED : SHARED + 6, :]
     lax.fori_loop(0, 4, attend_back, 0)
 
+    sums_core = [
+        remote(SUMS.at[2 * n + 1], SUMS_CORE.at[n], total_sems, n, net.core) for n in range(2)
+    ]
+    sums_far = [
+        remote(SUMS.at[2 - 2 * (n > 0)], SUMS_FAR.at[n], total_sems, 2 + n, partner)
+        for n, partner in enumerate([net.y] + net.dp)
+    ]
+    for copy in sums_core:
+        copy.start()
     perm = (iota((rows, rows), 1) == ((iota((rows, rows), 0) + begin) & (rows - 1))).astype(BF)
     gin_ref[...] = tn(perm, ACC[...].astype(BF)).astype(BF)
-
-    for r in range(4):
-        pltpu.make_async_copy(RW.at[r], grw_hbm.at[r], local_sems.at[5 + r]).wait()
-        pltpu.make_async_copy(EW.at[r], gew_hbm.at[r], local_sems.at[9 + r]).wait()
-        pltpu.make_async_copy(AS.at[r, :width], gat_hbm.at[r], local_sems.at[13 + r]).wait()
+    take(2, 1, 0, 2)()
+    send(2, 1, "y")()
+    take(2, 2, 1, 2)()
+    send(2, 2, 0, 2)()
+    for n, copy in enumerate(sums_core):
+        copy.wait_recv()
+        SUMS[2 * n] = SUMS[2 * n] + SUMS_CORE[n]
+    SUMS[2, SHARED : SHARED + 6, :] = SUMS[0, SHARED : SHARED + 6, :]
+    sums_far[0].start()
+    take(2, 2, 1, 0)()
+    send(2, 2, 0, 0)()
+    take(2, 0, "y")()
+    send(2, 0, 0)()
+    take(2, 1, 0, 0)()
+
+    def finish(unit, chunk, out_ref):
+        stage = flows[unit, chunk][2, 0]
+        stage.all_of_it().wait_recv()
+        (start, count), = stage.ours()
+        here = stage.values(0, start, count)
+        return here[...].astype(F32) + stage.room(0, count)[...].astype(F32)
+
+    def lanes_of(chunk):
+        return slice(chunk * CHUNK, (chunk + 1) * CHUNK)
+
+    for chunk in range(3):
+        grw_ref[:, lanes_of(chunk)] = finish(0, chunk, grw_ref)
+    sums_far[0].wait_recv()
+    SUMS[0] = SUMS[0] + SUMS_FAR[0]
+    sums_far[1].start()
+    take(2, 2, 0, 2)()
+    send(2, 2, "y")()
+    take(2, 1, "y")()
+    send(2, 1, 1)()
+    for chunk in range(3):
+        gew_ref[:, lanes_of(chunk)] = finish(1, chunk, gew_ref)
+    sums_far[1].wait()
+    SUMS[0] = SUMS[0] + SUMS_FAR[1]
+    sums_far[2].start()
+    take(2, 2, 0, 0)()
+    take(2, 0, 0)()
+    send(2, 0, 1)()
+    take(2, 2, "y")()
+    send(2, 2, 2)()
+    sums_far[2].wait()
+    SUMS[0] = SUMS[0] + SUMS_FAR[2]
+    sums_far[3].start()
+    take(2, 1, 1)()
+    send(2, 1, 2)()
+    take(2, 0, 1)()
+    send(2, 0, 2)()
+    mixed = jnp.concatenate(
+        [finish(2, chunk, None) for chunk in (0, 1, 2)], axis=1
+    )
+    gmw_ref[...] = jnp.transpose(mixed[:, :256])[:local, :]
+    for m in range(3):
+        gaw_ref[m] = mixed[:, (m + 1) * local : (m + 2) * local]
+    sums_far[3].wait()
+    both_ref[...] = SUMS[0] + SUMS_FAR[3]
+    for row in range(2 * heads):
+        both_ref[3 + row : 4 + row, :BUCKETS] = lax.dot_general(
+            both_ref[3 + row : 4 + row, :128], fold_f32, (((1,), (1,)), ((), ())),
+            precision=lax.Precision.HIGHEST, preferred_element_type=F32,
+        )
+
+    for stages in flows.values():
+        for stage in stages.values():
+            stage.sent()
+    for unit in range(3):
+        for slot in (1, 3):
+            to_core(unit, slot).wait_send()
+    for copy in sums_core + sums_far[:1]:
+        copy.wait_send()
     for piece in pieces[:4]:
         piece.event(5)
     for copy in give_own + [small_core, small_y, small_far]:
@@ -459,24 +748,18 @@
     return lax.ppermute(value, axis, [(i, i ^ bit) for i in range(size)])
 
 
-def reduce_slots(partial_sums, dp):
-    add = lambda a, b: (a.astype(F32) + b.astype(F32))
-    got = swap(partial_sums[1::2], "tensor", 4, 1)
-    two = add(partial_sums[0::2], got).astype(BF)
-    got = swap(two[1], "tensor", 4, 2)
-    one = add(two[0], got)
-    lead = one.shape[:-2]
-    rows, cols = one.shape[-2:]
-    bits = dp.bit_length() - 1
-    one = one.reshape(lead + (2,) * bits + (rows // dp, cols))
+def finish_rows(value, dp, bits_done):
     me = lax.axis_index("dp")
-    for bit in range(bits):
-        axis = one.ndim - 3
+    left = dp.bit_length() - 1 - bits_done
+    rows, cols = value.shape
+    value = value.reshape((2,) * left + (rows >> left, cols))
+    for bit in range(left):
+        axis = value.ndim - 3
         mine = (me >> bit) & 1
-        keep = lax.dynamic_index_in_dim(one, mine, axis, keepdims=False)
-        send = lax.dynamic_index_in_dim(one, 1 - mine, axis, keepdims=False).astype(BF)
-        one = add(keep, swap(send, "dp", dp, 1 << bit))
-    return one
+        keep = lax.dynamic_index_in_dim(value, mine, axis, keepdims=False)
+        send = lax.dynamic_index_in_dim(value, 1 - mine, axis, keepdims=False)
+        value = keep + swap(send, "dp", dp, 1 << bit)
+    return value
 
 
 def on_device(
@@ -514,22 +797,27 @@
         return layer_kernel(bits, *refs)
 
     dma = pltpu.SemaphoreType.DMA
-    output, input_grad, small, ges, gsh, gpair, grw, gew, gat = pl.pallas_call(
+    count = sum(len(order) for orders in ORDERS for order in orders) + sum(
+        order.index("y") for orders in ORDERS for order in orders
+    )
+    block = width // 8
+    output, input_grad, gaw, gmw, gew, grw, both = pl.pallas_call(
         kernel,
         in_specs=[smem] + [vmem] * 9 + [hbm] * 5,
-        out_specs=[vmem] * 6 + [hbm] * 3,
+        out_specs=[vmem] * 7,
         out_shape=[
-            sds((rows, width), BF), sds((rows, width), BF), sds((8, width), F32),
-            sds((4, 1, hidden), F32), sds((4, 2, local), F32), sds((4, 2 * BUCKETS, 256), F32),
-            sds((4, width, hidden), BF), sds((4, width, hidden), BF), sds((4, width, 4 * local), BF),
+            sds((rows, width), BF), sds((rows, width), BF), sds((3, block, local), F32),
+            sds((local, block), F32), sds((block, hidden), F32), sds((block, hidden), F32),
+            sds((SMALL_ROWS, width), F32),
         ],
         scratch_shapes=[
-            pltpu.VMEM((4, 3, width, local), BF),
+            pltpu.VMEM((4, 3, local, width), BF),
             pltpu.VMEM((4, local, width), BF),
             pltpu.VMEM((4, width, hidden), BF),
             pltpu.VMEM((4, hidden, width), BF),
             pltpu.VMEM((rows, width), BF),
             pltpu.VMEM((rows, 128), BF),
+            pltpu.VMEM((rows, 2 * BUCKETS), BF),
             pltpu.VMEM((4, rows, 256), BF),
             pltpu.VMEM((4, rows, 256), BF),
             pltpu.VMEM((4, rows, 256), BF),
@@ -548,65 +836,46 @@
             pltpu.VMEM((rows, 256), BF),
             pltpu.VMEM((rows, 4 * local), BF),
             pltpu.VMEM((4, SMALL_ROWS, hidden), F32),
-            dma((2, 8)), dma((2, 8)), dma((2, 8)), dma((2, 8)), dma((2, 4)), dma((2, 3)), dma((17,)),
+            pltpu.VMEM((3, 2, width, hidden), BF),
+            pltpu.VMEM((9, 15 * block, CHUNK), BF),
+            pltpu.VMEM((4, SMALL_ROWS, width), F32),
+            pltpu.VMEM((2, SMALL_ROWS, width), F32),
+            pltpu.VMEM((4, SMALL_ROWS, width), F32),
+            dma((2, 8)), dma((2, 8)), dma((2, 8)), dma((2, 8)), dma((2, 4)), dma((2, 3)), dma((5,)),
+            dma((2, 6)), dma((2, count)), dma((2, 6)),
         ],
         compiler_params=pltpu.CompilerParams(
             collective_id=0, has_side_effects=True, vmem_limit_bytes=VMEM_LIMIT
         ),
     )(
-        page_lengths, inputs, layout_cells, attend_shift, expand_shift.reshape(1, hidden),
-        bias_tables.reshape(2 * heads, BUCKETS), merge_shift.reshape(1, width),
-        reduce_shift.reshape(1, width), norm_gains, norm_shifts,
-        attend_weight, merge_weight, expand_weight, reduce_weight, cotangent,
-    )
-
-    grad_rw = reduce_slots(grw, dp).T
-    grad_ew = reduce_slots(gew, dp)
-    grad_at = reduce_slots(gat, dp)
-    grad_mw = grad_at[:, :local].T
-    grad_aw = jnp.transpose(grad_at[:, local:].reshape(-1, 3, local), (1, 0, 2))
-
-    spot = jnp.arange(BUCKETS, dtype=jnp.int32)
-    bucket_of = jnp.clip(spot[:, None] - spot[None, :] + BUCKETS // 2, 0, BUCKETS - 1)
-    folding = (bucket_of[:, :, None] == spot[None, None, :]).astype(F32)
-    split = gpair.reshape(4, 2, BUCKETS, 4, 2, BUCKETS)
-    grad_pairs = jnp.stack([split[:, a, :, :heads, a, :] for a in range(2)], axis=1)
-    grad_tables = jnp.einsum("raxhy,xyb->rahb", grad_pairs, folding, precision=lax.Precision.HIGHEST)
-    spare = -(2 * local + hidden + 2 * heads * BUCKETS) % width
-    own = jnp.concatenate(
-        [
-            gsh.reshape(4, -1),
-            ges.reshape(4, -1),
-            grad_tables.reshape(4, -1),
-            jnp.zeros((4, spare), F32),
-        ],
-        axis=1,
-    ).reshape(4, -1, width)
-    shared = small[:6]
-    lines = own.shape[1]
-    for bit, take in ((1, 2), (2, 1)):
-        got = swap(jnp.concatenate([shared, own[1::2].reshape(-1, width)], axis=0), "tensor", 4, bit)
-        shared = shared + got[:6]
-        own = own[0::2] + got[6:].reshape(take, lines, width)
-    both = jnp.concatenate([shared, own[0]], axis=0)
-    for bit in range(dp.bit_length() - 1):
-        both = both + swap(both, "dp", dp, 1 << bit)
-    flat = both[6:].reshape(-1)
-    cut = 2 * local + hidden
+        page_lengths, inputs, layout_cells, attend_shift, expand_shift,
+        jnp.transpose(bias_tables, (1, 0, 2)), merge_shift, reduce_shift, norm_gains, norm_shifts,
+        jnp.transpose(attend_weight, (0, 2, 1)), merge_weight, expand_weight, reduce_weight, cotangent,
+    )
+
+    if top > 3:
+        grw = finish_rows(grw, dp, 3)
+        gew = finish_rows(gew, dp, 3)
+        gmw = finish_rows(gmw.T, dp, 3).T
+        gaw = jnp.stack([finish_rows(gaw[m], dp, 3) for m in range(3)])
+        for bit in range(top - 3):
+            both = both + swap(both, "dp", dp, 1 << bit)
+    first = SHARED
+    tables = both[3 : 3 + 2 * heads, :BUCKETS].reshape(heads, 2, BUCKETS)
     return (
         output,
         input_grad,
-        grad_aw,
-        flat[: 2 * local].reshape(2, local),
-        grad_mw,
-        both[2],
-        jnp.stack([both[0], both[3]]),
-        jnp.stack([both[1], both[4]]),
-        grad_ew,
-        flat[2 * local : cut],
-        grad_rw,
-        both[5],
-        flat[cut : cut + 2 * heads * BUCKETS].reshape(2, heads, BUCKETS),
+        gaw,
+        both[1:3, :local],
+        gmw,
+        both[first + 2],
+        jnp.stack([both[first], both[first + 3]]),
+        jnp.stack([both[first + 1], both[first + 4]]),
+        gew,
+        both[0],
+        grw.T,
+        both[first + 5],
+        jnp.transpose(tables, (1, 0, 2)),
     )
 
 

time: 255 us -> 149 us (0.58)
  waiting for transfers between devices: 75.4 us -> 0 us
  Pallas kernels: 92.2 us -> 137 us
  local copies, waits for them, and re-layouts: 38.8 us -> 10.1 us
  other arithmetic: 24.3 us -> 0.61 us
  starting transfers between devices: 21.2 us -> 0 us
    ppermute x20 -> x0, waiting for transfers between devices: 75.4 us -> none  [swap(): return lax.ppermute(value, axis, [(i, i ^ bit) for i in range(size)])]
    pallas_call x1, Pallas kernels: 92.2 us -> 137 us  [on_device(): pl.pallas_call(kernel, in_specs=[smem] + [vmem] * 9 + [hbm] * 5, out_spec...]
    ppermute x20 -> x0, starting transfers between devices: 21.2 us -> none  [swap(): return lax.ppermute(value, axis, [(i, i ^ bit) for i in range(size)])]
    add x17 -> x0, other arithmetic: 11.9 us -> none  [the longest x11 11.9 us: reduce_slots(): add = lambda a, b: a.astype(F32) + b.astype(F32)]
    slice x14 -> x3, local copies, waits for them, and re-layouts: 12.4 us -> 3.68 us  [the longest x1 1.71 us: on_device(): both[first + 1]]
    convert_element_type x3 -> x0, other arithmetic: 8.08 us -> none  [reduce_slots(): two = add(partial_sums[0::2], got).astype(BF)]
    reshape x12 -> x1, local copies, waits for them, and re-layouts: 6.45 us -> 0.59 us  [on_device(): tables = both[3:3 + 2 * heads, :BUCKETS].reshape(heads, 2, BUCKETS)]
    convert_element_type x9 -> x0, local copies, waits for them, and re-layouts: 5.01 us -> none  [reduce_slots(): lax.dynamic_index_in_dim(one, 1 - mine, axis, keepdims=False).astype(BF)]
  transfers between devices with their start and end apart: 20 -> 0, of which waited for: 11 -> 0; matrix products, arithmetic and copies ran while one was open for 19% -> 0% of each run, Pallas kernels for 0% -> 0%
where the time goes in v3:
time: 149 us
  Pallas kernels  137 us (92%)
  local copies, waits for them, and re-layouts  10.1 us (7%)
    pallas_call x1, Pallas kernels, on_device(): pl.pallas_call(kernel, in_specs=[smem] + [vmem] * 9 + [hbm] * 5, out_spec...  137 us
    unnamed x16, local copies, waits for them, and re-layouts  5.79 us

profile of v3, /device:TPU:0, one launch (start us, length us, event | category | flops | bytes accessed | tf_op | source)
XLA Modules:
  0.0 148.7 jit_solution(832883276258062047)
XLA Ops:
  0.7 137.3 %shard_map.246 = (bf16[512,768]{1,0:T(8,128)(2,1)}, bf16[512,768]{1,0:T(8,128)(2,1)}, f32[3,96,192]{2,1,0:T(8,128)}, f32[192,96]{1,0:T(8,128)}, f32[96,768]{1,0:...) custom-call(s32[4,8]{1,0:T(4,128)} %refs_0_.1, bf16[512,768]{1,0:T(8,128)(2,1)} %refs_1_.1, s32[2,2048]{1,0:T(2,128)} %refs_2_.1, ...), custom_call_target="tpu_custom_call" | custom-call | tf_op jit(solution)/shard_map/pallas_call | solution.py:804
  138.0 0.0 copy-start
  138.0 1.7 %fusion = (f32[1,768]{1,0:T(1,128)S(1)}, f32[1,768]{1,0:T(1,128)S(1)}, f32[1,768]{1,0:T(1,128)S(1)}, f32[1,768]{1,0:T(1,128)S(1)}, f32[768]{0:T(1024)}, /*index=5*/f32[768]{0:T(1024)}, f32[768]{0:T(1024)}) fusion(f32[16,768]{1,0:T(8,128)} %get-tuple-element.23), kind=kLoop, calls=%fused_computation.5 | loop fusion | bytes 43008 | tf_op jit(solution)/shard_map/slice | solution.py:873
  139.7 0.6 pad_maximum_fusion
  140.3 0.7 slice.35
  141.0 0.6 reshape.29
  141.6 1.3 slice.27
  142.9 0.0 copy-start.3
  142.9 2.1 %copy.34 = bf16[512,768]{1,0:T(8,128)(2,1)} copy(bf16[512,768]{1,0:T(8,128)(2,1)} %get-tuple-element.52) | data formatting | bytes 1572864
  145.0 0.0 copy-done
  145.0 0.0 copy-start.4
  145.0 0.0 copy-start.2
  145.0 0.0 copy-start.1
  145.0 0.9 copy.35
  145.9 0.0 copy-done.3
  145.9 0.7 copy.36
  146.6 0.0 copy-done.4
  146.6 0.6 copy.37
  147.3 0.0 copy-done.2
  147.3 0.7 copy.38
  148.0 0.0 copy-done.1
  148.0 0.7 copy.39
Async XLA Ops:
  138.0 7.0 %copy-start = (bf16[512,768]{1,0:T(8,128)(2,1)S(1)}, bf16[512,768]{1,0:T(8,128)(2,1)}, u32[]{:S(2)}) copy-start(bf16[512,768]{1,0:T(8,128)(2,1)} %get-tuple-element.53) | copy-start | bytes 2359300
  142.9 3.0 %copy-start.3 = (f32[3,96,192]{2,1,0:T(8,128)S(1)}, f32[3,96,192]{2,1,0:T(8,128)}, u32[]{:S(2)}) copy-start(f32[3,96,192]{2,1,0:T(8,128)} %get-tuple-element.54) | copy-start | bytes 663556
  145.0 1.6 %copy-start.4 = (f32[192,96]{1,0:T(8,128)S(1)}, f32[192,96]{1,0:T(8,128)}, u32[]{:S(2)}) copy-start(f32[192,96]{1,0:T(8,128)} %get-tuple-element.56) | copy-start | bytes 221188
  145.0 2.3 %copy-start.2 = (f32[96,768]{1,0:T(8,128)S(1)}, f32[96,768]{1,0:T(8,128)}, u32[]{:S(2)}) copy-start(f32[96,768]{1,0:T(8,128)} %get-tuple-element.60) | copy-start | bytes 884740
  145.0 3.0 %copy-start.1 = (f32[96,768]{1,0:T(8,128)S(1)}, f32[96,768]{1,0:T(8,128)}, u32[]{:S(2)}) copy-start(f32[96,768]{1,0:T(8,128)} %get-tuple-element.26) | copy-start | bytes 884740

commit v4 on v3

--- a/solution.py
+++ b/solution.py
@@ -14,6 +14,275 @@
 BF = jnp.bfloat16
 F32 = jnp.float32
 VMEM_LIMIT = 60 * 1024 * 1024
+PIECES = (
+    ("aw0", 0, 192, (0, 1)),
+    ("aw1", 0, 192, (1, 0)),
+    ("aw2", 0, 192, (1,)),
+    ("mw", 0, 192, (1, 0)),
+    ("ew", 0, 384, (0, 1)),
+    ("ew", 384, 384, (1, 0)),
+    ("rw", 0, 384, (0, 1)),
+    ("rw", 384, 384, ()),
+)
+CHUNKS = (
+    (
+        (0, 256, ("y", 0, 1, 2)),
+        (256, 256, (0, "y", 1, 2)),
+        (512, 256, (1, "y", 0, 2)),
+    ),
+    (
+        (0, 256, ("y", 0, 1, 2)),
+        (256, 256, (0, "y", 1, 2)),
+        (512, 256, (1, 0, "y", 2)),
+    ),
+    (
+        (0, 256, ("y", 0, 1, 2)),
+        (256, 256, (0, "y", 1, 2)),
+        (512, 256, (1, 0, "y", 2)),
+    ),
+)
+PLAN = {
+    ("start", 0, 0): (
+        ("gs", 0, 0),
+        ("gs", 1, 0),
+        ("gs", 2, 0),
+        ("gs", 3, 0),
+        ("gs", 4, 0),
+        ("gs", 5, 0),
+        ("gs", 6, 0),
+        ("gs", 7, 0),
+    ),
+    ("att", 1, 0): (
+        ("gt", 0, 1),
+        ("gs", 0, 1),
+        ("gt", 1, 1),
+        ("gs", 1, 1),
+    ),
+    ("att", 2, 0): (
+        ("gt", 3, 1),
+        ("gs", 3, 1),
+        ("gt", 0, 2),
+        ("gs", 0, 2),
+        ("gt", 1, 2),
+        ("gs", 1, 2),
+        ("gt", 2, 1),
+        ("gs", 2, 1),
+        ("gt", 3, 2),
+        ("gs", 3, 2),
+        ("gt", 4, 1),
+        ("gs", 4, 1),
+        ("gt", 1, 3),
+        ("gs", 1, 3),
+        ("gt", 1, 4),
+        ("gt", 5, 1),
+        ("gs", 5, 1),
+        ("gt", 0, 3),
+        ("gs", 0, 3),
+        ("gt", 2, 2),
+    ),
+    ("att", 2, 1): (
+        ("gs", 2, 2),
+    ),
+    ("att", 2, 3): (
+        ("gt", 0, 4),
+        ("gt", 6, 1),
+        ("gs", 6, 1),
+        ("gt", 3, 3),
+    ),
+    ("att", 3, 0): (
+        ("gs", 3, 3),
+        ("gt", 4, 2),
+        ("gs", 4, 2),
+        ("gt", 2, 3),
+    ),
+    ("att", 3, 1): (
+        ("gt", 5, 2),
+        ("gs", 5, 2),
+    ),
+    ("att", 3, 3): (
+        ("gt", 3, 4),
+    ),
+    ("feed", 0, 1): (
+        ("gt", 6, 2),
+        ("gs", 6, 2),
+    ),
+    ("feed", 1, 1): (
+        ("gt", 4, 3),
+        ("gs", 4, 3),
+    ),
+    ("feed", 2, 0): (
+        ("gt", 7, 1),
+        ("gs", 7, 1),
+        ("gt", 5, 3),
+    ),
+    ("feed", 2, 1): (
+        ("gs", 5, 3),
+        ("gt", 4, 4),
+        ("gt", 7, 2),
+        ("gt", 6, 3),
+    ),
+    ("feed", 3, 0): (
+        ("gs", 6, 3),
+        ("gt", 5, 4),
+    ),
+    ("feed", 3, 1): (
+        ("gt", 6, 4),
+    ),
+    ("fa", 3, 1): (
+        ("cs", 0, 3),
+    ),
+    ("fa", 1, 1): (
+        ("cs", 0, 1),
+    ),
+    ("fa", 0, 0): (
+        ("ct", 0, 2),
+        ("s", 0, 0, "y", 2),
+        ("s", 0, 1, 0, 2),
+        ("s", 0, 2, 1, 2),
+    ),
+    ("fb", 3, 1): (
+        ("cs", 1, 3),
+        ("ct", 0, 0),
+        ("s", 0, 1, 0, 0),
+        ("s", 0, 2, 1, 0),
+    ),
+    ("fb", 1, 0): (
+        ("ct", 1, 2),
+        ("s", 1, 0, "y", 2),
+        ("s", 1, 1, 0, 2),
+        ("s", 1, 2, 1, 2),
+    ),
+    ("fb", 1, 1): (
+        ("cs", 1, 1),
+        ("t", 0, 1, 0, 2),
+        ("s", 0, 1, "y", 2),
+        ("t", 0, 2, 1, 2),
+        ("s", 0, 2, "y", 2),
+    ),
+    ("lnb", 0, 0): (
+        ("ct", 1, 0),
+        ("s", 1, 1, 0, 0),
+        ("s", 1, 2, 1, 0),
+    ),
+    ("ab", 3, 0): (
+        ("t", 0, 0, "y", 2),
+        ("s", 0, 0, 0, 0),
+        ("t", 0, 1, 0, 0),
+        ("t", 0, 2, 1, 0),
+    ),
+    ("ab", 3, 2): (
+        ("t", 1, 1, 0, 2),
+        ("s", 1, 1, "y", 2),
+        ("t", 1, 2, 1, 2),
+        ("s", 1, 2, 0, 2),
+    ),
+    ("ab", 3, 3): (
+        ("cs", 2, 3),
+    ),
+    ("ab", 2, 1): (
+        ("t", 1, 2, 1, 0),
+        ("s", 1, 2, 0, 0),
+    ),
+    ("ab", 2, 2): (
+        ("t", 0, 1, "y", 2),
+        ("s", 0, 1, 1, 0),
+    ),
+    ("ab", 2, 3): (
+        ("ct", 2, 2),
+        ("s", 2, 0, "y", 2),
+        ("s", 2, 1, 0, 2),
+        ("s", 2, 2, 1, 2),
+    ),
+    ("ab", 1, 0): (
+        ("t", 1, 1, 0, 0),
+    ),
+    ("ab", 1, 1): (
+        ("t", 0, 0, 0, 0),
+        ("s", 0, 0, 1, 0),
+    ),
+    ("ab", 1, 2): (
+        ("t", 0, 1, 1, 0),
+        ("s", 0, 1, 2, 0),
+        ("t", 1, 0, "y", 2),
+        ("s", 1, 0, 0, 0),
+    ),
+    ("ab", 1, 3): (
+        ("cs", 2, 1),
+        ("t", 1, 2, 0, 2),
+        ("s", 1, 2, "y", 2),
+    ),
+    ("ab", 0, 0): (
+        ("t", 1, 2, 0, 0),
+    ),
+    ("ab", 0, 1): (
+        ("t", 0, 2, "y", 2),
+        ("s", 0, 2, 0, 0),
+    ),
+    ("ab", 0, 2): (
+        ("t", 0, 0, 1, 0),
+        ("s", 0, 0, 2, 0),
+    ),
+    ("ab", 0, 3): (
+        ("ms", 0),
+        ("ct", 2, 0),
+        ("s", 2, 1, 0, 0),
+        ("s", 2, 2, 1, 0),
+        ("t", 2, 2, 1, 2),
+        ("s", 2, 2, 0, 2),
+    ),
+    ("end", 0, 0): (
+        ("t", 0, 1, 2, 0),
+        ("t", 1, 1, "y", 2),
+        ("s", 1, 1, 1, 0),
+        ("t", 2, 1, 0, 2),
+        ("s", 2, 1, "y", 2),
+        ("mt", 0),
+        ("ms", 1),
+        ("t", 0, 0, 2, 0),
+        ("t", 1, 0, 0, 0),
+        ("s", 1, 0, 1, 0),
+        ("t", 1, 2, "y", 2),
+        ("s", 1, 2, 2, 0),
+        ("t", 0, 2, 0, 0),
+        ("s", 0, 2, 2, 0),
+        ("t", 1, 1, 1, 0),
+        ("s", 1, 1, 2, 0),
+        ("t", 2, 2, 1, 0),
+        ("s", 2, 2, 0, 0),
+        ("t", 2, 2, 0, 2),
+        ("s", 2, 2, "y", 2),
+        ("t", 2, 1, 0, 0),
+        ("t", 1, 0, 1, 0),
+        ("s", 1, 0, 2, 0),
+        ("t", 1, 2, 2, 0),
+        ("t", 2, 0, "y", 2),
+        ("s", 2, 0, 0, 0),
+        ("t", 2, 2, 0, 0),
+        ("t", 2, 1, "y", 2),
+        ("s", 2, 1, 1, 0),
+        ("mt", 1),
+        ("ms", 2),
+        ("t", 0, 2, 2, 0),
+        ("t", 1, 1, 2, 0),
+        ("t", 2, 2, "y", 2),
+        ("s", 2, 2, 2, 0),
+        ("t", 1, 0, 2, 0),
+        ("mt", 2),
+        ("ms", 3),
+        ("t", 2, 1, 1, 0),
+        ("s", 2, 1, 2, 0),
+        ("t", 2, 0, 0, 0),
+        ("s", 2, 0, 1, 0),
+        ("t", 2, 2, 2, 0),
+        ("mt", 3),
+        ("ms", 4),
+        ("t", 2, 1, 2, 0),
+        ("t", 2, 0, 1, 0),
+        ("s", 2, 0, 2, 0),
+        ("mt", 4),
+        ("t", 2, 0, 2, 0),
+    ),
+}
 
 
 def mm(a, b, da, db):
@@ -107,79 +376,38 @@
 
 
 class Piece:
-    def __init__(self, net, number, own, slots, start, count, x_first, sems):
-        self.net, self.number, self.own, self.slots = net, number, own, slots
-        self.start, self.count, self.x_first = start, count, x_first
-        self.y_sems, self.one_sems, self.two_sems, self.core_sems = sems
-        self.first, self.second = (0, 1) if x_first else (1, 0)
-
-    def quarter(self, ref, flip):
-        net = self.net
-        fast = net.bit[self.first]
-        if flip:
-            fast = 1 - fast
-        index = net.bit[self.second] * 2 + fast
-        return rows_at(ref, self.start + index * (self.count // 4), self.count // 4)
-
-    def half(self, ref, flip):
-        slow = self.net.bit[self.second]
-        if flip:
-            slow = 1 - slow
-        return rows_at(ref, self.start + slow * (self.count // 2), self.count // 2)
-
-    def full(self, ref):
-        return rows_at(ref, self.start, self.count)
-
-    def over_y(self):
-        return remote(
-            self.quarter(self.own, False), self.quarter(self.slots(2), False),
-            self.y_sems, self.number, self.net.y,
-        )
-
-    def hop_one(self, flip=False):
-        here = self.quarter(self.slots(2), flip)
-        return remote(here, here, self.one_sems, self.number, self.net.dp[self.first])
-
-    def hop_two(self, flip=False):
-        here = self.half(self.slots(2), flip)
-        return remote(here, here, self.two_sems, self.number, self.net.dp[self.second])
-
-    def to_core(self):
-        return remote(
-            self.full(self.slots(2)), self.full(self.slots(3)),
-            self.core_sems, self.number, self.net.core,
-        )
-
-    def event(self, stage):
-        if stage == 0:
-            self.over_y().start()
-        elif stage == 1:
-            self.over_y().wait_recv()
-            self.hop_one().start()
-        elif stage == 2:
-            self.hop_one(True).wait_recv()
-            self.hop_two().start()
-        elif stage == 3:
-            self.hop_two(True).wait_recv()
-            self.to_core().start()
-        elif stage == 4:
-            self.to_core().wait_recv()
+    def __init__(self, net, own, slots, start, count, axes, sems, first):
+        self.net, self.own, self.slots, self.start, self.count = net, own, slots, start, count
+        self.axes, self.sems, self.first = axes, sems, first
+
+    def region(self, hop, flip):
+        index, weight = 0, 1
+        for axis in self.axes[hop - 1 :]:
+            bit = self.net.bit[axis]
+            index = index + weight * ((1 - bit) if flip and weight == 1 else bit)
+            weight *= 2
+        rows = self.count // weight
+        return self.start + index * rows, rows
+
+    def hop(self, number, arriving=False):
+        if number == len(self.axes) + 1:
+            here = rows_at(self.slots(2), self.start, self.count)
+            there, partner = rows_at(self.slots(3), self.start, self.count), self.net.core
+        elif number == 0:
+            start, rows = self.region(1, False)
+            here, partner = rows_at(self.own, start, rows), self.net.y
+            there = rows_at(self.slots(2), start, rows)
         else:
-            self.over_y().wait_send()
-            self.hop_one().wait_send()
-            self.hop_two().wait_send()
-            self.to_core().wait_send()
-
-
-CHUNK = 256
+            here = there = rows_at(self.slots(2), *self.region(number, arriving))
+            partner = self.net.dp[self.axes[number - 1]]
+        return remote(here, there, self.sems, self.first + number, partner)
+
+    def sent(self):
+        for number in range(len(self.axes) + 2):
+            self.hop(number).wait_send()
+
+
 SHARED = 9
-ORDERS = (
-    (("y", 0, 1, 2), (0, "y", 1, 2), (1, "y", 0, 2)),
-    (("y", 0, 1, 2), (0, "y", 1, 2), (1, 0, "y", 2)),
-    (("y", 0, 1, 2), (0, "y", 1, 2), (1, 0, "y", 2)),
-)
-
-
 class Stage:
     def __init__(self, net, axis, slot, fixed, values, room, index, sems, block):
         self.net, self.axis, self.slot, self.fixed, self.values = net, axis, slot, dict(fixed), values
@@ -234,18 +462,16 @@
         self.all_of_it().wait_send()
 
 
-def chunk_stages(net, unit, chunk, slots, got, sems, first, block):
-    lanes = pl.ds(chunk * CHUNK, CHUNK)
-
+def chunk_stages(net, order, lanes, slots, got, sems, first, block):
     def values(slot, start, count):
         return slots(slot).at[pl.ds(pl.multiple_of(start, 32), count), lanes]
 
     stages, fixed, live, at = {}, {}, (2, 0), 0
-    for axis in ORDERS[unit][chunk]:
+    for axis in order:
         exchanges = (2,) if axis == "y" else live
         for slot in exchanges:
             count = (8 * block) >> (len(fixed) + (axis != "y"))
-            room = lambda start, rows, at=at: got.at[pl.ds(at + start, rows), :]
+            room = lambda start, rows, at=at: got.at[pl.ds(at + start, rows), lanes]
             stages[(axis, slot)] = Stage(
                 net, axis, slot, fixed, values, room, first + len(stages), sems, block
             )
@@ -257,23 +483,14 @@
     return stages
 
 
-def at_step(index, table):
-    for value, actions in table.items():
-
-        @pl.when(index == value)
-        def _():
-            for action in actions:
-                action()
-
-
 def layer_kernel(
     bits,
     pages_ref, x_ref, cells_ref, shift_ref, es_ref, tables_ref, ms_ref, rs_ref, gain_ref, nshift_ref,
     aw_hbm, mw_hbm, ew_hbm, rw_hbm, cot_hbm,
     out_ref, gin_ref, gaw_ref, gmw_ref, gew_ref, grw_ref, both_ref,
     AW, MW, EW, RW, XR, HOT, BACK, Q, K, V, PR, CTX, NB, HAT, SCALE, AS, ACC, GB, GC, DQ, DK, DV, E, DD, SM,
-    FROM_CORE, FROM, SUMS, SUMS_CORE, SUMS_FAR,
-    y_sems, one_sems, two_sems, core_sems, own_sems, small_sems, local_sems,
+    FROM_CORE, FROM, MIX, SUMS, SUMS_CORE, SUMS_FAR,
+    in_sems, own_sems, small_sems, local_sems,
     unit_sems, stage_sems, total_sems,
 ):
     net = Net(bits)
@@ -293,17 +510,18 @@
     for h in range(heads):
         SM[0, 8 + 2 * h : 10 + 2 * h, :BUCKETS] = tables_ref[h].astype(F32)
 
-    plan = []
-    sems = (y_sems, one_sems, two_sems, core_sems)
-    for m in range(3):
-        plan.append((aw_hbm.at[m], (lambda s, m=m: AW.at[s, m]), 0, local, m % 2 == 0))
-    plan.append((mw_hbm, (lambda s: MW.at[s]), 0, local, False))
-    for own, ref, count in ((ew_hbm, EW, width), (rw_hbm, RW, hidden)):
-        for part in range(2):
-            plan.append(
-                (own, (lambda s, ref=ref: ref.at[s]), part * (count // 2), count // 2, part == 0)
-            )
-    pieces = [Piece(net, n, *entry, sems) for n, entry in enumerate(plan)]
+    whole_of = {
+        "aw0": (aw_hbm.at[0], lambda s: AW.at[s, 0]),
+        "aw1": (aw_hbm.at[1], lambda s: AW.at[s, 1]),
+        "aw2": (aw_hbm.at[2], lambda s: AW.at[s, 2]),
+        "mw": (mw_hbm, lambda s: MW.at[s]),
+        "ew": (ew_hbm, lambda s: EW.at[s]),
+        "rw": (rw_hbm, lambda s: RW.at[s]),
+    }
+    pieces = [
+        Piece(net, *whole_of[name], start, count, axes, in_sems, 4 * n)
+        for n, (name, start, count, axes) in enumerate(PIECES)
+    ]
     weights = ((aw_hbm, AW), (mw_hbm, MW), (ew_hbm, EW), (rw_hbm, RW))
     keep_own = [
         pltpu.make_async_copy(own, ref.at[0], local_sems.at[n]) for n, (own, ref) in enumerate(weights)
@@ -317,18 +535,6 @@
     keep_own[0].start()
     keep_own[1].start()
     pl.semaphore_wait(barrier, len(greeted))
-    small_y.start()
-    for piece in pieces[:4]:
-        piece.event(0)
-    small_core.start()
-    for copy in give_own:
-        copy.start()
-    for piece in pieces[4:]:
-        piece.event(0)
-    keep_own[2].start()
-    keep_own[3].start()
-    fetch_cot.start()
-
     block = width // 8
     units = (
         (lambda slot: RW.at[slot]),
@@ -336,10 +542,10 @@
         (lambda slot: AS.at[slot, pl.ds(0, width), :]),
     )
     flows, first = {}, 0
-    for unit in range(3):
-        for chunk in range(3):
+    for unit, chunks in enumerate(CHUNKS):
+        for chunk, (lane, lanes, order) in enumerate(chunks):
             stages = chunk_stages(
-                net, unit, chunk, units[unit], FROM.at[unit * 3 + chunk], stage_sems, first, block
+                net, order, pl.ds(lane, lanes), units[unit], FROM.at[unit], stage_sems, first, block
             )
             flows[unit, chunk] = stages
             first += len(stages)
@@ -354,23 +560,93 @@
         here = units[unit](slot)
         here[...] = here[...] + FROM_CORE[unit, slot // 2]
 
-    def send(unit, chunk, axis, slot=0):
-        return flows[unit, chunk][axis, 2 if axis == "y" else slot].send
-
-    def take(unit, chunk, axis, slot=0):
-        return flows[unit, chunk][axis, 2 if axis == "y" else slot].take
-
-    def open_far(unit):
-        return [
-            lambda: add_core(unit, 2),
-            send(unit, 0, "y"), send(unit, 1, 0, 2), send(unit, 2, 1, 2),
-        ]
-
-    def open_near(unit):
-        return [lambda: add_core(unit, 0), send(unit, 1, 0, 0), send(unit, 2, 1, 0)]
-
-    def happen(*pairs):
-        return [lambda n=n, s=s: pieces[n].event(s) for n, s in pairs]
+    sums_core = [
+        remote(SUMS.at[2 * n + 1], SUMS_CORE.at[n], total_sems, n, net.core) for n in range(2)
+    ]
+    sums_far = [
+        remote(SUMS.at[2 - 2 * (n > 0)], SUMS_FAR.at[n], total_sems, 2 + n, partner)
+        for n, partner in enumerate([net.y] + net.dp)
+    ]
+    shared = slice(SHARED, SHARED + 6)
+
+    def send_totals(k):
+        if k == 0:
+            for copy in sums_core:
+                copy.start()
+        else:
+            sums_far[k - 1].start()
+
+    def take_totals(k):
+        if k == 0:
+            for n, copy in enumerate(sums_core):
+                copy.wait_recv()
+                SUMS[2 * n] = SUMS[2 * n] + SUMS_CORE[n]
+            SUMS[2, shared, :] = SUMS[0, shared, :]
+        else:
+            sums_far[k - 1].wait_recv()
+            if k > 1:
+                sums_far[k - 1].wait_send()
+            SUMS[0] = SUMS[0] + SUMS_FAR[k - 1]
+
+    results = (grw_ref, gew_ref, MIX)
+
+    def take(unit, chunk, axis, slot):
+        stages = flows[unit, chunk]
+        stage = stages[axis, slot]
+        if stage is not list(stages.values())[-1]:
+            stage.take()
+            return
+        stage.all_of_it().wait_recv()
+        (start, count), = stage.ours()
+        lane, lanes, _ = CHUNKS[unit][chunk]
+        mine = stage.values(0, start, count)[...].astype(F32)
+        results[unit][:, lane : lane + lanes] = mine + stage.room(0, count)[...].astype(F32)
+
+    def act(kind, *what):
+        if kind == "gs":
+            pieces[what[0]].hop(what[1]).start()
+        elif kind == "gt":
+            pieces[what[0]].hop(what[1] - 1, True).wait_recv()
+        elif kind == "cs":
+            to_core(*what).start()
+        elif kind == "ct":
+            add_core(*what)
+        elif kind == "s":
+            flows[what[0], what[1]][what[2], what[3]].send()
+        elif kind == "t":
+            take(*what)
+        elif kind == "ms":
+            send_totals(*what)
+        else:
+            take_totals(*what)
+
+    def do(actions):
+        for action in actions:
+            act(*action)
+
+    def at(phase, point, index=None, before=None):
+        if index is None:
+            do(PLAN.get((phase, 0, point), ()))
+            return
+        for r in range(4):
+            first = (before or {}).get(r, ())
+            actions = PLAN.get((phase, r, point), ())
+            if first or actions:
+
+                @pl.when(index == r)
+                def _():
+                    for wait in first:
+                        wait()
+                    do(actions)
+
+    small_y.start()
+    at("start", 0)
+    small_core.start()
+    for copy in give_own:
+        copy.start()
+    keep_own[2].start()
+    keep_own[3].start()
+    fetch_cot.start()
 
     begin, bounds = page_scalars(pages_ref, net.t, half)
     perm = (iota((rows, rows), 1) == ((iota((rows, rows), 0) + begin) & (rows - 1))).astype(BF)
@@ -402,13 +678,12 @@
     keep_own[1].wait()
 
     def attend(r, _):
-        at_step(
-            r,
+        at(
+            "att", 0, r,
             {
                 1: [small_core.wait_recv, give_own[0].wait_recv, give_own[1].wait_recv],
-                2: happen((2, 1), (1, 2), (3, 1), (0, 3), (2, 2), (3, 2), (4, 1), (1, 3), (2, 3), (3, 3))
-                + [small_far.wait_recv]
-                + happen((0, 4), (1, 4), (2, 4), (3, 4)),
+                2: [small_y.wait_recv, small_far.start],
+                3: [small_far.wait_recv],
             },
         )
         line = nn(SM[r, 8 : 8 + 2 * heads, :BUCKETS].astype(BF), fold)
@@ -434,20 +709,20 @@
         Q[r, :, :local] = queries * jnp.asarray(HEAD_DIM ** -0.5, BF)
         K[r, :, :local] = nt(XR[...], AW[r, 1]).astype(BF)
         V[r, :, :local] = (nt(XR[...], AW[r, 2]) + SM[r, 1:2, :local]).astype(BF)
-        at_step(r, {1: happen((0, 1), (1, 1)) + [small_y.wait_recv, small_far.start]})
+        at("att", 1, r)
         same = col == row
         for block in range(2):
-            at = slice(block * half, (block + 1) * half)
+            span = slice(block * half, (block + 1) * half)
             if block == 1:
-                at_step(r, {1: happen((0, 2)), 2: happen((5, 1)), 3: happen((7, 1), (5, 2))})
+                at("att", 2, r)
             for pair in range(2):
                 lanes = slice(pair * 128, (pair + 1) * 128)
-                key_side = jnp.concatenate([K[r, at, lanes], HOT[at, :]], axis=1)
+                key_side = jnp.concatenate([K[r, span, lanes], HOT[span, :]], axis=1)
                 total = None
                 for which in range(min(2, heads - 2 * pair)):
                     keep = half_lanes(which)
                     query_side = jnp.concatenate(
-                        [Q[r, at, lanes] * keep, left[at, lanes] * keep], axis=1
+                        [Q[r, span, lanes] * keep, left[span, lanes] * keep], axis=1
                     )
                     scores = nt(key_side, query_side)
                     if block == 1:
@@ -455,10 +730,10 @@
                     weights = jnp.exp(scores - jnp.max(scores, axis=0, keepdims=True))
                     probs = (weights * (1.0 / jnp.sum(weights, axis=0, keepdims=True))).astype(BF)
                     PR[r, (2 * pair + which) * 2 + block] = probs
-                    part = tn(probs, V[r, at, lanes]) * keep.astype(F32)
+                    part = tn(probs, V[r, span, lanes]) * keep.astype(F32)
                     total = part if total is None else total + part
-                CTX[r, at, lanes] = total.astype(BF)
-        at_step(r, {2: happen((4, 2), (6, 1)), 3: happen((4, 3), (6, 2))})
+                CTX[r, span, lanes] = total.astype(BF)
+        at("att", 3, r)
         ACC[...] += nn(CTX[r, :, :local], MW[r])
         return 0
 
@@ -474,20 +749,14 @@
     keep_own[3].wait()
 
     def feed(r, _):
-        at_step(
-            r,
-            {
-                0: happen((7, 2)),
-                1: [give_own[2].wait_recv, give_own[3].wait_recv] + happen((5, 3)),
-                2: happen((6, 3), (7, 3), (4, 4), (5, 4), (6, 4), (7, 4)),
-            },
-        )
+        at("feed", 0, r, {1: [give_own[2].wait_recv, give_own[3].wait_recv]})
         pre = nn(NB[...], EW[r]) + SM[r, 2:3, :]
         gate = 0.5 * (1.0 + lax.erf(pre * (0.5 ** 0.5)))
         AS[r, :rows] = (pre * gate).astype(BF)
         AS[r, rows:] = (
             gate + pre * (jnp.exp(-0.5 * (pre * pre)) * (1.0 / math.sqrt(2.0 * math.pi)))
         ).astype(BF)
+        at("feed", 1, r)
         ACC[...] += nn(AS[r, :rows], RW[r])
         return 0
 
@@ -498,7 +767,7 @@
     gain = gain_ref[1:2, :].astype(F32)
     result = (hat * gain + nshift_ref[1:2, :].astype(F32)).astype(BF)
     perm = (iota((rows, rows), 1) == ((iota((rows, rows), 0) + begin) & (rows - 1))).astype(BF)
-    out_ref[...] = tn(perm, result).astype(BF)
+    out_ref[...] = result
     cot = nn(perm, GB[...])
     grad = norm_back(cot, hat, scale, gain)
     ACC[...] = grad
@@ -511,37 +780,31 @@
     for n, line in enumerate(shared_two):
         SUMS[0, SHARED + 3 + n : SHARED + 4 + n, :] = line
 
-    for piece in pieces[4:]:
-        piece.event(5)
-
-    def feed_back(i, _):
+    for (name, *_), piece in zip(PIECES, pieces):
+        if name in ("ew", "rw"):
+            piece.sent()
+
+    def reduce_back(i, _):
         r = 3 - i
         grad_pre = (nt(GB[...], RW[r]) * AS[r, rows:].astype(F32)).astype(BF)
+        AS[r, rows:] = grad_pre
+        SUMS[r, 0:1, :] = jnp.sum(grad_pre.astype(F32), axis=0, keepdims=True)
+        at("fa", 0, r)
         RW[r] = tn(GB[...], AS[r, :rows]).astype(BF)
-        at_step(
-            r,
-            {
-                3: [to_core(0, 3).start],
-                2: open_far(0),
-                1: [to_core(0, 1).start],
-                0: open_near(0),
-            },
-        )
-        SUMS[r, 0:1, :] = jnp.sum(grad_pre.astype(F32), axis=0, keepdims=True)
-        ACC[...] += nt(grad_pre, EW[r])
-        EW[r] = tn(NB[...], grad_pre).astype(BF)
-        at_step(
-            r,
-            {
-                3: [to_core(1, 3).start],
-                2: open_far(1),
-                1: [to_core(1, 1).start],
-                0: open_near(1),
-            },
-        )
+        at("fa", 1, r)
         return 0
 
-    lax.fori_loop(0, 4, feed_back, 0)
+    lax.fori_loop(0, 4, reduce_back, 0)
+
+    def expand_back(i, _):
+        r = 3 - i
+        ACC[...] += nt(AS[r, rows:], EW[r])
+        at("fb", 0, r)
+        EW[r] = tn(NB[...], AS[r, rows:]).astype(BF)
+        at("fb", 1, r)
+        return 0
+
+    lax.fori_loop(0, 4, expand_back, 0)
 
     grad = ACC[...]
     hat = HAT[...]
@@ -556,64 +819,24 @@
     for n, line in enumerate(shared_one):
         SUMS[0, SHARED + n : SHARED + 1 + n, :] = line
 
-    for action in (
-        take(0, 0, "y"), send(0, 0, 0),
-        take(0, 1, 0, 2), send(0, 1, "y"),
-        take(0, 2, 1, 2), send(0, 2, "y"),
-    ):
-        action()
+    at("lnb", 0)
 
     def attend_back(i, _):
         r = 3 - i
 
-        def early():
-            at_step(
-                r,
-                {
-                    3: [
-                        take(0, 1, 0, 0), take(0, 2, 1, 0),
-                        take(1, 1, 0, 2), send(1, 1, "y"),
-                        take(1, 2, 1, 2), send(1, 2, 0, 2),
-                    ],
-                    2: [take(1, 1, 0, 0), take(1, 2, 1, 0), send(1, 2, 0, 0)],
-                    1: [take(0, 2, "y"), send(0, 2, 0), take(1, 2, 0, 2), send(1, 2, "y")],
-                    0: [
-                        take(1, 1, "y"), send(1, 1, 1), take(1, 2, 0, 0),
-                        take(0, 2, 0), send(0, 2, 2),
-                    ],
-                },
-            )
-
-        def late():
-            at_step(
-                r,
-                {
-                    3: [to_core(2, 3).start, take(1, 0, "y"), send(1, 0, 0)],
-                    2: open_far(2)
-                    + [take(0, 0, 0), send(0, 0, 1), take(0, 1, "y"), send(0, 1, 1)],
-                    1: [
-                        to_core(2, 1).start,
-                        take(1, 0, 0), send(1, 0, 1),
-                        take(0, 0, 1), send(0, 0, 2), take(0, 1, 1), send(0, 1, 2),
-                    ],
-                    0: open_near(2)
-                    + [take(1, 2, "y"), send(1, 2, 2), take(1, 0, 1), send(1, 0, 2)]
-                    + [take(1, 1, 1), send(1, 1, 2)],
-                },
-            )
-
         GC[:, :local] = nt(GB[...], MW[r]).astype(BF)
+        at("ab", 0, r)
         for block in range(2):
-            at = slice(block * half, (block + 1) * half)
+            span = slice(block * half, (block + 1) * half)
             for pair in range(2):
                 lanes = slice(pair * 128, (pair + 1) * 128)
-                key_side = jnp.concatenate([K[r, at, lanes], HOT[at, :]], axis=1)
+                key_side = jnp.concatenate([K[r, span, lanes], HOT[span, :]], axis=1)
                 sums = None
                 for which in range(min(2, heads - 2 * pair)):
                     keep = half_lanes(which)
                     wide = keep.astype(F32)
                     probs = PR[r, (2 * pair + which) * 2 + block]
-                    grad_probs = nt(V[r, at, lanes] * keep, GC[at, lanes])
+                    grad_probs = nt(V[r, span, lanes] * keep, GC[span, lanes])
                     soft = probs.astype(F32)
                     inner = jnp.sum(soft * grad_probs, axis=0, keepdims=True)
                     grad_scores = (soft * (grad_probs - inner)).astype(BF)
@@ -621,23 +844,21 @@
                     parts = (
                         both[:, :128] * wide,
                         both[:, 128:] * wide,
-                        nn(grad_scores, Q[r, at, lanes]) * wide,
-                        nn(probs, GC[at, lanes]) * wide,
+                        nn(grad_scores, Q[r, span, lanes]) * wide,
+                        nn(probs, GC[span, lanes]) * wide,
                     )
                     sums = parts if sums is None else tuple(a + b for a, b in zip(sums, parts))
-                DQ[at, lanes] = (sums[0] * (HEAD_DIM ** -0.5)).astype(BF)
-                E[at, lanes] = sums[1].astype(BF)
-                DK[at, lanes] = sums[2].astype(BF)
-                DV[at, lanes] = sums[3].astype(BF)
-            if block == 0:
-                early()
+                DQ[span, lanes] = (sums[0] * (HEAD_DIM ** -0.5)).astype(BF)
+                E[span, lanes] = sums[1].astype(BF)
+                DK[span, lanes] = sums[2].astype(BF)
+                DV[span, lanes] = sums[3].astype(BF)
+            at("ab", 1 + block, r)
         for m, ref in enumerate((DQ, DK, DV)):
             DD[:, (m + 1) * local : (m + 2) * local] = ref[:, :local]
             ACC[...] += nn(ref[:, :local], AW[r, m])
         weight_grad = tn(XR[...], DD[...])
         AS[r, :width, 256:] = weight_grad[:, 256:].astype(BF)
         AS[r, :width, :256] = (weight_grad[:, :256] + tn(GB[...], CTX[r])).astype(BF)
-        late()
         SUMS[r, 1:2, :local] = jnp.sum(DQ[:, :local].astype(F32), axis=0, keepdims=True)
         SUMS[r, 2:3, :local] = jnp.sum(DV[:, :local].astype(F32), axis=0, keepdims=True)
         grad_pairs = tn(BACK[...], E[...])
@@ -649,81 +870,21 @@
                 part = jnp.where((lanes_at >= off) & (lanes_at < off + BUCKETS), part, 0.0)
                 part = pltpu.roll(part, (129 - BUCKETS - off) % 128, axis=1, stride=1, stride_axis=0)
                 SUMS[r, 3 + 2 * h + a : 4 + 2 * h + a, :128] = jnp.sum(part, axis=0, keepdims=True)
+        at("ab", 3, r)
         return 0
 
-    SUMS[1, SHARED : SHARED + 6, :] = SUMS[0, SHARED : SHARED + 6, :]
+    SUMS[1, shared, :] = SUMS[0, shared, :]
     lax.fori_loop(0, 4, attend_back, 0)
 
-    sums_core = [
-        remote(SUMS.at[2 * n + 1], SUMS_CORE.at[n], total_sems, n, net.core) for n in range(2)
-    ]
-    sums_far = [
-        remote(SUMS.at[2 - 2 * (n > 0)], SUMS_FAR.at[n], total_sems, 2 + n, partner)
-        for n, partner in enumerate([net.y] + net.dp)
-    ]
-    for copy in sums_core:
-        copy.start()
+    at("fin", 0)
     perm = (iota((rows, rows), 1) == ((iota((rows, rows), 0) + begin) & (rows - 1))).astype(BF)
     gin_ref[...] = tn(perm, ACC[...].astype(BF)).astype(BF)
-    take(2, 1, 0, 2)()
-    send(2, 1, "y")()
-    take(2, 2, 1, 2)()
-    send(2, 2, 0, 2)()
-    for n, copy in enumerate(sums_core):
-        copy.wait_recv()
-        SUMS[2 * n] = SUMS[2 * n] + SUMS_CORE[n]
-    SUMS[2, SHARED : SHARED + 6, :] = SUMS[0, SHARED : SHARED + 6, :]
-    sums_far[0].start()
-    take(2, 2, 1, 0)()
-    send(2, 2, 0, 0)()
-    take(2, 0, "y")()
-    send(2, 0, 0)()
-    take(2, 1, 0, 0)()
-
-    def finish(unit, chunk, out_ref):
-        stage = flows[unit, chunk][2, 0]
-        stage.all_of_it().wait_recv()
-        (start, count), = stage.ours()
-        here = stage.values(0, start, count)
-        return here[...].astype(F32) + stage.room(0, count)[...].astype(F32)
-
-    def lanes_of(chunk):
-        return slice(chunk * CHUNK, (chunk + 1) * CHUNK)
-
-    for chunk in range(3):
-        grw_ref[:, lanes_of(chunk)] = finish(0, chunk, grw_ref)
-    sums_far[0].wait_recv()
-    SUMS[0] = SUMS[0] + SUMS_FAR[0]
-    sums_far[1].start()
-    take(2, 2, 0, 2)()
-    send(2, 2, "y")()
-    take(2, 1, "y")()
-    send(2, 1, 1)()
-    for chunk in range(3):
-        gew_ref[:, lanes_of(chunk)] = finish(1, chunk, gew_ref)
-    sums_far[1].wait()
-    SUMS[0] = SUMS[0] + SUMS_FAR[1]
-    sums_far[2].start()
-    take(2, 2, 0, 0)()
-    take(2, 0, 0)()
-    send(2, 0, 1)()
-    take(2, 2, "y")()
-    send(2, 2, 2)()
-    sums_far[2].wait()
-    SUMS[0] = SUMS[0] + SUMS_FAR[2]
-    sums_far[3].start()
-    take(2, 1, 1)()
-    send(2, 1, 2)()
-    take(2, 0, 1)()
-    send(2, 0, 2)()
-    mixed = jnp.concatenate(
-        [finish(2, chunk, None) for chunk in (0, 1, 2)], axis=1
-    )
-    gmw_ref[...] = jnp.transpose(mixed[:, :256])[:local, :]
+    out_ref[...] = tn(perm, out_ref[...]).astype(BF)
+    at("end", 0)
+    gmw_ref[...] = jnp.transpose(MIX[:, :256])[:local, :]
     for m in range(3):
-        gaw_ref[m] = mixed[:, (m + 1) * local : (m + 2) * local]
-    sums_far[3].wait()
-    both_ref[...] = SUMS[0] + SUMS_FAR[3]
+        gaw_ref[m] = MIX[:, (m + 1) * local : (m + 2) * local]
+    both_ref[...] = SUMS[0]
     for row in range(2 * heads):
         both_ref[3 + row : 4 + row, :BUCKETS] = lax.dot_general(
             both_ref[3 + row : 4 + row, :128], fold_f32, (((1,), (1,)), ((), ())),
@@ -738,8 +899,9 @@
             to_core(unit, slot).wait_send()
     for copy in sums_core + sums_far[:1]:
         copy.wait_send()
-    for piece in pieces[:4]:
-        piece.event(5)
+    for (name, *_), piece in zip(PIECES, pieces):
+        if name not in ("ew", "rw"):
+            piece.sent()
     for copy in give_own + [small_core, small_y, small_far]:
         copy.wait_send()
 
@@ -797,9 +959,7 @@
         return layer_kernel(bits, *refs)
 
     dma = pltpu.SemaphoreType.DMA
-    count = sum(len(order) for orders in ORDERS for order in orders) + sum(
-        order.index("y") for orders in ORDERS for order in orders
-    )
+    count = sum(len(order) + order.index("y") for chunks in CHUNKS for _, _, order in chunks)
     block = width // 8
     output, input_grad, gaw, gmw, gew, grw, both = pl.pallas_call(
         kernel,
@@ -837,11 +997,12 @@
             pltpu.VMEM((rows, 4 * local), BF),
             pltpu.VMEM((4, SMALL_ROWS, hidden), F32),
             pltpu.VMEM((3, 2, width, hidden), BF),
-            pltpu.VMEM((9, 15 * block, CHUNK), BF),
+            pltpu.VMEM((3, 15 * block, hidden), BF),
+            pltpu.VMEM((block, width), F32),
             pltpu.VMEM((4, SMALL_ROWS, width), F32),
             pltpu.VMEM((2, SMALL_ROWS, width), F32),
             pltpu.VMEM((4, SMALL_ROWS, width), F32),
-            dma((2, 8)), dma((2, 8)), dma((2, 8)), dma((2, 8)), dma((2, 4)), dma((2, 3)), dma((5,)),
+            dma((2, 4 * len(PIECES))), dma((2, 4)), dma((2, 3)), dma((5,)),
             dma((2, 6)), dma((2, count)), dma((2, 6)),
         ],
         compiler_params=pltpu.CompilerParams(

time: 149 us -> 135 us (0.906)
  Pallas kernels: 137 us -> 124 us
    pallas_call x1, Pallas kernels: 137 us -> 124 us  [on_device(): pl.pallas_call(kernel, in_specs=[smem] + [vmem] * 9 + [hbm] * 5, out_spec...]
where the time goes in v4:
time: 135 us
  Pallas kernels  124 us (92%)
  local copies, waits for them, and re-layouts  10.1 us (7%)
    pallas_call x1, Pallas kernels, on_device(): pl.pallas_call(kernel, in_specs=[smem] + [vmem] * 9 + [hbm] * 5, out_spec...  124 us
    unnamed x16, local copies, waits for them, and re-layouts  5.79 us

profile of v4, /device:TPU:0, one launch (start us, length us, event | category | flops | bytes accessed | tf_op | source)
XLA Modules:
  0.0 135.1 jit_solution(4460403749162583029)
XLA Ops:
  0.7 123.7 %shard_map.246 = (bf16[512,768]{1,0:T(8,128)(2,1)}, bf16[512,768]{1,0:T(8,128)(2,1)}, f32[3,96,192]{2,1,0:T(8,128)}, f32[192,96]{1,0:T(8,128)}, f32[96,768]{1,0:...) custom-call(s32[4,8]{1,0:T(4,128)} %refs_0_.1, bf16[512,768]{1,0:T(8,128)(2,1)} %refs_1_.1, s32[2,2048]{1,0:T(2,128)} %refs_2_.1, ...), custom_call_target="tpu_custom_call" | custom-call | tf_op jit(solution)/shard_map/pallas_call | solution.py:964
  124.4 0.0 copy-start
  124.4 1.7 %fusion = (f32[1,768]{1,0:T(1,128)S(1)}, f32[1,768]{1,0:T(1,128)S(1)}, f32[1,768]{1,0:T(1,128)S(1)}, f32[1,768]{1,0:T(1,128)S(1)}, f32[768]{0:T(1024)}, /*index=5*/f32[768]{0:T(1024)}, f32[768]{0:T(1024)}) fusion(f32[16,768]{1,0:T(8,128)} %get-tuple-element.23), kind=kLoop, calls=%fused_computation.5 | loop fusion | bytes 43008 | tf_op jit(solution)/shard_map/slice | solution.py:1034
  126.1 0.6 pad_maximum_fusion
  126.7 0.7 slice.35
  127.4 0.6 reshape.29
  128.0 1.3 slice.27
  129.3 0.0 copy-start.3
  129.3 2.1 %copy.34 = bf16[512,768]{1,0:T(8,128)(2,1)} copy(bf16[512,768]{1,0:T(8,128)(2,1)} %get-tuple-element.52) | data formatting | bytes 1572864
  131.4 0.0 copy-done
  131.4 0.0 copy-start.4
  131.4 0.0 copy-start.2
  131.4 0.0 copy-start.1
  131.4 0.9 copy.35
  132.3 0.0 copy-done.3
  132.3 0.7 copy.36
  133.0 0.0 copy-done.4
  133.0 0.6 copy.37
  133.6 0.0 copy-done.2
  133.6 0.7 copy.38
  134.4 0.0 copy-done.1
  134.4 0.7 copy.39
Async XLA Ops:
  124.4 7.0 %copy-start = (bf16[512,768]{1,0:T(8,128)(2,1)S(1)}, bf16[512,768]{1,0:T(8,128)(2,1)}, u32[]{:S(2)}) copy-start(bf16[512,768]{1,0:T(8,128)(2,1)} %get-tuple-element.53) | copy-start | bytes 2359300
  129.3 3.0 %copy-start.3 = (f32[3,96,192]{2,1,0:T(8,128)S(1)}, f32[3,96,192]{2,1,0:T(8,128)}, u32[]{:S(2)}) copy-start(f32[3,96,192]{2,1,0:T(8,128)} %get-tuple-element.54) | copy-start | bytes 663556
  131.4 1.6 %copy-start.4 = (f32[192,96]{1,0:T(8,128)S(1)}, f32[192,96]{1,0:T(8,128)}, u32[]{:S(2)}) copy-start(f32[192,96]{1,0:T(8,128)} %get-tuple-element.56) | copy-start | bytes 221188
  131.4 2.3 %copy-start.2 = (f32[96,768]{1,0:T(8,128)S(1)}, f32[96,768]{1,0:T(8,128)}, u32[]{:S(2)}) copy-start(f32[96,768]{1,0:T(8,128)} %get-tuple-element.60) | copy-start | bytes 884740
  131.4 3.0 %copy-start.1 = (f32[96,768]{1,0:T(8,128)S(1)}, f32[96,768]{1,0:T(8,128)}, u32[]{:S(2)}) copy-start(f32[96,768]{1,0:T(8,128)} %get-tuple-element.26) | copy-start | bytes 884740

commit v5 on v4

--- a/solution.py
+++ b/solution.py
@@ -15,272 +15,311 @@
 F32 = jnp.float32
 VMEM_LIMIT = 60 * 1024 * 1024
 PIECES = (
+    ("ew", 0, 192, (1, 0)),
+    ("ew", 192, 192, (1, 0)),
+    ("rw", 0, 192, (1, 0)),
     ("aw0", 0, 192, (0, 1)),
+    ("rw", 192, 192, ()),
     ("aw1", 0, 192, (1, 0)),
-    ("aw2", 0, 192, (1,)),
-    ("mw", 0, 192, (1, 0)),
-    ("ew", 0, 384, (0, 1)),
-    ("ew", 384, 384, (1, 0)),
-    ("rw", 0, 384, (0, 1)),
-    ("rw", 384, 384, ()),
+    ("ew", 384, 192, ()),
+    ("aw2", 0, 192, (0, 1)),
+    ("mw", 0, 192, (0,)),
+    ("rw", 384, 192, (1, 0)),
+    ("ew", 576, 192, (1,)),
+    ("rw", 576, 192, (0, 1)),
 )
 CHUNKS = (
     (
         (0, 256, ("y", 0, 1, 2)),
         (256, 256, (0, "y", 1, 2)),
-        (512, 256, (1, "y", 0, 2)),
+        (512, 128, (1, "y", 0, 2)),
+        (640, 128, (1, 0, 2, "y")),
+    ),
+    (
+        (0, 128, ("y", 2, 0, 1)),
+        (128, 256, (0, "y", 1, 2)),
+        (384, 384, (1, 0, "y", 2)),
     ),
     (
         (0, 256, ("y", 0, 1, 2)),
         (256, 256, (0, "y", 1, 2)),
         (512, 256, (1, 0, "y", 2)),
     ),
-    (
-        (0, 256, ("y", 0, 1, 2)),
-        (256, 256, (0, "y", 1, 2)),
-        (512, 256, (1, 0, "y", 2)),
-    ),
 )
 PLAN = {
     ("start", 0, 0): (
         ("gs", 0, 0),
+        ("gs", 3, 0),
+        ("gs", 5, 0),
+    ),
+    ("att", 0, 2): (
+        ("gs", 7, 0),
+    ),
+    ("att", 1, 0): (
+        ("gs", 8, 0),
+        ("gs", 9, 0),
+        ("gs", 11, 0),
+        ("gt", 0, 1),
+        ("gs", 0, 1),
+        ("gt", 3, 1),
+        ("gs", 3, 1),
+    ),
+    ("att", 1, 2): (
         ("gs", 1, 0),
         ("gs", 2, 0),
-        ("gs", 3, 0),
+        ("gs", 10, 0),
+    ),
+    ("att", 1, 3): (
+        ("gt", 5, 1),
+        ("gs", 5, 1),
+    ),
+    ("att", 2, 0): (
         ("gs", 4, 0),
-        ("gs", 5, 0),
         ("gs", 6, 0),
-        ("gs", 7, 0),
-    ),
-    ("att", 1, 0): (
-        ("gt", 0, 1),
-        ("gs", 0, 1),
+        ("gt", 7, 1),
+        ("gs", 7, 1),
+        ("gt", 0, 2),
+        ("gs", 0, 2),
+        ("gt", 3, 2),
+        ("gs", 3, 2),
+        ("gt", 9, 1),
+        ("gs", 9, 1),
+        ("gt", 5, 2),
+        ("gs", 5, 2),
+        ("gt", 8, 1),
+        ("gs", 8, 1),
+        ("gt", 11, 1),
+        ("gs", 11, 1),
+        ("gt", 7, 2),
+        ("gs", 7, 2),
         ("gt", 1, 1),
         ("gs", 1, 1),
-    ),
-    ("att", 2, 0): (
-        ("gt", 3, 1),
-        ("gs", 3, 1),
-        ("gt", 0, 2),
-        ("gs", 0, 2),
+        ("gt", 9, 2),
+        ("gs", 9, 2),
+        ("gt", 2, 1),
+        ("gs", 2, 1),
+        ("gt", 3, 3),
+        ("gs", 3, 3),
+        ("gt", 0, 3),
+        ("gs", 0, 3),
+        ("gt", 3, 4),
+        ("gt", 0, 4),
+        ("gt", 7, 3),
+        ("gs", 7, 3),
+        ("gt", 5, 3),
+    ),
+    ("att", 2, 1): (
+        ("gs", 5, 3),
+        ("gt", 7, 4),
+    ),
+    ("att", 2, 3): (
         ("gt", 1, 2),
         ("gs", 1, 2),
-        ("gt", 2, 1),
-        ("gs", 2, 1),
-        ("gt", 3, 2),
-        ("gs", 3, 2),
+        ("gt", 2, 2),
+        ("gs", 2, 2),
+        ("gt", 5, 4),
+        ("gt", 8, 2),
+        ("gs", 8, 2),
+        ("gt", 10, 1),
+        ("gs", 10, 1),
+    ),
+    ("att", 3, 1): (
+        ("gt", 8, 3),
+        ("gt", 11, 2),
+        ("gs", 11, 2),
+    ),
+    ("feed", 0, 0): (
         ("gt", 4, 1),
         ("gs", 4, 1),
+        ("gt", 9, 3),
+        ("gs", 9, 3),
+    ),
+    ("feed", 1, 0): (
+        ("gt", 4, 2),
+        ("gt", 9, 4),
+        ("gt", 10, 2),
+        ("gs", 10, 2),
+    ),
+    ("feed", 1, 1): (
         ("gt", 1, 3),
         ("gs", 1, 3),
-        ("gt", 1, 4),
-        ("gt", 5, 1),
-        ("gs", 5, 1),
-        ("gt", 0, 3),
-        ("gs", 0, 3),
-        ("gt", 2, 2),
-    ),
-    ("att", 2, 1): (
-        ("gs", 2, 2),
-    ),
-    ("att", 2, 3): (
-        ("gt", 0, 4),
+        ("gt", 2, 3),
+        ("gs", 2, 3),
         ("gt", 6, 1),
         ("gs", 6, 1),
-        ("gt", 3, 3),
-    ),
-    ("att", 3, 0): (
-        ("gs", 3, 3),
-        ("gt", 4, 2),
-        ("gs", 4, 2),
-        ("gt", 2, 3),
-    ),
-    ("att", 3, 1): (
-        ("gt", 5, 2),
-        ("gs", 5, 2),
-    ),
-    ("att", 3, 3): (
-        ("gt", 3, 4),
-    ),
-    ("feed", 0, 1): (
+        ("gt", 10, 3),
+        ("gt", 11, 3),
+        ("gs", 11, 3),
+    ),
+    ("feed", 3, 0): (
+        ("gt", 1, 4),
+        ("gt", 2, 4),
         ("gt", 6, 2),
-        ("gs", 6, 2),
-    ),
-    ("feed", 1, 1): (
-        ("gt", 4, 3),
-        ("gs", 4, 3),
-    ),
-    ("feed", 2, 0): (
-        ("gt", 7, 1),
-        ("gs", 7, 1),
-        ("gt", 5, 3),
-    ),
-    ("feed", 2, 1): (
-        ("gs", 5, 3),
-        ("gt", 4, 4),
-        ("gt", 7, 2),
-        ("gt", 6, 3),
-    ),
-    ("feed", 3, 0): (
-        ("gs", 6, 3),
-        ("gt", 5, 4),
-    ),
-    ("feed", 3, 1): (
-        ("gt", 6, 4),
+        ("gt", 11, 4),
     ),
     ("fa", 3, 1): (
         ("cs", 0, 3),
     ),
+    ("fa", 1, 0): (
+        ("ct", 0, 2),
+        ("s", 0, 0, "y", 2),
+        ("s", 0, 3, 1, 2),
+        ("s", 0, 1, 0, 2),
+        ("s", 0, 2, 1, 2),
+    ),
     ("fa", 1, 1): (
         ("cs", 0, 1),
     ),
-    ("fa", 0, 0): (
-        ("ct", 0, 2),
-        ("s", 0, 0, "y", 2),
-        ("s", 0, 1, 0, 2),
-        ("s", 0, 2, 1, 2),
+    ("fb", 3, 0): (
+        ("ct", 0, 0),
+        ("s", 0, 3, 1, 0),
+        ("s", 0, 1, 0, 0),
+        ("s", 0, 2, 1, 0),
     ),
     ("fb", 3, 1): (
         ("cs", 1, 3),
-        ("ct", 0, 0),
-        ("s", 0, 1, 0, 0),
-        ("s", 0, 2, 1, 0),
     ),
     ("fb", 1, 0): (
         ("ct", 1, 2),
+        ("s", 1, 1, 0, 2),
         ("s", 1, 0, "y", 2),
-        ("s", 1, 1, 0, 2),
         ("s", 1, 2, 1, 2),
-    ),
-    ("fb", 1, 1): (
-        ("cs", 1, 1),
+        ("t", 0, 3, 1, 2),
+        ("s", 0, 3, 0, 2),
         ("t", 0, 1, 0, 2),
         ("s", 0, 1, "y", 2),
         ("t", 0, 2, 1, 2),
         ("s", 0, 2, "y", 2),
     ),
-    ("lnb", 0, 0): (
+    ("fb", 1, 1): (
+        ("cs", 1, 1),
+    ),
+    ("fb", 0, 1): (
+        ("t", 0, 0, "y", 2),
+        ("s", 0, 0, 0, 0),
+        ("t", 0, 3, 1, 0),
+        ("s", 0, 3, 0, 0),
         ("ct", 1, 0),
         ("s", 1, 1, 0, 0),
         ("s", 1, 2, 1, 0),
-    ),
-    ("ab", 3, 0): (
-        ("t", 0, 0, "y", 2),
-        ("s", 0, 0, 0, 0),
         ("t", 0, 1, 0, 0),
         ("t", 0, 2, 1, 0),
     ),
-    ("ab", 3, 2): (
+    ("lnb", 0, 0): (
+        ("t", 0, 3, 0, 2),
+        ("s", 0, 3, 2, 2),
+    ),
+    ("ab", 3, 3): (
+        ("cs", 2, 3),
         ("t", 1, 1, 0, 2),
         ("s", 1, 1, "y", 2),
+    ),
+    ("ab", 2, 1): (
+        ("t", 0, 3, 0, 0),
+        ("s", 0, 3, 2, 0),
+        ("t", 0, 1, "y", 2),
+        ("s", 0, 1, 1, 0),
+        ("t", 1, 0, "y", 2),
+        ("s", 1, 0, 2, 0),
+        ("t", 0, 3, 2, 2),
+        ("s", 0, 3, "y", 2),
         ("t", 1, 2, 1, 2),
         ("s", 1, 2, 0, 2),
     ),
-    ("ab", 3, 3): (
-        ("cs", 2, 3),
-    ),
-    ("ab", 2, 1): (
+    ("ab", 2, 2): (
+        ("t", 0, 2, "y", 2),
+        ("s", 0, 2, 0, 0),
+    ),
+    ("ab", 2, 3): (
+        ("ct", 2, 2),
+        ("s", 2, 1, 0, 2),
+        ("s", 2, 2, 1, 2),
+        ("s", 2, 0, "y", 2),
+        ("t", 0, 0, 0, 0),
+        ("s", 0, 0, 1, 0),
+    ),
+    ("ab", 1, 1): (
+        ("t", 0, 3, 2, 0),
+        ("t", 0, 3, "y", 2),
         ("t", 1, 2, 1, 0),
         ("s", 1, 2, 0, 0),
     ),
-    ("ab", 2, 2): (
-        ("t", 0, 1, "y", 2),
-        ("s", 0, 1, 1, 0),
-    ),
-    ("ab", 2, 3): (
-        ("ct", 2, 2),
-        ("s", 2, 0, "y", 2),
-        ("s", 2, 1, 0, 2),
-        ("s", 2, 2, 1, 2),
-    ),
-    ("ab", 1, 0): (
+    ("ab", 1, 2): (
         ("t", 1, 1, 0, 0),
-    ),
-    ("ab", 1, 1): (
-        ("t", 0, 0, 0, 0),
-        ("s", 0, 0, 1, 0),
-    ),
-    ("ab", 1, 2): (
+        ("t", 1, 1, "y", 2),
+        ("s", 1, 1, 1, 0),
+    ),
+    ("ab", 1, 3): (
+        ("cs", 2, 1),
         ("t", 0, 1, 1, 0),
         ("s", 0, 1, 2, 0),
-        ("t", 1, 0, "y", 2),
+    ),
+    ("ab", 0, 0): (
+        ("t", 0, 2, 0, 0),
+        ("s", 0, 2, 2, 0),
+        ("t", 1, 0, 2, 0),
         ("s", 1, 0, 0, 0),
     ),
-    ("ab", 1, 3): (
-        ("cs", 2, 1),
+    ("ab", 0, 1): (
         ("t", 1, 2, 0, 2),
         ("s", 1, 2, "y", 2),
-    ),
-    ("ab", 0, 0): (
-        ("t", 1, 2, 0, 0),
-    ),
-    ("ab", 0, 1): (
-        ("t", 0, 2, "y", 2),
-        ("s", 0, 2, 0, 0),
-    ),
-    ("ab", 0, 2): (
-        ("t", 0, 0, 1, 0),
-        ("s", 0, 0, 2, 0),
     ),
     ("ab", 0, 3): (
         ("ms", 0),
         ("ct", 2, 0),
         ("s", 2, 1, 0, 0),
         ("s", 2, 2, 1, 0),
+        ("t", 0, 0, 1, 0),
+        ("s", 0, 0, 2, 0),
+    ),
+    ("end", 0, 0): (
+        ("mt", 0),
+        ("ms", 1),
+        ("t", 2, 0, "y", 2),
+        ("s", 2, 0, 0, 0),
+        ("t", 1, 2, 0, 0),
         ("t", 2, 2, 1, 2),
         ("s", 2, 2, 0, 2),
-    ),
-    ("end", 0, 0): (
-        ("t", 0, 1, 2, 0),
-        ("t", 1, 1, "y", 2),
-        ("s", 1, 1, 1, 0),
         ("t", 2, 1, 0, 2),
         ("s", 2, 1, "y", 2),
-        ("mt", 0),
-        ("ms", 1),
-        ("t", 0, 0, 2, 0),
+        ("t", 1, 1, 1, 0),
+        ("s", 1, 1, 2, 0),
+        ("t", 1, 2, "y", 2),
+        ("s", 1, 2, 2, 0),
         ("t", 1, 0, 0, 0),
         ("s", 1, 0, 1, 0),
-        ("t", 1, 2, "y", 2),
-        ("s", 1, 2, 2, 0),
-        ("t", 0, 2, 0, 0),
-        ("s", 0, 2, 2, 0),
-        ("t", 1, 1, 1, 0),
-        ("s", 1, 1, 2, 0),
+        ("t", 0, 2, 2, 0),
+        ("t", 0, 1, 2, 0),
+        ("mt", 1),
+        ("ms", 2),
+        ("t", 0, 0, 2, 0),
+        ("t", 1, 1, 2, 0),
+        ("t", 2, 1, 0, 0),
+        ("t", 2, 1, "y", 2),
+        ("s", 2, 1, 1, 0),
         ("t", 2, 2, 1, 0),
         ("s", 2, 2, 0, 0),
+        ("t", 2, 0, 0, 0),
+        ("s", 2, 0, 1, 0),
+        ("t", 1, 2, 2, 0),
+        ("t", 1, 0, 1, 0),
         ("t", 2, 2, 0, 2),
         ("s", 2, 2, "y", 2),
-        ("t", 2, 1, 0, 0),
-        ("t", 1, 0, 1, 0),
-        ("s", 1, 0, 2, 0),
-        ("t", 1, 2, 2, 0),
-        ("t", 2, 0, "y", 2),
-        ("s", 2, 0, 0, 0),
-        ("t", 2, 2, 0, 0),
-        ("t", 2, 1, "y", 2),
-        ("s", 2, 1, 1, 0),
-        ("mt", 1),
-        ("ms", 2),
-        ("t", 0, 2, 2, 0),
-        ("t", 1, 1, 2, 0),
-        ("t", 2, 2, "y", 2),
-        ("s", 2, 2, 2, 0),
-        ("t", 1, 0, 2, 0),
         ("mt", 2),
         ("ms", 3),
         ("t", 2, 1, 1, 0),
         ("s", 2, 1, 2, 0),
-        ("t", 2, 0, 0, 0),
-        ("s", 2, 0, 1, 0),
-        ("t", 2, 2, 2, 0),
+        ("t", 2, 2, 0, 0),
+        ("t", 2, 0, 1, 0),
+        ("s", 2, 0, 2, 0),
+        ("t", 2, 2, "y", 2),
+        ("s", 2, 2, 2, 0),
         ("mt", 3),
         ("ms", 4),
         ("t", 2, 1, 2, 0),
-        ("t", 2, 0, 1, 0),
-        ("s", 2, 0, 2, 0),
+        ("t", 2, 0, 2, 0),
+        ("t", 2, 2, 2, 0),
         ("mt", 4),
-        ("t", 2, 0, 2, 0),
     ),
 }
 
@@ -922,6 +961,21 @@
         send = lax.dynamic_index_in_dim(value, 1 - mine, axis, keepdims=False)
         value = keep + swap(send, "dp", dp, 1 << bit)
     return value
+
+
+def finish_kernel(*refs):
+    sources, both, targets, small = refs[:6], refs[6], refs[7:13], refs[13:20]
+    for source, target in zip(sources, targets):
+        target[...] = source[...]
+    shifts, merge, gains, norm_shift, expand, reduced, tables = small
+    shifts[...] = both[1:3, : shifts.shape[1]]
+    for target, row in ((merge, SHARED + 2), (expand, 0), (reduced, SHARED + 5)):
+        target[...] = both[row : row + 1, :].reshape(target.shape)
+    for target, row in ((gains, SHARED), (norm_shift, SHARED + 1)):
+        target[0:1, :] = both[row : row + 1, :]
+        target[1:2, :] = both[row + 3 : row + 4, :]
+    for h in range(tables.shape[0]):
+        tables[h] = both[3 + 2 * h : 5 + 2 * h, :BUCKETS]
 
 
 def on_device(
@@ -1021,21 +1075,20 @@
         gaw = jnp.stack([finish_rows(gaw[m], dp, 3) for m in range(3)])
         for bit in range(top - 3):
             both = both + swap(both, "dp", dp, 1 << bit)
-    first = SHARED
-    tables = both[3 : 3 + 2 * heads, :BUCKETS].reshape(heads, 2, BUCKETS)
+    big = (output, input_grad, gaw, gmw, gew, grw)
+    done = pl.pallas_call(
+        finish_kernel,
+        in_specs=[vmem] * 7,
+        out_specs=[vmem] * 13,
+        out_shape=[sds(a.shape, a.dtype) for a in big]
+        + [
+            sds((2, local), F32), sds((width,), F32), sds((2, width), F32), sds((2, width), F32),
+            sds((hidden,), F32), sds((width,), F32), sds((heads, 2, BUCKETS), F32),
+        ],
+    )(*big, both)
+    output, input_grad, gaw, gmw, gew, grw, shifts, merge, gains, norm_shift, expand, reduced, tables = done
     return (
-        output,
-        input_grad,
-        gaw,
-        both[1:3, :local],
-        gmw,
-        both[first + 2],
-        jnp.stack([both[first], both[first + 3]]),
-        jnp.stack([both[first + 1], both[first + 4]]),
-        gew,
-        both[0],
-        grw.T,
-        both[first + 5],
+        output, input_grad, gaw, shifts, gmw, merge, gains, norm_shift, gew, expand, grw.T, reduced,
         jnp.transpose(tables, (1, 0, 2)),
     )
 

time: 135 us -> 121 us (0.90)
  local copies, waits for them, and re-layouts: 10.1 us -> 0 us
  Pallas kernels: 124 us -> 120 us
    pallas_call x1, Pallas kernels: 124 us -> 117 us  [on_device(): pl.pallas_call(kernel, in_specs=[smem] + [vmem] * 9 + [hbm] * 5, out_spec...]
    unnamed x16 -> x0, local copies, waits for them, and re-layouts: 5.79 us -> none
    slice x3 -> x0, local copies, waits for them, and re-layouts: 3.68 us -> none  [the longest x1 1.71 us: on_device(): both[first + 1]]
    pallas_call x0 -> x1, Pallas kernels: none -> 3.2 us  [on_device(): pl.pallas_call(finish_kernel, in_specs=[vmem] * 7, out_specs=[vmem] * 13,...]
where the time goes in v5:
time: 121 us
  Pallas kernels  120 us (99%)
    pallas_call x1, Pallas kernels, on_device(): pl.pallas_call(kernel, in_specs=[smem] + [vmem] * 9 + [hbm] * 5, out_spec...  117 us
    pallas_call x1, Pallas kernels, on_device(): pl.pallas_call(finish_kernel, in_specs=[vmem] * 7, out_specs=[vmem] * 13,...  3.2 us

profile of v5, /device:TPU:0, one launch (start us, length us, event | category | flops | bytes accessed | tf_op | source)
XLA Modules:
  0.0 120.6 jit_solution(770607433070619407)
XLA Ops:
  0.7 116.6 %shard_map.246 = (bf16[512,768]{1,0:T(8,128)(2,1)}, bf16[512,768]{1,0:T(8,128)(2,1)}, f32[3,96,192]{2,1,0:T(8,128)}, f32[192,96]{1,0:T(8,128)}, f32[96,768]{1,0:...) custom-call(s32[4,8]{1,0:T(4,128)} %refs_0_.1, bf16[512,768]{1,0:T(8,128)(2,1)} %refs_1_.1, s32[2,2048]{1,0:T(2,128)} %refs_2_.1, ...), custom_call_target="tpu_custom_call" | custom-call | tf_op jit(solution)/shard_map/pallas_call | solution.py:1018
  117.2 3.2 %shard_map.247 = (bf16[512,768]{1,0:T(8,128)(2,1)}, bf16[512,768]{1,0:T(8,128)(2,1)}, f32[3,96,192]{2,1,0:T(8,128)}, f32[192,96]{1,0:T(8,128)}, f32[96,768]{1,0:...) custom-call(bf16[512,768]{1,0:T(8,128)(2,1)} %get-tuple-element.33.r, ...), custom_call_target="tpu_custom_call" | custom-call | tf_op jit(solution)/shard_map/pallas_call | solution.py:1079

commit v6 on v5

--- a/solution.py
+++ b/solution.py
@@ -181,8 +181,8 @@
     ),
     ("fb", 1, 0): (
         ("ct", 1, 2),
+        ("s", 1, 0, "y", 2),
         ("s", 1, 1, 0, 2),
-        ("s", 1, 0, "y", 2),
         ("s", 1, 2, 1, 2),
         ("t", 0, 3, 1, 2),
         ("s", 0, 3, 0, 2),
@@ -233,8 +233,8 @@
     ("ab", 2, 3): (
         ("ct", 2, 2),
         ("s", 2, 1, 0, 2),
+        ("s", 2, 0, "y", 2),
         ("s", 2, 2, 1, 2),
-        ("s", 2, 0, "y", 2),
         ("t", 0, 0, 0, 0),
         ("s", 0, 0, 1, 0),
     ),
@@ -524,20 +524,23 @@
 
 def layer_kernel(
     bits,
-    pages_ref, x_ref, cells_ref, shift_ref, es_ref, tables_ref, ms_ref, rs_ref, gain_ref, nshift_ref,
-    aw_hbm, mw_hbm, ew_hbm, rw_hbm, cot_hbm,
-    out_ref, gin_ref, gaw_ref, gmw_ref, gew_ref, grw_ref, both_ref,
+    pages_ref, cells_ref, shift_ref, es_ref, tables_ref, ms_ref, rs_ref, gain_ref, nshift_ref,
+    aw_hbm, mw_hbm, ew_hbm, rw_hbm, cot_hbm, x_hbm,
+    gaw_ref, gmw_ref, both_ref, out_hbm, gin_hbm, gew_hbm, grw_hbm,
     AW, MW, EW, RW, XR, HOT, BACK, Q, K, V, PR, CTX, NB, HAT, SCALE, AS, ACC, GB, GC, DQ, DK, DV, E, DD, SM,
-    FROM_CORE, FROM, MIX, SUMS, SUMS_CORE, SUMS_FAR,
+    FROM_CORE, FROM, GRW, GEW, MIX, RESULT, SUMS, SUMS_CORE, SUMS_FAR,
     in_sems, own_sems, small_sems, local_sems,
     unit_sems, stage_sems, total_sems,
 ):
     net = Net(bits)
-    rows, width = x_ref.shape
+    rows, width = x_hbm.shape
     half = rows // 2
     local = aw_hbm.shape[1]
     heads = local // HEAD_DIM
     hidden = ew_hbm.shape[1]
+
+    fetch_x = pltpu.make_async_copy(x_hbm, NB, local_sems.at[5])
+    fetch_x.start()
 
     barrier = pltpu.get_barrier_semaphore()
     greeted = (net.core, net.y, net.dp[0], net.dp[1], net.dp[2])
@@ -627,7 +630,7 @@
                 sums_far[k - 1].wait_send()
             SUMS[0] = SUMS[0] + SUMS_FAR[k - 1]
 
-    results = (grw_ref, gew_ref, MIX)
+    results = (GRW, GEW, MIX)
 
     def take(unit, chunk, axis, slot):
         stages = flows[unit, chunk]
@@ -689,7 +692,8 @@
 
     begin, bounds = page_scalars(pages_ref, net.t, half)
     perm = (iota((rows, rows), 1) == ((iota((rows, rows), 0) + begin) & (rows - 1))).astype(BF)
-    XR[...] = nn(perm, x_ref[...]).astype(BF)
+    fetch_x.wait()
+    XR[...] = nn(perm, NB[...]).astype(BF)
     bucket = iota((BUCKETS, rows), 0)
     mine = pl.ds(pl.multiple_of(net.t * rows, 128), rows)
     one = (cells_ref[0:1, mine] == bucket).astype(BF)
@@ -806,7 +810,7 @@
     gain = gain_ref[1:2, :].astype(F32)
     result = (hat * gain + nshift_ref[1:2, :].astype(F32)).astype(BF)
     perm = (iota((rows, rows), 1) == ((iota((rows, rows), 0) + begin) & (rows - 1))).astype(BF)
-    out_ref[...] = result
+    RESULT[...] = result
     cot = nn(perm, GB[...])
     grad = norm_back(cot, hat, scale, gain)
     ACC[...] = grad
@@ -917,9 +921,19 @@
 
     at("fin", 0)
     perm = (iota((rows, rows), 1) == ((iota((rows, rows), 0) + begin) & (rows - 1))).astype(BF)
-    gin_ref[...] = tn(perm, ACC[...].astype(BF)).astype(BF)
-    out_ref[...] = tn(perm, out_ref[...]).astype(BF)
+    GB[...] = tn(perm, ACC[...].astype(BF)).astype(BF)
+    RESULT[...] = tn(perm, RESULT[...]).astype(BF)
+    leave = [
+        pltpu.make_async_copy(source, target, local_sems.at[6 + n])
+        for n, (source, target) in enumerate(
+            ((RESULT, out_hbm), (GB, gin_hbm), (GEW, gew_hbm), (GRW, grw_hbm))
+        )
+    ]
+    leave[0].start()
+    leave[1].start()
     at("end", 0)
+    leave[2].start()
+    leave[3].start()
     gmw_ref[...] = jnp.transpose(MIX[:, :256])[:local, :]
     for m in range(3):
         gaw_ref[m] = MIX[:, (m + 1) * local : (m + 2) * local]
@@ -943,6 +957,8 @@
             piece.sent()
     for copy in give_own + [small_core, small_y, small_far]:
         copy.wait_send()
+    for copy in leave:
+        copy.wait()
 
 
 def swap(value, axis, size, bit):
@@ -1015,14 +1031,14 @@
     dma = pltpu.SemaphoreType.DMA
     count = sum(len(order) + order.index("y") for chunks in CHUNKS for _, _, order in chunks)
     block = width // 8
-    output, input_grad, gaw, gmw, gew, grw, both = pl.pallas_call(
+    gaw, gmw, both, output, input_grad, gew, grw = pl.pallas_call(
         kernel,
-        in_specs=[smem] + [vmem] * 9 + [hbm] * 5,
-        out_specs=[vmem] * 7,
+        in_specs=[smem] + [vmem] * 8 + [hbm] * 6,
+        out_specs=[vmem] * 3 + [hbm] * 4,
         out_shape=[
-            sds((rows, width), BF), sds((rows, width), BF), sds((3, block, local), F32),
-            sds((local, block), F32), sds((block, hidden), F32), sds((block, hidden), F32),
-            sds((SMALL_ROWS, width), F32),
+            sds((3, block, local), F32), sds((local, block), F32), sds((SMALL_ROWS, width), F32),
+            sds((rows, width), BF), sds((rows, width), BF), sds((block, hidden), F32),
+            sds((block, hidden), F32),
         ],
         scratch_shapes=[
             pltpu.VMEM((4, 3, local, width), BF),
@@ -1052,20 +1068,24 @@
             pltpu.VMEM((4, SMALL_ROWS, hidden), F32),
             pltpu.VMEM((3, 2, width, hidden), BF),
             pltpu.VMEM((3, 15 * block, hidden), BF),
+            pltpu.VMEM((block, hidden), F32),
+            pltpu.VMEM((block, hidden), F32),
             pltpu.VMEM((block, width), F32),
+            pltpu.VMEM((rows, width), BF),
             pltpu.VMEM((4, SMALL_ROWS, width), F32),
             pltpu.VMEM((2, SMALL_ROWS, width), F32),
             pltpu.VMEM((4, SMALL_ROWS, width), F32),
-            dma((2, 4 * len(PIECES))), dma((2, 4)), dma((2, 3)), dma((5,)),
+            dma((2, 4 * len(PIECES))), dma((2, 4)), dma((2, 3)), dma((10,)),
             dma((2, 6)), dma((2, count)), dma((2, 6)),
         ],
         compiler_params=pltpu.CompilerParams(
             collective_id=0, has_side_effects=True, vmem_limit_bytes=VMEM_LIMIT
         ),
     )(
-        page_lengths, inputs, layout_cells, attend_shift, expand_shift,
+        page_lengths, layout_cells, attend_shift, expand_shift,
         jnp.transpose(bias_tables, (1, 0, 2)), merge_shift, reduce_shift, norm_gains, norm_shifts,
         jnp.transpose(attend_weight, (0, 2, 1)), merge_weight, expand_weight, reduce_weight, cotangent,
+        inputs,
     )
 
     if top > 3:

time: 121 us -> 120 us (level)
  no operation moved by 1% of the time
where the time goes in v6:
time: 120 us
  Pallas kernels  119 us (99%)
    pallas_call x1, Pallas kernels, on_device(): pl.pallas_call(kernel, in_specs=[smem] + [vmem] * 8 + [hbm] * 6, out_spec...  116 us
    pallas_call x1, Pallas kernels, on_device(): pl.pallas_call(finish_kernel, in_specs=[vmem] * 7, out_specs=[vmem] * 13,...  3.2 us

profile of v6, /device:TPU:0, one launch (start us, length us, event | category | flops | bytes accessed | tf_op | source)
XLA Modules:
  0.0 120.0 jit_solution(10606788778641066604)
XLA Ops:
  0.7 115.9 %shard_map.246 = (f32[3,96,192]{2,1,0:T(8,128)}, f32[192,96]{1,0:T(8,128)}, f32[16,768]{1,0:T(8,128)}, bf16[512,768]{1,0:T(8,128)(2,1)}, bf16[512,768]{1,0:T(8,1...) custom-call(s32[4,8]{1,0:T(4,128)} %refs_0_.1, s32[2,2048]{1,0:T(2,128)} %refs_1_.1, bf16[2,192]{1,0:T(2,128)(2,1)} %refs_2_.1, ...), custom_call_target="tpu_custom_call" | custom-call | tf_op jit(solution)/shard_map/pallas_call | solution.py:1034
  116.6 3.2 %shard_map.247 = (bf16[512,768]{1,0:T(8,128)(2,1)}, bf16[512,768]{1,0:T(8,128)(2,1)}, f32[3,96,192]{2,1,0:T(8,128)}, f32[192,96]{1,0:T(8,128)}, f32[96,768]{1,0:...) custom-call(bf16[512,768]{1,0:T(8,128)(2,1)} %get-tuple-element.33.r, ...), custom_call_target="tpu_custom_call" | custom-call | tf_op jit(solution)/shard_map/pallas_call | solution.py:1099

commit v7 on v6

--- a/solution.py
+++ b/solution.py
@@ -684,11 +684,9 @@
     small_y.start()
     at("start", 0)
     small_core.start()
-    for copy in give_own:
-        copy.start()
-    keep_own[2].start()
-    keep_own[3].start()
-    fetch_cot.start()
+    give_own[0].start()
+    give_own[1].start()
+    not_urgent = give_own[2:] + keep_own[2:] + [fetch_cot]
 
     begin, bounds = page_scalars(pages_ref, net.t, half)
     perm = (iota((rows, rows), 1) == ((iota((rows, rows), 0) + begin) & (rows - 1))).astype(BF)
@@ -776,7 +774,7 @@
                     part = tn(probs, V[r, span, lanes]) * keep.astype(F32)
                     total = part if total is None else total + part
                 CTX[r, span, lanes] = total.astype(BF)
-        at("att", 3, r)
+        at("att", 3, r, {0: [copy.start for copy in not_urgent]})
         ACC[...] += nn(CTX[r, :, :local], MW[r])
         return 0
 

time: 120 us -> 120 us (level)
  no operation moved by 1% of the time
where the time goes in v7:
time: 120 us
  Pallas kernels  119 us (99%)
    pallas_call x1, Pallas kernels, on_device(): pl.pallas_call(kernel, in_specs=[smem] + [vmem] * 8 + [hbm] * 6, out_spec...  116 us
    pallas_call x1, Pallas kernels, on_device(): pl.pallas_call(finish_kernel, in_specs=[vmem] * 7, out_specs=[vmem] * 13,...  3.2 us

profile of v7, /device:TPU:0, one launch (start us, length us, event | category | flops | bytes accessed | tf_op | source)
XLA Modules:
  0.0 120.0 jit_solution(1106505958745518949)
XLA Ops:
  0.7 116.0 %shard_map.246 = (f32[3,96,192]{2,1,0:T(8,128)}, f32[192,96]{1,0:T(8,128)}, f32[16,768]{1,0:T(8,128)}, bf16[512,768]{1,0:T(8,128)(2,1)}, bf16[512,768]{1,0:T(8,1...) custom-call(s32[4,8]{1,0:T(4,128)} %refs_0_.1, s32[2,2048]{1,0:T(2,128)} %refs_1_.1, bf16[2,192]{1,0:T(2,128)(2,1)} %refs_2_.1, ...), custom_call_target="tpu_custom_call" | custom-call | tf_op jit(solution)/shard_map/pallas_call | solution.py:1032
  116.7 3.2 %shard_map.247 = (bf16[512,768]{1,0:T(8,128)(2,1)}, bf16[512,768]{1,0:T(8,128)(2,1)}, f32[3,96,192]{2,1,0:T(8,128)}, f32[192,96]{1,0:T(8,128)}, f32[96,768]{1,0:...) custom-call(bf16[512,768]{1,0:T(8,128)(2,1)} %get-tuple-element.33.r, ...), custom_call_target="tpu_custom_call" | custom-call | tf_op jit(solution)/shard_map/pallas_call | solution.py:1097
